TPU v7x, 32 devices: a whole 2x2x4 slice. The times are simulated.
32 devices in a mesh: items: 8 (over y, x, core), mem: 4 (over z).
Axes of the slice: x: 2, y: 2, z: 4, core: 2. Of those that a mesh axis runs over, the one named last changes fastest.
Arguments:
- tokens: bfloat16 [8192, 1024], P(('items', 'mem')), may hold values from -6 to 6
- memory: bfloat16 [64, 1024, 1024], P('items', 'mem'), may hold values from -6 to 6
- cotangent: bfloat16 [8192, 1024], P(('items', 'mem')), may hold values from -6 to 6
- mem_len: int32 [64], P('items'), may hold values from 128 to 1024, as said below
- dec_len: int32 [64], P('items'), may hold values from 32 to 128, as said below
- self_query: bfloat16 [1024, 1024], P('items', 'mem'), may hold values from -0.1875 to 0.1875
- self_key: bfloat16 [1024, 1024], P('items', 'mem'), may hold values from -0.1875 to 0.1875
- self_value: bfloat16 [1024, 1024], P('items', 'mem'), may hold values from -0.1875 to 0.1875
- self_out: bfloat16 [1024, 1024], P('items', 'mem'), may hold values from -0.875 to 0.875
- cross_query: bfloat16 [1024, 1024], P('items', 'mem'), may hold values from -0.1875 to 0.1875
- cross_key: bfloat16 [1024, 1024], P('items', 'mem'), may hold values from -0.1875 to 0.1875
- cross_value: bfloat16 [1024, 1024], P('items', 'mem'), may hold values from -0.1875 to 0.1875
- cross_out: bfloat16 [1024, 1024], P('items', 'mem'), may hold values from -3.5 to 3.5
- feed_in: bfloat16 [1024, 4096], P('items', 'mem'), may hold values from -0.1875 to 0.1875
- feed_out: bfloat16 [4096, 1024], P('items', 'mem'), may hold values from -0.09375 to 0.09375
- shifts: bfloat16 [10, 1024], P(None, 'items'), may hold values from -3 to 3
- gains: bfloat16 [3, 1024], P(None, 'items'), may hold values from 0.5 to 1.5
- inner_bias: bfloat16 [4096], P('items'), may hold values from -3 to 3
Outputs:
- layer_out: float32 [8192, 1024], P(('items', 'mem'))
- tokens_grad: float32 [8192, 1024], P(('items', 'mem'))
- memory_grad: float32 [64, 1024, 1024], P('items', 'mem')
- self_query_grad: float32 [1024, 1024], P('items', 'mem')
- self_key_grad: float32 [1024, 1024], P('items', 'mem')
- self_value_grad: float32 [1024, 1024], P('items', 'mem')
- self_out_grad: float32 [1024, 1024], P('items', 'mem')
- cross_query_grad: float32 [1024, 1024], P('items', 'mem')
- cross_key_grad: float32 [1024, 1024], P('items', 'mem')
- cross_value_grad: float32 [1024, 1024], P('items', 'mem')
- cross_out_grad: float32 [1024, 1024], P('items', 'mem')
- feed_in_grad: float32 [1024, 4096], P('items', 'mem')
- feed_out_grad: float32 [4096, 1024], P('items', 'mem')
- shifts_grad: float32 [10, 1024], P(None, 'items')
- gains_grad: float32 [3, 1024], P(None, 'items')
- inner_bias_grad: float32 [4096], P('items')
Inputs may be any that keep to these rules, and one draw needn't show every extreme that they name: Memory slots below mem_len[i] hold item i's encoded table and question; the rest are padding. Decoder positions at or above dec_len[i] are padding that no query attends to.
All inputs are finite; a program needn't handle non-finite values.
Results may differ from a plain program's by a relative error of at most 0.03.
Values may be sent and summed in bfloat16 or wider, within the bound.
A program may use at most 256 MiB of HBM per device.

v0:
```python
import jax
import jax.numpy as jnp
from jax import lax
from jax.sharding import PartitionSpec as P

D = 1024
HEADS = 16
HEAD_DIM = 64
DEC = 128


half_root = 0.7071067811865476
normal_peak = 0.3989422804014327


def product(first_op, second_op):
    return jnp.dot(first_op, second_op, preferred_element_type=jnp.float32)


def left_product(first_op, second_op):
    return lax.dot_general(
        first_op, second_op, (((0,), (0,)), ((), ())), preferred_element_type=jnp.float32
    )


def right_product(first_op, second_op):
    return lax.dot_general(
        first_op, second_op, (((1,), (1,)), ((), ())), preferred_element_type=jnp.float32
    )


def column_sums(values):
    return jnp.sum(values.astype(jnp.float32), 0)


def norm_forward(values, gain, shift):
    center = values - jnp.mean(values, -1, keepdims=True)
    inverse = lax.rsqrt(jnp.mean(center * center, -1, keepdims=True) + 1e-05)
    normed = center * inverse
    return (normed * gain + shift, normed, inverse)


def norm_backward(grad_out, normed, inverse, gain):
    scaled = grad_out * gain
    grad_in = inverse * (
        scaled
        - jnp.mean(scaled, -1, keepdims=True)
        - normed * jnp.mean(scaled * normed, -1, keepdims=True)
    )
    return (grad_in, jnp.sum(grad_out * normed, 0), jnp.sum(grad_out, 0))


def split_heads(values, item_count):
    return values.reshape(item_count, -1, HEADS, HEAD_DIM)


def attend_forward(queries, keys_in, values_in, allowed):
    scores = jnp.einsum("iqhd,ikhd->ihqk", queries, keys_in, preferred_element_type=jnp.float32)
    exp_scores = jnp.where(allowed[:, None], jnp.exp(scores), 0.0)
    numerator = jnp.einsum(
        "ihqk,ikhd->iqhd",
        exp_scores.astype(jnp.bfloat16),
        values_in,
        preferred_element_type=jnp.float32,
    )
    return (numerator, jnp.transpose(jnp.sum(exp_scores, -1), (0, 2, 1)))


def attend_backward(queries, keys_in, values_in, allowed, grad_numer, grad_total):
    scores = jnp.einsum("iqhd,ikhd->ihqk", queries, keys_in, preferred_element_type=jnp.float32)
    exp_scores = jnp.where(allowed[:, None], jnp.exp(scores), 0.0)
    grad_exp = jnp.einsum(
        "iqhd,ikhd->ihqk", grad_numer, values_in, preferred_element_type=jnp.float32
    )
    grad_exp = grad_exp + jnp.transpose(grad_total.astype(jnp.float32), (0, 2, 1))[..., None]
    grad_scores = (exp_scores * grad_exp).astype(jnp.bfloat16)
    query_grad = jnp.einsum(
        "ihqk,ikhd->iqhd", grad_scores, keys_in, preferred_element_type=jnp.float32
    )
    key_grad = jnp.einsum(
        "ihqk,iqhd->ikhd", grad_scores, queries, preferred_element_type=jnp.float32
    )
    value_grad = jnp.einsum(
        "ihqk,iqhd->ikhd",
        exp_scores.astype(jnp.bfloat16),
        grad_numer,
        preferred_element_type=jnp.float32,
    )
    return (query_grad, key_grad, value_grad)


def reshape_block(values):
    return values.reshape((values.shape[0] // 4, 4) + values.shape[1:])


def merge_block(values):
    return values.reshape((-1,) + values.shape[2:])


def cross_forward(pieces):
    return attend_forward(pieces[0], pieces[1], pieces[2], pieces[3])


def cross_backward(pieces):
    return attend_backward(pieces[0], pieces[1], pieces[2], pieces[3], pieces[4], pieces[5])


def body(
    tokens,
    memory,
    cotangent,
    mem_len,
    dec_len,
    self_query,
    self_key,
    self_value,
    self_out,
    cross_query,
    cross_key,
    cross_value,
    cross_out,
    feed_in,
    feed_out,
    shifts,
    gains,
    inner_bias,
):
    cols_whole = (
        lax.all_gather(self_query, "mem", axis=1, tiled=True),
        lax.all_gather(self_key, "mem", axis=1, tiled=True),
        lax.all_gather(self_value, "mem", axis=1, tiled=True),
        lax.all_gather(self_out, "mem", axis=1, tiled=True),
        lax.all_gather(cross_query, "mem", axis=1, tiled=True),
        lax.all_gather(cross_key, "mem", axis=1, tiled=True),
        lax.all_gather(cross_value, "mem", axis=1, tiled=True),
        lax.all_gather(cross_out, "mem", axis=1, tiled=True),
        lax.all_gather(feed_in, "mem", axis=1, tiled=True),
        lax.all_gather(feed_out, "mem", axis=1, tiled=True),
    )
    whole = (
        lax.all_gather(cols_whole[0], "items", axis=0, tiled=True),
        lax.all_gather(cols_whole[1], "items", axis=0, tiled=True),
        lax.all_gather(cols_whole[2], "items", axis=0, tiled=True),
        lax.all_gather(cols_whole[3], "items", axis=0, tiled=True),
        lax.all_gather(cols_whole[4], "items", axis=0, tiled=True),
        lax.all_gather(cols_whole[5], "items", axis=0, tiled=True),
        lax.all_gather(cols_whole[6], "items", axis=0, tiled=True),
        lax.all_gather(cols_whole[7], "items", axis=0, tiled=True),
        lax.all_gather(cols_whole[8], "items", axis=0, tiled=True),
        lax.all_gather(cols_whole[9], "items", axis=0, tiled=True),
        lax.all_gather(shifts, "items", axis=1, tiled=True),
        lax.all_gather(gains, "items", axis=1, tiled=True),
        lax.all_gather(inner_bias, "items", axis=0, tiled=True),
    )
    (
        query_self,
        key_self,
        value_self,
        output_self,
        query_cross,
        key_cross,
        value_cross,
        output_cross,
        feed_up,
        feed_down,
        shift_part,
        gain_part,
        inner_part,
    ) = whole
    shift_rows = shift_part.astype(jnp.float32)
    gain_rows = gain_part.astype(jnp.float32)
    inner_shift = inner_part.astype(jnp.float32)
    rows_here = tokens.shape[0]
    item_count = rows_here // DEC
    group_items = memory.shape[0]
    mem_local = memory.shape[1]
    member = lax.axis_index("mem")
    tokens_float = tokens.astype(jnp.float32)
    queries_one = ((product(tokens, query_self) + shift_rows[0]) * 0.125).astype(jnp.bfloat16)
    keys_one = product(tokens, key_self).astype(jnp.bfloat16)
    values_one = (product(tokens, value_self) + shift_rows[1]).astype(jnp.bfloat16)
    own_len = lax.dynamic_slice_in_dim(dec_len, member * item_count, item_count)
    position = jnp.arange(DEC)
    allowed_one = (position[None, None, :] <= position[None, :, None]) & (
        position[None, None, :] < own_len[:, None, None]
    )
    heads_q_one = split_heads(queries_one, item_count)
    heads_k_one = split_heads(keys_one, item_count)
    heads_v_one = split_heads(values_one, item_count)
    numer_one, total_one = attend_forward(heads_q_one, heads_k_one, heads_v_one, allowed_one)
    mixed_one = (numer_one / total_one[..., None]).reshape(rows_here, D).astype(jnp.bfloat16)
    resid_one = tokens_float + product(mixed_one, output_self) + shift_rows[2]
    hidden_one, normed_one, inverse_one = norm_forward(resid_one, gain_rows[0], shift_rows[7])
    hidden_one_low = hidden_one.astype(jnp.bfloat16)
    queries_two = ((product(hidden_one_low, query_cross) + shift_rows[3]) * 0.125).astype(
        jnp.bfloat16
    )
    queries_group = lax.all_gather(queries_two, "mem", axis=0, tiled=True)
    memory_flat = memory.reshape(-1, D)
    keys_two = product(memory_flat, key_cross).astype(jnp.bfloat16)
    values_two = (product(memory_flat, value_cross) + shift_rows[4]).astype(jnp.bfloat16)
    local_slot = member * mem_local + jnp.arange(mem_local)
    allowed_two = (local_slot[None, :] < mem_len[:, None])[:, None, :]
    heads_q_two = split_heads(queries_group, group_items)
    heads_k_two = split_heads(keys_two, group_items)
    heads_v_two = split_heads(values_two, group_items)
    numer_blocks, total_blocks = lax.map(
        cross_forward,
        (
            reshape_block(heads_q_two),
            reshape_block(heads_k_two),
            reshape_block(heads_v_two),
            reshape_block(allowed_two),
        ),
    )
    numer_part = merge_block(numer_blocks).reshape(group_items * DEC, D)
    total_part = merge_block(total_blocks).reshape(group_items * DEC, HEADS)
    numer_all, total_all = lax.psum((numer_part, total_part), "mem")
    numer_own = lax.dynamic_slice_in_dim(numer_all, member * rows_here, rows_here)
    total_own = lax.dynamic_slice_in_dim(total_all, member * rows_here, rows_here)
    numer_view = numer_own.reshape(rows_here, HEADS, HEAD_DIM)
    mixed_two = (numer_view / total_own[..., None]).reshape(rows_here, D).astype(jnp.bfloat16)
    resid_two = hidden_one + product(mixed_two, output_cross) + shift_rows[5]
    hidden_two, normed_two, inverse_two = norm_forward(resid_two, gain_rows[1], shift_rows[8])
    hidden_two_low = hidden_two.astype(jnp.bfloat16)
    inner_pre = product(hidden_two_low, feed_up) + inner_shift
    cdf_part = 0.5 * (1.0 + jax.scipy.special.erf(inner_pre * half_root))
    active_low = (inner_pre * cdf_part).astype(jnp.bfloat16)
    resid_three = hidden_two + product(active_low, feed_down) + shift_rows[6]
    layer_out, normed_three, inverse_three = norm_forward(resid_three, gain_rows[2], shift_rows[9])
    grad_three, gain_grad_three, shift_grad_three = norm_backward(
        cotangent.astype(jnp.float32), normed_three, inverse_three, gain_rows[2]
    )
    grad_down = grad_three.astype(jnp.bfloat16)
    feed_down_grad = left_product(active_low, grad_down)
    out_bias_grad = column_sums(grad_down)
    grad_active = right_product(grad_down, feed_down)
    slope = cdf_part + inner_pre * jnp.exp(-0.5 * inner_pre * inner_pre) * normal_peak
    grad_inner = (grad_active * slope).astype(jnp.bfloat16)
    feed_up_grad = left_product(hidden_two_low, grad_inner)
    inner_bias_grad = column_sums(grad_inner)
    grad_hidden_two = grad_three + right_product(grad_inner, feed_up)
    grad_two, gain_grad_two, shift_grad_two = norm_backward(
        grad_hidden_two, normed_two, inverse_two, gain_rows[1]
    )
    grad_cross_branch = grad_two.astype(jnp.bfloat16)
    output_cross_grad = left_product(mixed_two, grad_cross_branch)
    cross_out_bias_grad = column_sums(grad_cross_branch)
    grad_mixed_two = right_product(grad_cross_branch, output_cross).reshape(
        rows_here, HEADS, HEAD_DIM
    )
    grad_numer_two = (
        (grad_mixed_two / total_own[..., None]).reshape(rows_here, D).astype(jnp.bfloat16)
    )
    grad_total_two = (-jnp.sum(grad_mixed_two * numer_view, -1) / (total_own * total_own)).astype(
        jnp.bfloat16
    )
    numer_grad_group, total_grad_group = (
        lax.all_gather(grad_numer_two, "mem", axis=0, tiled=True),
        lax.all_gather(grad_total_two, "mem", axis=0, tiled=True),
    )
    heads_gn_two = split_heads(numer_grad_group, group_items)
    heads_gt_two = total_grad_group.reshape(group_items, DEC, HEADS)
    query_blocks, key_blocks, value_blocks = lax.map(
        cross_backward,
        (
            reshape_block(heads_q_two),
            reshape_block(heads_k_two),
            reshape_block(heads_v_two),
            reshape_block(allowed_two),
            reshape_block(heads_gn_two),
            reshape_block(heads_gt_two),
        ),
    )
    query_part = merge_block(query_blocks).reshape(group_items * DEC, D)
    key_grad_two = merge_block(key_blocks).reshape(group_items * mem_local, D).astype(jnp.bfloat16)
    value_grad_two = (
        merge_block(value_blocks).reshape(group_items * mem_local, D).astype(jnp.bfloat16)
    )
    query_own = lax.psum_scatter(query_part, "mem", scatter_dimension=0, tiled=True)
    query_grad_two = query_own.astype(jnp.bfloat16) * 0.125
    query_cross_grad = left_product(hidden_one_low, query_grad_two)
    cross_query_bias_grad = column_sums(query_grad_two)
    grad_hidden_one = grad_two + right_product(query_grad_two, query_cross)
    key_cross_grad = left_product(memory_flat, key_grad_two)
    value_cross_grad = left_product(memory_flat, value_grad_two)
    cross_value_bias_grad = column_sums(value_grad_two)
    memory_grad = (
        right_product(key_grad_two, key_cross) + right_product(value_grad_two, value_cross)
    ).reshape(group_items, mem_local, D)
    grad_one, gain_grad_one, shift_grad_one = norm_backward(
        grad_hidden_one, normed_one, inverse_one, gain_rows[0]
    )
    grad_self_branch = grad_one.astype(jnp.bfloat16)
    output_self_grad = left_product(mixed_one, grad_self_branch)
    self_out_bias_grad = column_sums(grad_self_branch)
    grad_mixed_one = right_product(grad_self_branch, output_self).reshape(
        item_count, DEC, HEADS, HEAD_DIM
    )
    grad_numer_one = (grad_mixed_one / total_one[..., None]).astype(jnp.bfloat16)
    grad_total_one = -jnp.sum(grad_mixed_one * numer_one, -1) / (total_one * total_one)
    query_grad_raw, key_grad_raw, value_grad_raw = attend_backward(
        heads_q_one, heads_k_one, heads_v_one, allowed_one, grad_numer_one, grad_total_one
    )
    query_grad_one = query_grad_raw.reshape(rows_here, D).astype(jnp.bfloat16) * 0.125
    key_grad_one = key_grad_raw.reshape(rows_here, D).astype(jnp.bfloat16)
    value_grad_one = value_grad_raw.reshape(rows_here, D).astype(jnp.bfloat16)
    tokens_grad = (
        grad_one
        + right_product(query_grad_one, query_self)
        + right_product(key_grad_one, key_self)
        + right_product(value_grad_one, value_self)
    )
    query_self_grad = left_product(tokens, query_grad_one)
    key_self_grad = left_product(tokens, key_grad_one)
    value_self_grad = left_product(tokens, value_grad_one)
    shift_grad_full = jnp.stack(
        [
            column_sums(query_grad_one),
            column_sums(value_grad_one),
            self_out_bias_grad,
            cross_query_bias_grad,
            cross_value_bias_grad,
            cross_out_bias_grad,
            out_bias_grad,
            shift_grad_one,
            shift_grad_two,
            shift_grad_three,
        ]
    )
    gain_grad_full = jnp.stack([gain_grad_one, gain_grad_two, gain_grad_three])
    vector_total = (
        lax.psum(shift_grad_full.astype(jnp.bfloat16), "mem").astype(jnp.float32),
        lax.psum(gain_grad_full.astype(jnp.bfloat16), "mem").astype(jnp.float32),
        lax.psum(inner_bias_grad.astype(jnp.bfloat16), "mem").astype(jnp.float32),
    )
    wide = (
        lax.psum_scatter(
            query_self_grad.astype(jnp.bfloat16), "items", scatter_dimension=0, tiled=True
        ).astype(jnp.float32),
        lax.psum_scatter(
            key_self_grad.astype(jnp.bfloat16), "items", scatter_dimension=0, tiled=True
        ).astype(jnp.float32),
        lax.psum_scatter(
            value_self_grad.astype(jnp.bfloat16), "items", scatter_dimension=0, tiled=True
        ).astype(jnp.float32),
        lax.psum_scatter(
            output_self_grad.astype(jnp.bfloat16), "items", scatter_dimension=0, tiled=True
        ).astype(jnp.float32),
        lax.psum_scatter(
            query_cross_grad.astype(jnp.bfloat16), "items", scatter_dimension=0, tiled=True
        ).astype(jnp.float32),
        lax.psum_scatter(
            key_cross_grad.astype(jnp.bfloat16), "items", scatter_dimension=0, tiled=True
        ).astype(jnp.float32),
        lax.psum_scatter(
            value_cross_grad.astype(jnp.bfloat16), "items", scatter_dimension=0, tiled=True
        ).astype(jnp.float32),
        lax.psum_scatter(
            output_cross_grad.astype(jnp.bfloat16), "items", scatter_dimension=0, tiled=True
        ).astype(jnp.float32),
        lax.psum_scatter(
            feed_up_grad.astype(jnp.bfloat16), "items", scatter_dimension=0, tiled=True
        ).astype(jnp.float32),
        lax.psum_scatter(
            feed_down_grad.astype(jnp.bfloat16), "items", scatter_dimension=0, tiled=True
        ).astype(jnp.float32),
        lax.psum_scatter(
            vector_total[0].astype(jnp.bfloat16), "items", scatter_dimension=1, tiled=True
        ).astype(jnp.float32),
        lax.psum_scatter(
            vector_total[1].astype(jnp.bfloat16), "items", scatter_dimension=1, tiled=True
        ).astype(jnp.float32),
        lax.psum_scatter(
            vector_total[2].astype(jnp.bfloat16), "items", scatter_dimension=0, tiled=True
        ).astype(jnp.float32),
    )
    narrow = (
        lax.psum_scatter(
            wide[0].astype(jnp.bfloat16), "mem", scatter_dimension=1, tiled=True
        ).astype(jnp.float32),
        lax.psum_scatter(
            wide[1].astype(jnp.bfloat16), "mem", scatter_dimension=1, tiled=True
        ).astype(jnp.float32),
        lax.psum_scatter(
            wide[2].astype(jnp.bfloat16), "mem", scatter_dimension=1, tiled=True
        ).astype(jnp.float32),
        lax.psum_scatter(
            wide[3].astype(jnp.bfloat16), "mem", scatter_dimension=1, tiled=True
        ).astype(jnp.float32),
        lax.psum_scatter(
            wide[4].astype(jnp.bfloat16), "mem", scatter_dimension=1, tiled=True
        ).astype(jnp.float32),
        lax.psum_scatter(
            wide[5].astype(jnp.bfloat16), "mem", scatter_dimension=1, tiled=True
        ).astype(jnp.float32),
        lax.psum_scatter(
            wide[6].astype(jnp.bfloat16), "mem", scatter_dimension=1, tiled=True
        ).astype(jnp.float32),
        lax.psum_scatter(
            wide[7].astype(jnp.bfloat16), "mem", scatter_dimension=1, tiled=True
        ).astype(jnp.float32),
        lax.psum_scatter(
            wide[8].astype(jnp.bfloat16), "mem", scatter_dimension=1, tiled=True
        ).astype(jnp.float32),
        lax.psum_scatter(
            wide[9].astype(jnp.bfloat16), "mem", scatter_dimension=1, tiled=True
        ).astype(jnp.float32),
    )
    final = (
        narrow[0],
        narrow[1],
        narrow[2],
        narrow[3],
        narrow[4],
        narrow[5],
        narrow[6],
        narrow[7],
        narrow[8],
        narrow[9],
        wide[10],
        wide[11],
        wide[12],
    )
    return (
        layer_out,
        tokens_grad,
        memory_grad,
        final[0],
        final[1],
        final[2],
        final[3],
        final[4],
        final[5],
        final[6],
        final[7],
        final[8],
        final[9],
        final[10],
        final[11],
        final[12],
    )


def solution(mesh):
    return jax.shard_map(
        body,
        mesh=mesh,
        in_specs=(
            P(("items", "mem"), None),
            P("items", "mem", None),
            P(("items", "mem"), None),
            P("items"),
            P("items"),
            P("items", "mem"),
            P("items", "mem"),
            P("items", "mem"),
            P("items", "mem"),
            P("items", "mem"),
            P("items", "mem"),
            P("items", "mem"),
            P("items", "mem"),
            P("items", "mem"),
            P("items", "mem"),
            P(None, "items"),
            P(None, "items"),
            P("items"),
        ),
        out_specs=(
            P(("items", "mem"), None),
            P(("items", "mem"), None),
            P("items", "mem", None),
            P("items", "mem"),
            P("items", "mem"),
            P("items", "mem"),
            P("items", "mem"),
            P("items", "mem"),
            P("items", "mem"),
            P("items", "mem"),
            P("items", "mem"),
            P("items", "mem"),
            P("items", "mem"),
            P(None, "items"),
            P(None, "items"),
            P("items"),
        ),
        check_vma=False,
    )
```

profile of v0, /device:TPU:0, one launch (start us, length us, event | category | flops | bytes accessed | tf_op | source)
XLA Modules:
  0.0 1651.8 jit_solution(3291153246775187423)
XLA Ops:
  7.3 17.6 %all_gather.81 = bf16[128,1024]{1,0:T(8,128)(2,1)} all-gather(bf16[128,256]{1,0:T(8,128)(2,1)} %param.27), channel_id=1, replica_groups=mesh['items'=8,'mem'=4] {'mem'}, dimensions={1}, use_global_device_ids=true | all-gather | bytes 327680 | tf_op jit(solution)/shard_map/all_gather | solution.py:129
  25.0 15.0 all_gather.83
  40.0 15.3 all_gather.78
  55.4 15.2 all_gather.85
  70.7 15.4 all_gather.90
  86.1 14.7 all_gather.88
  101.0 14.7 all_gather.93
  151.8 20.2 %all-gather.26.cloned.1.call-done = bf16[1024,1024]{1,0:T(8,128)(2,1)} async-done(((bf16[128,1024]{1,0:T(8,128)(2,1)}), bf16[1024,1024]{1,0:T(8,128)(2,1)}) %all-gather.26.cloned.1.call-update) | async-done | bytes 2097168 | tf_op jit(solution)/shard_map/all_gather | solution.py:145
  177.2 24.4 %all-gather.24.cloned.1.call-done = bf16[1024,1024]{1,0:T(8,128)(2,1)} async-done(((bf16[128,1024]{1,0:T(8,128)(2,1)}), bf16[1024,1024]{1,0:T(8,128)(2,1)}) %all-gather.24.cloned.1.call-update) | async-done | bytes 2097168 | tf_op jit(solution)/shard_map/all_gather | solution.py:147
  201.6 9.4 add_convert_fusion
  211.1 11.6 reshape.236
  222.6 10.4 copy.116
  242.4 11.5 reshape.238
  254.0 10.4 copy.118
  264.3 15.2 all-gather.28.cloned.1.call-done
  290.9 15.7 while.26
  322.2 17.5 %all_gather.95 = bf16[128,1024]{1,0:T(8,128)(2,1)} all-gather(bf16[128,256]{1,0:T(8,128)(2,1)S(1)} %copy-done.45), channel_id=1, replica_groups=mesh['items'=8,'mem'=4] {'mem'}, dimensions={1}, use_global_device_ids=true | all-gather | bytes 327680 | tf_op jit(solution)/shard_map/all_gather | solution.py:136
  350.9 150.5 %all-reduce.5.cloned.1.call-done = (f32[1024,16]{0,1:T(8,128)}, f32[1024,1024]{1,0:T(8,128)}) async-done(((f32[1024,16]{0,1:T(8,128)}, f32[1024,1024]{1,0:T(8,128)}), (f32[1024,16]{0,1:T(8,128)}, f32[1024,1024]{1,0:T(8,128)})) %all-reduce.5.cloned.1.call-update) | async-done | bytes 4259856 | tf_op jit(solution)/shard_map/psum | solution.py:218
  508.2 21.9 %all-gather.32.cloned.1.call-done = bf16[1024,1024]{1,0:T(8,128)(2,1)} async-done(((bf16[128,1024]{1,0:T(8,128)(2,1)}), bf16[1024,1024]{1,0:T(8,128)(2,1)}) %all-gather.32.cloned.1.call-update) | async-done | bytes 2097168 | tf_op jit(solution)/shard_map/all_gather | solution.py:148
  534.0 52.6 %all-gather.36.cloned.1.call-done = bf16[1024,4096]{1,0:T(8,128)(2,1)} async-done(((bf16[128,4096]{1,0:T(8,128)(2,1)}), bf16[1024,4096]{1,0:T(8,128)(2,1)}) %all-gather.36.cloned.1.call-update) | async-done | bytes 8388624 | tf_op jit(solution)/shard_map/all_gather | solution.py:149
  595.4 47.6 %all-gather.40.cloned.1.call-done = bf16[4096,1024]{1,0:T(8,128)(2,1)} async-done(((bf16[512,1024]{1,0:T(8,128)(2,1)}), bf16[4096,1024]{1,0:T(8,128)(2,1)}) %all-gather.40.cloned.1.call-update) | async-done | bytes 8388624 | tf_op jit(solution)/shard_map/all_gather | solution.py:150
  670.8 13.4 all_gather.103
  684.2 28.3 %all-gather.42.cloned.1.call-done = bf16[1024,1024]{1,0:T(8,128)(2,1)} async-done(((bf16[256,1024]{1,0:T(8,128)(2,1)}), bf16[1024,1024]{1,0:T(8,128)(2,1)}) %all-gather.42.cloned.1.call-update) | async-done | bytes 2097168 | tf_op jit(solution)/shard_map/all_gather | solution.py:259
  725.0 36.4 %while.27 = (s32[]{:T(128)}, f32[2,4,128,16,64]{2,1,0,4,3:T(4,128)}, bf16[2,4,256,16,64]{2,4,3,1,0:T(8,128)(2,1)}, bf16[2,4,256,16,64]{2,4,3,1,0:T(8,128)(2,1)},...) while((s32[]{:T(128)}, ...), condition=%wide.region_18.19_spmd, body=%wide.region_17.18_spmd.sunk | while | flops 1354768384 | bytes 163701072 | solution.py:264
  887.8 44.7 %reduce-scatter.76.cloned.1.call-done = bf16[128,1024]{1,0:T(8,128)(2,1)} async-done(((bf16[1024,1024]{1,0:T(8,128)(2,1)}), bf16[128,1024]{1,0:T(8,128)(2,1)}) %reduce-scatter.76.cloned.1.call-update) | async-done | bytes 262160
  934.3 42.7 %reduce-scatter.78.cloned.1.call-done = bf16[128,1024]{1,0:T(8,128)(2,1)} async-done(((bf16[1024,1024]{1,0:T(8,128)(2,1)}), bf16[128,1024]{1,0:T(8,128)(2,1)}) %reduce-scatter.78.cloned.1.call-update) | async-done | bytes 262160
  994.1 58.5 %reduce-scatter.62.cloned.1.call-done = bf16[128,4096]{1,0:T(8,128)(2,1)} async-done(((bf16[1024,4096]{1,0:T(8,128)(2,1)}), bf16[128,4096]{1,0:T(8,128)(2,1)}) %reduce-scatter.62.cloned.1.call-update) | async-done | bytes 1048592 | tf_op jit(solution)/shard_map/reduce_scatter | solution.py:362
  1052.6 74.7 %reduce-scatter.66.cloned.1.call-done = bf16[512,1024]{1,0:T(8,128)(2,1)} async-done(((bf16[4096,1024]{1,0:T(8,128)(2,1)}), bf16[512,1024]{1,0:T(8,128)(2,1)}) %reduce-scatter.66.cloned.1.call-update) | async-done | bytes 1048592 | tf_op jit(solution)/shard_map/reduce_scatter | solution.py:365
  1127.4 44.8 %reduce-scatter.50.cloned.1.call-done = bf16[128,1024]{1,0:T(8,128)(2,1)} async-done(((bf16[1024,1024]{1,0:T(8,128)(2,1)}), bf16[128,1024]{1,0:T(8,128)(2,1)}) %reduce-scatter.50.cloned.1.call-update) | async-done | bytes 262160 | tf_op jit(solution)/shard_map/reduce_scatter | solution.py:350
  1172.3 44.5 %reduce-scatter.46.cloned.1.call-done = bf16[128,1024]{1,0:T(8,128)(2,1)} async-done(((bf16[1024,1024]{1,0:T(8,128)(2,1)}), bf16[128,1024]{1,0:T(8,128)(2,1)}) %reduce-scatter.46.cloned.1.call-update) | async-done | bytes 262160 | tf_op jit(solution)/shard_map/reduce_scatter | solution.py:347
  1218.1 13.0 all-reduce
  1231.2 30.3 %reduce-scatter.74.cloned.1.call-done = bf16[128,1024]{1,0:T(8,128)(2,1)} async-done(((bf16[1024,1024]{1,0:T(8,128)(2,1)}), bf16[128,1024]{1,0:T(8,128)(2,1)}) %reduce-scatter.74.cloned.1.call-update) | async-done | bytes 262160
  1263.4 10.9 fusion.117
  1274.3 31.8 %reduce-scatter.72.cloned.1.call-done = bf16[128,1024]{1,0:T(8,128)(2,1)} async-done(((bf16[1024,1024]{1,0:T(8,128)(2,1)}), bf16[128,1024]{1,0:T(8,128)(2,1)}) %reduce-scatter.72.cloned.1.call-update) | async-done | bytes 262160
  1308.1 13.2 convolution_add_fusion.1
  1329.5 18.5 %reduce-scatter.54.cloned.1.call-done = bf16[128,256]{0,1:T(8,128)(2,1)} async-done(((bf16[128,1024]{0,1:T(8,128)(2,1)}), bf16[128,256]{0,1:T(8,128)(2,1)}) %reduce-scatter.54.cloned.1.call-update) | async-done | bytes 65552 | tf_op jit(solution)/shard_map/reduce_scatter | solution.py:394
  1349.7 18.6 %reduce-scatter.56.cloned.1.call-done = bf16[128,256]{0,1:T(8,128)(2,1)} async-done(((bf16[128,1024]{0,1:T(8,128)(2,1)}), bf16[128,256]{0,1:T(8,128)(2,1)}) %reduce-scatter.56.cloned.1.call-update) | async-done | bytes 65552 | tf_op jit(solution)/shard_map/reduce_scatter | solution.py:397
  1373.2 37.9 %reduce-scatter.70.cloned.1.call-done = bf16[128,1024]{1,0:T(8,128)(2,1)} async-done(((bf16[1024,1024]{1,0:T(8,128)(2,1)}), bf16[128,1024]{1,0:T(8,128)(2,1)}) %reduce-scatter.70.cloned.1.call-update) | async-done | bytes 262160
  1417.3 30.6 %reduce-scatter.82.cloned.1.call-done = bf16[128,3]{1,0:T(8,128)(2,1)} async-done(((bf16[1024,3]{1,0:T(8,128)(2,1)}), bf16[128,3]{1,0:T(8,128)(2,1)}) %reduce-scatter.82.cloned.1.call-update) | async-done | bytes 784
  1448.7 35.9 %reduce-scatter.80.cloned.1.call-done = bf16[128,10]{1,0:T(8,128)(2,1)} async-done(((bf16[1024,10]{1,0:T(8,128)(2,1)}), bf16[128,10]{1,0:T(8,128)(2,1)}) %reduce-scatter.80.cloned.1.call-update) | async-done | bytes 2576
  1485.4 12.0 all-reduce.2
  1499.1 15.0 reduce-scatter.64.cloned.1.call-done
  1515.9 26.2 %reduce-scatter.68.cloned.1.call-done = bf16[512,256]{1,0:T(8,128)(2,1)} async-done(((bf16[512,1024]{1,0:T(8,128)(2,1)}), bf16[512,256]{1,0:T(8,128)(2,1)}) %reduce-scatter.68.cloned.1.call-update) | async-done | bytes 262160 | tf_op jit(solution)/shard_map/reduce_scatter | solution.py:406
  1543.9 18.9 %reduce-scatter.52.cloned.1.call-done = bf16[128,256]{1,0:T(8,128)(2,1)} async-done(((bf16[128,1024]{1,0:T(8,128)(2,1)}), bf16[128,256]{1,0:T(8,128)(2,1)}) %reduce-scatter.52.cloned.1.call-update) | async-done | bytes 65552 | tf_op jit(solution)/shard_map/reduce_scatter | solution.py:391
  1564.3 18.7 %reduce-scatter.48.cloned.1.call-done = bf16[128,256]{1,0:T(8,128)(2,1)} async-done(((bf16[128,1024]{1,0:T(8,128)(2,1)}), bf16[128,256]{1,0:T(8,128)(2,1)}) %reduce-scatter.48.cloned.1.call-update) | async-done | bytes 65552 | tf_op jit(solution)/shard_map/reduce_scatter | solution.py:388
  1584.5 18.6 %reduce-scatter.44.cloned.1.call-done = bf16[128,256]{0,1:T(8,128)(2,1)} async-done(((bf16[128,1024]{0,1:T(8,128)(2,1)}), bf16[128,256]{0,1:T(8,128)(2,1)}) %reduce-scatter.44.cloned.1.call-update) | async-done | bytes 65552 | tf_op jit(solution)/shard_map/reduce_scatter | solution.py:385
  1604.7 18.3 %reduce-scatter.42.cloned.1.call-done = bf16[128,256]{0,1:T(8,128)(2,1)} async-done(((bf16[128,1024]{0,1:T(8,128)(2,1)}), bf16[128,256]{0,1:T(8,128)(2,1)}) %reduce-scatter.42.cloned.1.call-update) | async-done | bytes 65552 | tf_op jit(solution)/shard_map/reduce_scatter | solution.py:382
  1624.7 18.8 %reduce-scatter.40.cloned.1.call-done = bf16[128,256]{0,1:T(8,128)(2,1)} async-done(((bf16[128,1024]{0,1:T(8,128)(2,1)}), bf16[128,256]{0,1:T(8,128)(2,1)}) %reduce-scatter.40.cloned.1.call-update) | async-done | bytes 65552 | tf_op jit(solution)/shard_map/reduce_scatter | solution.py:379
  (429 shorter events, 385.0 us)
Async XLA Ops:
  7.2 126.4 %copy-start.65 = (s32[8]{0:T(128)S(1)}, s32[8]{0:T(128)}, u32[]{:S(2)}) copy-start(s32[8]{0:T(128)} %param.26) | copy-start | bytes 100
  7.2 126.8 %copy-start.11 = (bf16[256,1024]{1,0:T(8,128)(2,1)S(1)}, bf16[256,1024]{1,0:T(8,128)(2,1)}, u32[]{:S(2)}) copy-start(bf16[256,1024]{1,0:T(8,128)(2,1)} %param.22) | copy-start | bytes 1572868
  7.2 126.7 %all-gather.18.cloned.1.call-start = ((), (), s32[]{:S(2)}) async-start(), calls=%async_computation.24 | async-start | bytes 2359296 | tf_op jit(solution)/shard_map/all_gather | solution.py:141
  24.9 112.9 %all-gather.20.cloned.1.call-start = ((), (), s32[]{:S(2)}) async-start(), calls=%async_computation.25 | async-start | bytes 2359296 | tf_op jit(solution)/shard_map/all_gather | solution.py:142
  40.0 101.9 %all-gather.16.cloned.1.call-start = ((), (), s32[]{:S(2)}) async-start(), calls=%async_computation.23 | async-start | bytes 2359296 | tf_op jit(solution)/shard_map/all_gather | solution.py:143
  55.4 93.5 %all-gather.22.cloned.1.call-start = ((), (), s32[]{:S(2)}) async-start(), calls=%async_computation.26 | async-start | bytes 2359296 | tf_op jit(solution)/shard_map/all_gather | solution.py:144
  70.6 101.3 %all-gather.26.cloned.1.call-start = ((), (), s32[]{:S(2)}) async-start(), calls=%async_computation.28 | async-start | bytes 2359296 | tf_op jit(solution)/shard_map/all_gather | solution.py:145
  86.1 115.6 %all-gather.24.cloned.1.call-start = ((), (), s32[]{:S(2)}) async-start(), calls=%async_computation.27 | async-start | bytes 2359296 | tf_op jit(solution)/shard_map/all_gather | solution.py:147
  100.9 132.1 %all-gather.30.cloned.1.call-start = ((), (), s32[]{:S(2)}) async-start(), calls=%async_computation.30 | async-start | bytes 2359296 | tf_op jit(solution)/shard_map/all_gather | solution.py:146
  115.7 163.9 %all-gather.28.cloned.1.call-start = ((), (), s32[]{:S(2)}) async-start(), calls=%async_computation.29 | async-start | bytes 2621440 | tf_op jit(solution)/shard_map/all_gather | solution.py:198
  133.7 396.4 %copy-start.46 = (f32[1,1024]{1,0:T(1,128)}, f32[1,1024]{1,0:T(1,128)S(1)}, u32[]{:S(2)}) copy-start(f32[1,1024]{1,0:T(1,128)S(1)} %get-tuple-element.286) | copy-start | bytes 12292
  133.9 396.2 %copy-start.50 = (f32[1,1024]{1,0:T(1,128)}, f32[1,1024]{1,0:T(1,128)S(1)}, u32[]{:S(2)}) copy-start(f32[1,1024]{1,0:T(1,128)S(1)} %get-tuple-element.278) | copy-start | bytes 12292
  133.9 509.0 %copy-start.41 = (f32[1,1024]{1,0:T(1,128)}, f32[1,1024]{1,0:T(1,128)S(1)}, u32[]{:S(2)}) copy-start(f32[1,1024]{1,0:T(1,128)S(1)} %get-tuple-element.276) | copy-start | bytes 12292
  151.5 378.7 %copy-start.4 = (f32[256,1024]{1,0:T(8,128)}, f32[256,1024]{1,0:T(8,128)S(1)}, u32[]{:S(2)}) copy-start(f32[256,1024]{1,0:T(8,128)S(1)} %get-tuple-element.292) | copy-start | bytes 3145732
  151.5 378.7 %copy-start.48 = (f32[256]{0:T(256)}, f32[256]{0:T(256)S(1)}, u32[]{:S(2)}) copy-start(f32[256]{0:T(256)S(1)} %broadcast_multiply_fusion.8) | copy-start | bytes 3076
  151.8 378.4 %copy-start.52 = (f32[256]{0:T(256)}, f32[256]{0:T(256)S(1)}, u32[]{:S(2)}) copy-start(f32[256]{0:T(256)S(1)} %add_rsqrt_fusion.2) | copy-start | bytes 3076
  175.2 164.7 %all-gather.34.cloned.1.call-start = ((), (), s32[]{:S(2)}) async-start(), calls=%async_computation.32 | async-start | bytes 1310720 | tf_op jit(solution)/shard_map/all_gather | solution.py:137
  175.9 165.8 %all-gather.38.cloned.1.call-start = ((), (), s32[]{:S(2)}) async-start(), calls=%async_computation.34 | async-start | bytes 1310720 | tf_op jit(solution)/shard_map/all_gather | solution.py:138
  176.5 324.9 %all-reduce.5.cloned.1.call-start = ((), (), s32[]{:S(2)}) async-start(), calls=%async_computation.60 | async-start | bytes 8519680 | tf_op jit(solution)/shard_map/psum | solution.py:218
  322.1 208.1 %all-gather.32.cloned.1.call-start = ((), (), s32[]{:S(2)}) async-start(), calls=%async_computation.31 | async-start | bytes 2359296 | tf_op jit(solution)/shard_map/all_gather | solution.py:148
  339.8 246.8 %all-gather.36.cloned.1.call-start = ((), (), s32[]{:S(2)}) async-start(), calls=%async_computation.33 | async-start | bytes 9437184 | tf_op jit(solution)/shard_map/all_gather | solution.py:149
  340.5 302.4 %all-gather.40.cloned.1.call-start = ((), (), s32[]{:S(2)}) async-start(), calls=%async_computation.35 | async-start | bytes 9437184 | tf_op jit(solution)/shard_map/all_gather | solution.py:150
  341.7 370.8 %all-gather.42.cloned.1.call-start = ((), (), s32[]{:S(2)}) async-start(), calls=%async_computation.36 | async-start | bytes 2621440 | tf_op jit(solution)/shard_map/all_gather | solution.py:259
  666.2 179.7 %reduce-scatter.38.cloned.1.call-start = ((), (), s32[]{:S(2)}) async-start(), calls=%async_computation.37 | async-start | bytes 5242880 | tf_op jit(solution)/shard_map/reduce_scatter | solution.py:280
  766.9 120.8 %reduce-scatter.58.cloned.1.call-start = ((), (), s32[]{:S(2)}) async-start(), calls=%async_computation.47 | async-start | bytes 2359296 | tf_op jit(solution)/shard_map/reduce_scatter | solution.py:359
  770.4 162.1 %reduce-scatter.76.cloned.1.call-start = ((), (), s32[]{:S(2)}) async-start(), calls=%async_computation.56 | async-start | bytes 2359296
  800.4 176.6 %reduce-scatter.78.cloned.1.call-start = ((), (), s32[]{:S(2)}) async-start(), calls=%async_computation.57 | async-start | bytes 2359296
  829.7 222.9 %reduce-scatter.62.cloned.1.call-start = ((), (), s32[]{:S(2)}) async-start(), calls=%async_computation.49 | async-start | bytes 9437184 | tf_op jit(solution)/shard_map/reduce_scatter | solution.py:362
  837.2 290.1 %reduce-scatter.66.cloned.1.call-start = ((), (), s32[]{:S(2)}) async-start(), calls=%async_computation.51 | async-start | bytes 9437184 | tf_op jit(solution)/shard_map/reduce_scatter | solution.py:365
  845.8 326.5 %reduce-scatter.50.cloned.1.call-start = ((), (), s32[]{:S(2)}) async-start(), calls=%async_computation.43 | async-start | bytes 2359296 | tf_op jit(solution)/shard_map/reduce_scatter | solution.py:350
  850.5 366.3 %reduce-scatter.46.cloned.1.call-start = ((), (), s32[]{:S(2)}) async-start(), calls=%async_computation.41 | async-start | bytes 2359296 | tf_op jit(solution)/shard_map/reduce_scatter | solution.py:347
  855.9 405.6 %reduce-scatter.74.cloned.1.call-start = ((), (), s32[]{:S(2)}) async-start(), calls=%async_computation.55 | async-start | bytes 2359296
  871.7 434.4 %reduce-scatter.72.cloned.1.call-start = ((), (), s32[]{:S(2)}) async-start(), calls=%async_computation.54 | async-start | bytes 2359296
  884.5 443.5 %reduce-scatter.60.cloned.1.call-start = ((), (), s32[]{:S(2)}) async-start(), calls=%async_computation.48 | async-start | bytes 327680 | tf_op jit(solution)/shard_map/reduce_scatter | solution.py:400
  887.7 460.3 %reduce-scatter.54.cloned.1.call-start = ((), (), s32[]{:S(2)}) async-start(), calls=%async_computation.45 | async-start | bytes 327680 | tf_op jit(solution)/shard_map/reduce_scatter | solution.py:394
  934.3 434.0 %reduce-scatter.56.cloned.1.call-start = ((), (), s32[]{:S(2)}) async-start(), calls=%async_computation.46 | async-start | bytes 327680 | tf_op jit(solution)/shard_map/reduce_scatter | solution.py:397
  978.8 432.3 %reduce-scatter.70.cloned.1.call-start = ((), (), s32[]{:S(2)}) async-start(), calls=%async_computation.53 | async-start | bytes 2359296
  987.7 460.2 %reduce-scatter.82.cloned.1.call-start = ((), (), s32[]{:S(2)}) async-start(), calls=%async_computation.59 | async-start | bytes 294912
  987.9 229.0 %copy-start.67 = (u32[32]{0:T(128)S(1)}, u32[32]{0:T(128)}, u32[]{:S(2)}) copy-start(u32[32]{0:T(128)} %constant.97) | copy-start | bytes 388
  987.9 230.2 %copy-start.56 = (bf16[4096]{0:T(1024)(128)(2,1)S(1)}, bf16[4096]{0:T(1024)(128)(2,1)}, u32[]{:S(2)}) copy-start(bf16[4096]{0:T(1024)(128)(2,1)} %get-tuple-element.305) | copy-start | bytes 24580
  992.6 492.0 %reduce-scatter.80.cloned.1.call-start = ((), (), s32[]{:S(2)}) async-start(), calls=%async_computation.58 | async-start | bytes 294912
  994.0 520.1 %reduce-scatter.64.cloned.1.call-start = ((), (), s32[]{:S(2)}) async-start(), calls=%async_computation.50 | async-start | bytes 1310720 | tf_op jit(solution)/shard_map/reduce_scatter | solution.py:403
  1052.6 489.5 %reduce-scatter.68.cloned.1.call-start = ((), (), s32[]{:S(2)}) async-start(), calls=%async_computation.52 | async-start | bytes 1310720 | tf_op jit(solution)/shard_map/reduce_scatter | solution.py:406
  1127.4 435.4 %reduce-scatter.52.cloned.1.call-start = ((), (), s32[]{:S(2)}) async-start(), calls=%async_computation.44 | async-start | bytes 327680 | tf_op jit(solution)/shard_map/reduce_scatter | solution.py:391
  1172.3 410.8 %reduce-scatter.48.cloned.1.call-start = ((), (), s32[]{:S(2)}) async-start(), calls=%async_computation.42 | async-start | bytes 327680 | tf_op jit(solution)/shard_map/reduce_scatter | solution.py:388
  1216.8 386.3 %reduce-scatter.44.cloned.1.call-start = ((), (), s32[]{:S(2)}) async-start(), calls=%async_computation.40 | async-start | bytes 327680 | tf_op jit(solution)/shard_map/reduce_scatter | solution.py:385
  1263.3 359.7 %reduce-scatter.42.cloned.1.call-start = ((), (), s32[]{:S(2)}) async-start(), calls=%async_computation.39 | async-start | bytes 327680 | tf_op jit(solution)/shard_map/reduce_scatter | solution.py:382
  1307.9 335.5 %reduce-scatter.40.cloned.1.call-start = ((), (), s32[]{:S(2)}) async-start(), calls=%async_computation.38 | async-start | bytes 327680 | tf_op jit(solution)/shard_map/reduce_scatter | solution.py:379
  (73 other events, 929.5 us)
Sparse Core Ops, SparseCore 0:
  25.0 27.9 all-gather.17
  54.9 27.8 all-gather.19
  84.7 27.8 all-gather.15
  114.4 27.8 all-gather.21
  144.0 27.8 all-gather.25
  173.7 27.8 all-gather.23
  203.5 27.8 all-gather.29
  233.6 45.9 all-gather.27
  281.2 26.6 all-gather.33
  309.2 32.4 all-gather.37
  344.7 156.5 all-reduce.4
  503.3 26.8 all-gather.31
  532.2 54.3 all-gather.35
  588.5 54.3 all-gather.39
  666.3 46.2 all-gather.41
  767.0 75.7 reduce-scatter.37
  845.9 41.7 reduce-scatter.57
  891.2 41.2 reduce-scatter.75
  935.7 41.1 reduce-scatter.77
  981.2 71.2 reduce-scatter.61
  1056.0 71.2 reduce-scatter.65
  1131.0 41.2 reduce-scatter.49
  1175.5 41.2 reduce-scatter.45
  1220.3 41.2 reduce-scatter.73
  1264.8 41.2 reduce-scatter.71
  1308.3 19.6 reduce-scatter.59
  1330.1 17.8 reduce-scatter.53
  1350.4 17.7 reduce-scatter.55
  1371.5 39.5 reduce-scatter.69
  1414.2 33.5 reduce-scatter.81
  1450.9 33.6 reduce-scatter.79
  1487.0 27.1 reduce-scatter.63
  1516.3 25.7 reduce-scatter.67
  1544.5 18.3 reduce-scatter.51
  1565.1 17.9 reduce-scatter.47
  1585.2 17.8 reduce-scatter.43
  1605.3 17.7 reduce-scatter.41
  1625.4 17.9 reduce-scatter.39
where the time goes:
time: 1660 us; the launch traced here: 1650 us
  waiting for transfers between devices  1020 us (61%)
  local copies, waits for them, and re-layouts  200 us (12%)
  matrix products  193 us (12%)
  blocking collectives  191 us (12%)
  other arithmetic  25.6 us (2%)
    unnamed x45, waiting for transfers between devices  256 us
    psum x1, waiting for transfers between devices, body(): numer_all, total_all = lax.psum((numer_part, total_part), 'mem')  150 us
    reduce_scatter x1, waiting for transfers between devices, body(): lax.psum_scatter(feed_down_grad.astype(jnp.bfloat16), 'items', scatter_di...  74.7 us
    reduce_scatter x1, waiting for transfers between devices, body(): lax.psum_scatter(feed_up_grad.astype(jnp.bfloat16), 'items', scatter_dime...  58.5 us
    all_gather x1, waiting for transfers between devices, body(): lax.all_gather(cols_whole[8], 'items', axis=0, tiled=True)  52.6 us
    dot_general x10, matrix products, product(): return jnp.dot(first_op, second_op, preferred_element_type=jnp.float32)  49.9 us
    dot_general x10, matrix products, right_product(): lax.dot_general(first_op, second_op, (((1,), (1,)), ((), ())), preferred_...  49.3 us
    all_gather x1, waiting for transfers between devices, body(): lax.all_gather(cols_whole[9], 'items', axis=0, tiled=True)  47.6 us
  transfers between devices with their start and end apart: 38, of which 31 were waited for; matrix products, arithmetic and copies ran while one was open for 20% of the time, Pallas kernels for 0%

commit v1 on v0

v1 whole, which is shorter than its diff:
```python
import functools

import jax
import jax.numpy as jnp
from jax import lax
from jax.experimental import pallas as pl
from jax.experimental.pallas import tpu as pltpu
from jax.sharding import PartitionSpec as P

D = 1024
HEADS = 16
HEAD_DIM = 64
PAIR = 2 * HEAD_DIM
PAIRS = HEADS // 2
DEC = 128
half_root = 0.7071067811865476
normal_peak = 0.3989422804014327
MESH = pl.DeviceIdType.MESH
F32 = jnp.float32
BF16 = jnp.bfloat16
ANY = pl.BlockSpec(memory_space=pl.ANY)


def product(first_op, second_op):
    return jnp.dot(first_op, second_op, preferred_element_type=F32)


def left_product(first_op, second_op):
    return lax.dot_general(
        first_op, second_op, (((0,), (0,)), ((), ())), preferred_element_type=F32
    )


def right_product(first_op, second_op):
    return lax.dot_general(
        first_op, second_op, (((1,), (1,)), ((), ())), preferred_element_type=F32
    )


def column_sums(values):
    return jnp.sum(values.astype(F32), 0)


def norm_forward(values, gain, shift):
    center = values - jnp.mean(values, -1, keepdims=True)
    inverse = lax.rsqrt(jnp.mean(center * center, -1, keepdims=True) + 1e-05)
    normed = center * inverse
    return (normed * gain + shift, normed, inverse)


def norm_backward(grad_out, normed, inverse, gain):
    scaled = grad_out * gain
    grad_in = inverse * (
        scaled
        - jnp.mean(scaled, -1, keepdims=True)
        - normed * jnp.mean(scaled * normed, -1, keepdims=True)
    )
    return (grad_in, jnp.sum(grad_out * normed, 0), jnp.sum(grad_out, 0))


def gather_kernel(members, items_here, units, *refs):
    count = len(units)
    weights = 1 + max(unit[0] for unit in units)
    shard_refs, memory_ref = refs[:weights], refs[weights]
    whole_refs, items_ref = refs[weights + 1 : 2 * weights + 1], refs[2 * weights + 1]
    send_sem, recv_sem, copy_sem, mem_send, mem_recv, mem_copy = refs[2 * weights + 2 :]
    row = lax.axis_index("items")
    member = lax.axis_index("mem")
    hops = members - 1
    core_peer, first_peer, second_peer = row ^ 1, row ^ 2, row ^ 4
    UP, DOWN = 0, hops
    ALONG_X, ALONG_Y, HALF_A, HALF_B, CORE = 2 * hops, 2 * hops + 1, 2 * hops + 2, 2 * hops + 3, 2 * hops + 4

    barrier = pltpu.get_barrier_semaphore()
    partners = [(core_peer, member), (first_peer, member), (second_peer, member)]
    partners += [(row, lax.rem(member + step, members)) for step in range(1, members)]
    for partner in partners:
        pl.semaphore_signal(barrier, inc=1, device_id=partner, device_id_type=MESH)
    pl.semaphore_wait(barrier, len(partners))

    def place(unit, owner):
        weight, start, depth, height = units[unit]
        return pl.ds(pl.multiple_of(owner * height + start, depth), depth)

    def cols(unit, who):
        width = shard_refs[units[unit][0]].shape[1]
        return pl.ds(pl.multiple_of(who * width, width), width)

    def shard(unit):
        weight, start, depth, height = units[unit]
        return shard_refs[weight].at[pl.ds(start, depth)]

    def remote(unit, kind, src, dst, device):
        return pltpu.make_async_remote_copy(
            src_ref=src,
            dst_ref=dst,
            send_sem=send_sem.at[unit, kind],
            recv_sem=recv_sem.at[unit, kind],
            device_id=device,
            device_id_type=MESH,
        )

    def along(unit, hop, upward):
        whole = whole_refs[units[unit][0]]
        origin = member - hop if upward else member + hop
        origin = jnp.clip(origin, 0, members - 1)
        piece = whole.at[place(unit, row), cols(unit, origin)]
        target = jnp.clip(member + 1 if upward else member - 1, 0, members - 1)
        return remote(
            unit, (UP if upward else DOWN) + hop, shard(unit) if hop == 0 else piece, piece, (row, target)
        )

    def along_start(unit, hop):
        @pl.when((member >= hop) & (member < members - 1))
        def _():
            along(unit, hop, True).start()

        @pl.when((member <= members - 1 - hop) & (member > 0))
        def _():
            along(unit, hop, False).start()

    def along_arrive(unit, hop):
        @pl.when(member >= hop + 1)
        def _():
            along(unit, hop, True).wait_recv()

        @pl.when(member <= members - 2 - hop)
        def _():
            along(unit, hop, False).wait_recv()

    def along_sent(unit, hop):
        @pl.when((member >= hop) & (member < members - 1))
        def _():
            along(unit, hop, True).wait_send()

        @pl.when((member <= members - 1 - hop) & (member > 0))
        def _():
            along(unit, hop, False).wait_send()

    def own_copy(unit):
        return pltpu.make_async_copy(
            shard(unit), whole_refs[units[unit][0]].at[place(unit, row), cols(unit, member)], copy_sem.at[unit]
        )

    def block(unit, kind, owner, device, half=None):
        weight, start, depth, height = units[unit]
        if half is None:
            rows = place(unit, owner)
        else:
            part = depth // 2
            rows = pl.ds(pl.multiple_of(owner * height + start + half * part, part), part)
        ref = whole_refs[weight].at[rows]
        return remote(unit, kind, ref, ref, (device, member))

    def to_x(unit):
        return block(unit, ALONG_X, row, first_peer)

    def to_y(unit):
        return block(unit, ALONG_Y, row, second_peer)

    def half_a(unit):
        return block(unit, HALF_A, first_peer, second_peer, 0)

    def half_b(unit):
        return block(unit, HALF_B, second_peer, first_peer, 1)

    def to_core(unit, which):
        owner = (row, first_peer, second_peer, row ^ 6)[which]
        return block(unit, CORE + which, owner, core_peer)

    pieces = memory_ref.shape[1] // 32 * items_here

    def memory_send(piece, step):
        which, start = piece // (pieces // items_here), piece % (pieces // items_here) * 32
        target = lax.rem(member + step, members)
        return pltpu.make_async_remote_copy(
            src_ref=memory_ref.at[target * items_here + which, pl.ds(start, 32)],
            dst_ref=items_ref.at[which, step, pl.ds(start, 32)],
            send_sem=mem_send.at[piece, step],
            recv_sem=mem_recv.at[piece, step],
            device_id=(row, target),
            device_id_type=MESH,
        )

    local = pltpu.make_async_copy(
        memory_ref.at[pl.ds(member * items_here, items_here)], items_ref.at[:, 0], mem_copy
    )
    local.start()

    depth_ticks = hops + 3
    for tick in range(max(count + depth_ticks, pieces)):
        unit = tick
        if unit < count:
            along_start(unit, 0)
            own_copy(unit).start()
        if tick < pieces:
            for step in range(1, members):
                memory_send(tick, step).start()
        for hop in range(1, hops):
            unit = tick - hop
            if 0 <= unit < count:
                along_arrive(unit, hop - 1)
                along_start(unit, hop)
        unit = tick - hops
        if 0 <= unit < count:
            along_arrive(unit, hops - 1)
            own_copy(unit).wait()
            to_x(unit).start()
            to_y(unit).start()
            to_core(unit, 0).start()
        unit = tick - hops - 1
        if 0 <= unit < count:
            to_x(unit).wait_recv()
            half_a(unit).start()
            to_core(unit, 1).start()
            to_y(unit).wait_recv()
            half_b(unit).start()
            to_core(unit, 2).start()
        unit = tick - hops - 2
        if 0 <= unit < count:
            half_a(unit).wait_recv()
            half_b(unit).wait_recv()
            to_core(unit, 3).start()
    for unit in range(count):
        for hop in range(hops):
            along_sent(unit, hop)
        to_x(unit).wait_send()
        to_y(unit).wait_send()
        half_a(unit).wait_send()
        half_b(unit).wait_send()
        for which in range(4):
            to_core(unit, which).wait()
    for piece in range(pieces):
        for step in range(1, members):
            memory_send(piece, step).wait()
    local.wait()


def gather_by_kernel(shards, memory, items_count, members):
    items_here = memory.shape[0] // members
    units = []
    for weight, shard in enumerate(shards):
        height, width = shard.shape
        depth = height * 256 // max(height * width // 128, 256)
        for start in range(0, height, depth):
            units.append((weight, start, depth, height))
    pieces = memory.shape[1] // 32 * items_here
    hops = members - 1
    kinds = 2 * hops + 8
    out_shape = [jax.ShapeDtypeStruct((s.shape[0] * items_count, s.shape[1] * members), s.dtype) for s in shards]
    out_shape.append(
        jax.ShapeDtypeStruct((items_here, members, memory.shape[1], memory.shape[2]), memory.dtype)
    )
    outs = pl.pallas_call(
        functools.partial(gather_kernel, members, items_here, tuple(units)),
        out_shape=out_shape,
        in_specs=[ANY] * (len(shards) + 1),
        out_specs=[ANY] * len(out_shape),
        scratch_shapes=[
            pltpu.SemaphoreType.DMA((len(units), kinds)),
            pltpu.SemaphoreType.DMA((len(units), kinds)),
            pltpu.SemaphoreType.DMA((len(units),)),
            pltpu.SemaphoreType.DMA((pieces, members)),
            pltpu.SemaphoreType.DMA((pieces, members)),
            pltpu.SemaphoreType.DMA,
        ],
        compiler_params=pltpu.CompilerParams(collective_id=0, has_side_effects=True),
        name="gather_all",
    )(*shards, memory)
    return outs[:-1], outs[-1]


def gather_by_collectives(shards, memory, items_count, members):
    whole = []
    for shard in shards:
        cols = lax.all_gather(shard, "mem", axis=1, tiled=True)
        whole.append(lax.all_gather(cols, "items", axis=0, tiled=True))
    items_here = memory.shape[0] // members
    member = lax.axis_index("mem")
    parts = []
    for step in range(members):
        target = lax.rem(member + step, members)
        part = lax.dynamic_slice_in_dim(memory, target * items_here, items_here)
        if step:
            part = lax.ppermute(part, "mem", [(a, (a + step) % members) for a in range(members)])
        parts.append(part)
    return whole, jnp.stack(parts, 1)


def stack_pair(values, lane_low):
    zero = jnp.zeros_like(values)
    return jnp.concatenate([jnp.where(lane_low, values, zero), jnp.where(lane_low, zero, values)], 0)


def low_lanes(rows):
    return lax.broadcasted_iota(jnp.int32, (rows, PAIR), 1) < HEAD_DIM


def allowed_slots(causal, chunk, lens_ref, bases_ref, which, step, key_dim):
    shape = (2 * DEC, chunk) if key_dim == 1 else (chunk, 2 * DEC)
    slot = lax.broadcasted_iota(jnp.int32, shape, key_dim)
    if causal:
        query = lax.broadcasted_iota(jnp.int32, shape, 1 - key_dim) % DEC
        return (slot <= query) & (slot < lens_ref[which])
    return slot < lens_ref[which] - bases_ref[step]


def attend_forward_kernel(causal, chunk, lens_ref, bases_ref, q_ref, k_ref, v_ref, mixed_ref, exact_ref, scale_ref):
    which = pl.program_id(0)
    lane_low = low_lanes(DEC)
    q2 = stack_pair(q_ref[...], lane_low)
    numer = jnp.zeros((2 * DEC, PAIR), F32)
    total = jnp.zeros((2 * DEC, 1), F32)
    for step in range(k_ref.shape[0] // chunk):
        rows = pl.ds(step * chunk, chunk)
        scores = right_product(q2, k_ref[rows, :])
        allowed = allowed_slots(causal, chunk, lens_ref, bases_ref, which, step, 1)
        exp_scores = jnp.where(allowed, jnp.exp(scores), 0.0)
        total += jnp.sum(exp_scores, -1, keepdims=True)
        numer += product(exp_scores.astype(BF16), v_ref[rows, :])
    numer = jnp.where(lane_low, numer[:DEC], numer[DEC:])
    scale = 1.0 / jnp.where(lane_low, total[:DEC], total[DEC:])
    exact = numer * scale
    mixed_ref[...] = exact.astype(BF16)
    exact_ref[...] = exact
    scale_ref[...] = scale


def attend_backward_kernel(
    causal, chunk, lens_ref, bases_ref, q_ref, k_ref, v_ref, grad_ref, exact_ref, scale_ref, gq_ref, gk_ref, gv_ref
):
    which = pl.program_id(0)
    lane_low = low_lanes(DEC)
    q2 = stack_pair(q_ref[...], lane_low)
    grad_numer = grad_ref[...] * scale_ref[...]
    gn2 = stack_pair(grad_numer.astype(BF16), lane_low)
    weighted = jnp.transpose(grad_numer * exact_ref[...])
    grad_total = -jnp.concatenate(
        [
            jnp.sum(weighted[:HEAD_DIM], 0, keepdims=True),
            jnp.sum(weighted[HEAD_DIM:], 0, keepdims=True),
        ],
        1,
    )
    gq2 = jnp.zeros((2 * DEC, PAIR), F32)
    for step in range(k_ref.shape[0] // chunk):
        rows = pl.ds(step * chunk, chunk)
        keys = k_ref[rows, :]
        scores = right_product(keys, q2)
        allowed = allowed_slots(causal, chunk, lens_ref, bases_ref, which, step, 0)
        exp_scores = jnp.where(allowed, jnp.exp(scores), 0.0)
        grad_exp = right_product(v_ref[rows, :], gn2) + grad_total
        grad_scores = (exp_scores * grad_exp).astype(BF16)
        gk_ref[rows, :] = product(grad_scores, q2).astype(BF16)
        gv_ref[rows, :] = product(exp_scores.astype(BF16), gn2).astype(BF16)
        gq2 += left_product(grad_scores, keys)
    gq_ref[...] = jnp.where(lane_low, gq2[:DEC], gq2[DEC:]).astype(BF16)


def attention_call(kernel, causal, chunk, lens, bases, queries, keys, values, more, outs):
    item_count = lens.shape[0]
    slots = keys.shape[0] // item_count
    q_spec = pl.BlockSpec((DEC, PAIR), lambda a, p, *_: (a, p))
    k_spec = pl.BlockSpec((slots, PAIR), lambda a, p, *_: (a, p))
    spec = {"q": q_spec, "k": k_spec}
    rows = {"q": queries.shape[0], "k": keys.shape[0]}
    return pl.pallas_call(
        functools.partial(kernel, causal, chunk),
        grid_spec=pltpu.PrefetchScalarGridSpec(
            num_scalar_prefetch=2,
            grid=(item_count, PAIRS),
            in_specs=[q_spec, k_spec, k_spec] + [q_spec] * len(more),
            out_specs=[spec[kind] for kind, _ in outs],
        ),
        out_shape=[jax.ShapeDtypeStruct((rows[kind], D), dtype) for kind, dtype in outs],
        cost_estimate=pl.CostEstimate(
            flops=4 * item_count * HEADS * DEC * slots * 256, bytes_accessed=16 * D * slots, transcendentals=0
        ),
        name="self_attention" if causal else "cross_attention",
    )(lens, bases, queries, keys, values, *more)


def attend_forward(causal, chunk, lens, bases, queries, keys, values):
    return attention_call(
        attend_forward_kernel, causal, chunk, lens, bases, queries, keys, values, (),
        (("q", BF16), ("q", F32), ("q", F32)),
    )


def attend_backward(causal, chunk, lens, bases, queries, keys, values, grad_mixed, exact, scale):
    return attention_call(
        attend_backward_kernel, causal, chunk, lens, bases, queries, keys, values, (grad_mixed, exact, scale),
        (("q", BF16), ("k", BF16), ("k", BF16)),
    )


def halving_order(items_count, flipped):
    bits = [1 << b for b in range(1, items_count.bit_length() - 1)]
    return [1] + (bits if flipped else bits[::-1])


def block_order(items_count, flipped):
    bits = halving_order(items_count, flipped)
    order = []
    for spot in range(items_count):
        distance = 0
        for place, bit in enumerate(bits):
            if spot >> (len(bits) - 1 - place) & 1:
                distance |= bit
        order.append(distance)
    return order


def order_columns(values, row, items_count, flipped):
    width = values.shape[1] // items_count
    return jnp.concatenate(
        [
            lax.dynamic_slice_in_dim(values, (row ^ distance) * width, width, 1)
            for distance in block_order(items_count, flipped)
        ],
        1,
    )


def reduce_rows(partial, items_count, flipped):
    for bit in halving_order(items_count, flipped):
        half = partial.shape[0] // 2
        arrived = lax.ppermute(partial[half:], "items", [(a, a ^ bit) for a in range(items_count)])
        partial = (partial[:half].astype(F32) + arrived.astype(F32)).astype(BF16)
    return partial


def reduce_columns(partial, member, members):
    bit = members // 2
    while bit:
        half = partial.shape[1] // 2
        high = (member & bit) != 0
        left, right = partial[:, :half], partial[:, half:]
        arrived = lax.ppermute(
            jnp.where(high, left, right), "mem", [(a, a ^ bit) for a in range(members)]
        )
        partial = jnp.where(high, right, left).astype(F32) + arrived.astype(F32)
        if bit > 1:
            partial = partial.astype(BF16)
        bit //= 2
    return partial


def weight_gradients(left_ordered, grads, items_count, member, members, flipped):
    width = grads[0].shape[1]
    joined = grads[0] if len(grads) == 1 else jnp.concatenate(grads, 1)
    partial = left_product(left_ordered, joined).astype(BF16)
    partial = reduce_rows(partial, items_count, flipped)
    return [
        reduce_columns(partial[:, k * width : (k + 1) * width], member, members) for k in range(len(grads))
    ]


def body(
    items_count,
    members,
    tokens,
    memory,
    cotangent,
    mem_len,
    dec_len,
    self_query,
    self_key,
    self_value,
    self_out,
    cross_query,
    cross_key,
    cross_value,
    cross_out,
    feed_in,
    feed_out,
    shifts,
    gains,
    inner_bias,
):
    row = lax.axis_index("items")
    member = lax.axis_index("mem")
    rows_here = tokens.shape[0]
    item_count = rows_here // DEC
    group_items = memory.shape[0]
    mem_local = memory.shape[1]
    shards = (
        self_query, self_key, self_value, self_out, cross_query, cross_key, cross_value, cross_out, feed_in, feed_out,
    )
    gather = gather_by_kernel if (items_count, members) == (8, 4) else gather_by_collectives
    whole, item_memory = gather(shards, memory, items_count, members)
    (
        query_self, key_self, value_self, output_self, query_cross, key_cross, value_cross, output_cross,
        feed_up, feed_down,
    ) = whole
    memory_flat = item_memory.reshape(-1, D)
    shift_rows = lax.all_gather(shifts, "items", axis=1, tiled=True).astype(F32)
    gain_rows = lax.all_gather(gains, "items", axis=1, tiled=True).astype(F32)
    inner_shift = lax.all_gather(inner_bias, "items", axis=0, tiled=True).astype(F32)

    own_dec = lax.dynamic_slice_in_dim(dec_len, member * item_count, item_count)
    own_mem = lax.dynamic_slice_in_dim(mem_len, member * item_count, item_count)
    bases = lax.rem(member - jnp.arange(members, dtype=jnp.int32) + members, members) * mem_local

    tokens_float = tokens.astype(F32)
    queries_one = ((product(tokens, query_self) + shift_rows[0]) * 0.125).astype(BF16)
    keys_one = product(tokens, key_self).astype(BF16)
    values_one = (product(tokens, value_self) + shift_rows[1]).astype(BF16)
    mixed_one, exact_one, scale_one = attend_forward(
        True, DEC, own_dec, bases, queries_one, keys_one, values_one
    )
    resid_one = tokens_float + product(mixed_one, output_self) + shift_rows[2]
    hidden_one, normed_one, inverse_one = norm_forward(resid_one, gain_rows[0], shift_rows[7])
    hidden_one_low = hidden_one.astype(BF16)
    queries_two = ((product(hidden_one_low, query_cross) + shift_rows[3]) * 0.125).astype(BF16)
    keys_two = product(memory_flat, key_cross).astype(BF16)
    values_two = (product(memory_flat, value_cross) + shift_rows[4]).astype(BF16)
    mixed_two, exact_two, scale_two = attend_forward(
        False, mem_local, own_mem, bases, queries_two, keys_two, values_two
    )
    resid_two = hidden_one + product(mixed_two, output_cross) + shift_rows[5]
    hidden_two, normed_two, inverse_two = norm_forward(resid_two, gain_rows[1], shift_rows[8])
    hidden_two_low = hidden_two.astype(BF16)
    inner_pre = product(hidden_two_low, feed_up) + inner_shift
    cdf_part = 0.5 * (1.0 + jax.scipy.special.erf(inner_pre * half_root))
    active_low = (inner_pre * cdf_part).astype(BF16)
    resid_three = hidden_two + product(active_low, feed_down) + shift_rows[6]
    layer_out, normed_three, inverse_three = norm_forward(resid_three, gain_rows[2], shift_rows[9])

    grad_three, gain_grad_three, shift_grad_three = norm_backward(
        cotangent.astype(F32), normed_three, inverse_three, gain_rows[2]
    )
    grad_down = grad_three.astype(BF16)

    def summed(values, grads, flipped):
        ordered = order_columns(values, row, items_count, flipped)
        return weight_gradients(ordered, grads, items_count, member, members, flipped)

    (feed_down_grad,) = summed(active_low, [grad_down], False)
    out_bias_grad = column_sums(grad_down)
    grad_active = right_product(grad_down, feed_down)
    slope = cdf_part + inner_pre * jnp.exp(-0.5 * inner_pre * inner_pre) * normal_peak
    grad_inner = (grad_active * slope).astype(BF16)
    (feed_up_grad,) = summed(hidden_two_low, [grad_inner], True)
    inner_bias_grad = column_sums(grad_inner)
    grad_hidden_two = grad_three + right_product(grad_inner, feed_up)
    grad_two, gain_grad_two, shift_grad_two = norm_backward(
        grad_hidden_two, normed_two, inverse_two, gain_rows[1]
    )
    grad_cross_branch = grad_two.astype(BF16)
    (output_cross_grad,) = summed(mixed_two, [grad_cross_branch], False)
    cross_out_bias_grad = column_sums(grad_cross_branch)
    grad_mixed_two = right_product(grad_cross_branch, output_cross)
    query_grad_two, key_grad_two, value_grad_two = attend_backward(
        False, mem_local, own_mem, bases, queries_two, keys_two, values_two, grad_mixed_two, exact_two, scale_two
    )
    query_grad_two = query_grad_two * jnp.asarray(0.125, BF16)

    memory_part = (
        right_product(key_grad_two, key_cross) + right_product(value_grad_two, value_cross)
    ).astype(BF16).reshape(item_count, members, mem_local, D)
    memory_grad = jnp.zeros((group_items, mem_local, D), F32)
    for step in range(members):
        part = memory_part[:, step]
        if step:
            part = lax.ppermute(part, "mem", [(a, (a - step) % members) for a in range(members)])
        owner = lax.rem(member + step, members)
        memory_grad = lax.dynamic_update_slice_in_dim(memory_grad, part.astype(F32), owner * item_count, 0)

    key_cross_grad, value_cross_grad = summed(memory_flat, [key_grad_two, value_grad_two], True)
    cross_value_bias_grad = column_sums(value_grad_two)
    (query_cross_grad,) = summed(hidden_one_low, [query_grad_two], False)
    cross_query_bias_grad = column_sums(query_grad_two)
    grad_hidden_one = grad_two + right_product(query_grad_two, query_cross)
    grad_one, gain_grad_one, shift_grad_one = norm_backward(
        grad_hidden_one, normed_one, inverse_one, gain_rows[0]
    )
    grad_self_branch = grad_one.astype(BF16)
    (output_self_grad,) = summed(mixed_one, [grad_self_branch], True)
    self_out_bias_grad = column_sums(grad_self_branch)
    grad_mixed_one = right_product(grad_self_branch, output_self)
    query_grad_one, key_grad_one, value_grad_one = attend_backward(
        True, DEC, own_dec, bases, queries_one, keys_one, values_one, grad_mixed_one, exact_one, scale_one
    )
    query_grad_one = query_grad_one * jnp.asarray(0.125, BF16)
    query_self_grad, key_self_grad, value_self_grad = summed(
        tokens, [query_grad_one, key_grad_one, value_grad_one], False
    )
    tokens_grad = (
        grad_one
        + right_product(query_grad_one, query_self)
        + right_product(key_grad_one, key_self)
        + right_product(value_grad_one, value_self)
    )
    vectors = jnp.concatenate(
        [
            column_sums(query_grad_one),
            column_sums(value_grad_one),
            self_out_bias_grad,
            cross_query_bias_grad,
            cross_value_bias_grad,
            cross_out_bias_grad,
            out_bias_grad,
            shift_grad_one,
            shift_grad_two,
            shift_grad_three,
            gain_grad_one,
            gain_grad_two,
            gain_grad_three,
            inner_bias_grad,
        ]
    )
    vectors = lax.psum(vectors.reshape(-1, 128), ("items", "mem")).reshape(-1)
    shift_count = shifts.shape[0] * D
    gain_count = gains.shape[0] * D
    shift_width, gain_width, bias_width = shifts.shape[1], gains.shape[1], inner_bias.shape[0]
    shifts_grad = lax.dynamic_slice_in_dim(
        vectors[:shift_count].reshape(-1, D), row * shift_width, shift_width, 1
    )
    gains_grad = lax.dynamic_slice_in_dim(
        vectors[shift_count : shift_count + gain_count].reshape(-1, D), row * gain_width, gain_width, 1
    )
    bias_grad = lax.dynamic_slice_in_dim(vectors[shift_count + gain_count :], row * bias_width, bias_width)
    return (
        layer_out,
        tokens_grad,
        memory_grad,
        query_self_grad,
        key_self_grad,
        value_self_grad,
        output_self_grad,
        query_cross_grad,
        key_cross_grad,
        value_cross_grad,
        output_cross_grad,
        feed_up_grad,
        feed_down_grad,
        shifts_grad,
        gains_grad,
        bias_grad,
    )


def solution(mesh):
    tiles = P("items", "mem")
    rows = P(("items", "mem"), None)
    blocks = P("items", "mem", None)
    return jax.shard_map(
        functools.partial(body, mesh.shape["items"], mesh.shape["mem"]),
        mesh=mesh,
        in_specs=(rows, blocks, rows, P("items"), P("items"))
        + (tiles,) * 10
        + (P(None, "items"), P(None, "items"), P("items")),
        out_specs=(rows, rows, blocks) + (tiles,) * 10 + (P(None, "items"), P(None, "items"), P("items")),
        check_vma=False,
    )
```

time: 1660 us -> 821 us (0.49)
  waiting for transfers between devices: 1020 us -> 249 us
  Pallas kernels: 0 us -> 249 us
  blocking collectives: 191 us -> 28 us
  local copies, waits for them, and re-layouts: 200 us -> 71.7 us
  matrix products: 193 us -> 100 us
  starting transfers between devices: 3.44 us -> 46.2 us
  other arithmetic: 25.6 us -> 51.7 us
    reduce_scatter x16 -> x0, waiting for transfers between devices: 404 us -> none  [the longest x1 74.7 us: body(): lax.psum_scatter(feed_down_grad.astype(jnp.bfloat16), 'items', scatter_di...]
    unnamed x45 -> x1, waiting for transfers between devices: 256 us -> 0.02 us
    pallas_call x0 -> x5, Pallas kernels: none -> 249 us  [the longest x1 183 us: gather_by_kernel(): pl.pallas_call(functools.partial(gather_kernel, members, items_here, tupl...]
    ppermute x0 -> x44, waiting for transfers between devices: none -> 234 us  [the longest x21 120 us: reduce_rows(): lax.ppermute(partial[half:], 'items', [(a, a ^ bit) for a in range(items_...]
    all_gather x14 -> x0, waiting for transfers between devices: 212 us -> none  [the longest x1 52.6 us: body(): lax.all_gather(cols_whole[8], 'items', axis=0, tiled=True)]
    all_gather x12 -> x3, blocking collectives: 166 us -> 28 us  [the longest x1 10.5 us: body(): shift_rows = lax.all_gather(shifts, 'items', axis=1, tiled=True).astype(F32)]
    psum x1, waiting for transfers between devices: 150 us -> 15.1 us  [body(): vectors = lax.psum(vectors.reshape(-1, 128), ('items', 'mem')).reshape(-1)]
    dot_general x30 -> x10, matrix products: 96.3 us -> 35.5 us  [product(): return jnp.dot(first_op, second_op, preferred_element_type=F32)]
  transfers between devices with their start and end apart: 38 -> 45, of which waited for: 31 -> 29; matrix products, arithmetic and copies ran while one was open for 20% -> 19% of each run, Pallas kernels for 0% -> 0%
where the time goes in v1:
time: 821 us; the launch traced here: 812 us
  Pallas kernels  249 us (30%)
  waiting for transfers between devices  249 us (30%)
  matrix products  100 us (12%)
  local copies, waits for them, and re-layouts  71.7 us (9%)
  other arithmetic  51.7 us (6%)
  starting transfers between devices  46.2 us (6%)
  blocking collectives  28 us (3%)
  between operations  15.9 us (2%)
    pallas_call x1, Pallas kernels, gather_by_kernel(): pl.pallas_call(functools.partial(gather_kernel, members, items_here, tupl...  183 us
    ppermute x21, waiting for transfers between devices, reduce_rows(): lax.ppermute(partial[half:], 'items', [(a, a ^ bit) for a in range(items_...  120 us
    pallas_call x4, Pallas kernels, attention_call(): pl.pallas_call(functools.partial(kernel, causal, chunk), grid_spec=pltpu....  66.2 us
    ppermute x3, waiting for transfers between devices, body(): lax.ppermute(part, 'mem', [(a, (a - step) % members) for a in range(membe...  57.6 us
    ppermute x20, waiting for transfers between devices, reduce_columns(): lax.ppermute(jnp.where(high, left, right), 'mem', [(a, a ^ bit) for a in...  56.5 us
    unnamed x201, local copies, waits for them, and re-layouts  37.5 us
    dot_general x10, matrix products, product(): return jnp.dot(first_op, second_op, preferred_element_type=F32)  35.5 us
    dot_general x10, matrix products, right_product(): lax.dot_general(first_op, second_op, (((1,), (1,)), ((), ())), preferred_...  34.7 us
  transfers between devices with their start and end apart: 45, of which 29 were waited for; matrix products, arithmetic and copies ran while one was open for 19% of the time, Pallas kernels for 0%

profile of v1, /device:TPU:0, one launch (start us, length us, event | category | flops | bytes accessed | tf_op | source)
XLA Modules:
  0.0 811.9 jit_solution(3740312505876542194)
XLA Ops:
  7.8 10.5 %all_gather.9 = bf16[10,1024]{1,0:T(8,128)(2,1)S(1)} all-gather(bf16[10,128]{1,0:T(8,128)(2,1)} %param.33), channel_id=1, replica_groups=mesh['items'=8,'mem'=4] {'items'}, dimensions={1}, use_global_device_ids=true | all-gather | bytes 23040 | tf_op jit(solution)/shard_map/all_gather | solution.py:497
  19.5 182.9 %gather_all.1 = (bf16[1024,1024]{1,0:T(8,128)(2,1)}, bf16[1024,1024]{1,0:T(8,128)(2,1)}, bf16[1024,1024]{1,0:T(8,128)(2,1)}, bf16[1024,1024]{1,0:T(8,128)(2,1)},...) custom-call(bf16[128,256]{1,0:T(8,128)(2,1)} %refs_0_.1, ...), custom_call_target="tpu_custom_call" | custom-call | tf_op jit(solution)/shard_map/gather_all/pallas_call | solution.py:254
  205.6 3.3 fusion.28.v_ref
  210.4 11.5 %self_attention.2 = (bf16[256,1024]{1,0:T(8,128)(2,1)}, f32[256,1024]{1,0:T(8,128)}, f32[256,1024]{1,0:T(8,128)}) custom-call(s32[2]{0:T(128)} %dynamic_slice.183.lens_ref, s32[4]{0:T(128)} %fusion.42.bases_ref, bf16[256,1024]{1,0:T(8,128)(2,1)} %fusion.30.q_ref, bf16[256,1024]{1,0:T(8,128)(2,1)} %fusion.29.k_ref, bf16[256,1024]{1,0:T(8,128)(2,1)} %fusion.28.v_ref), custom_call_target="tpu_custom_call" | custom-call | flops 536870912 | bytes 2097152 | tf_op jit(solution)/shard_map/self_attention/pallas_call | solution.py:367
  224.4 8.6 %all_gather.10 = bf16[3,1024]{1,0:T(4,128)(2,1)S(1)} all-gather(bf16[3,128]{1,0:T(4,128)(2,1)S(1)} %copy-done.51), channel_id=1, replica_groups=mesh['items'=8,'mem'=4] {'items'}, dimensions={1}, use_global_device_ids=true | all-gather | bytes 6912 | tf_op jit(solution)/shard_map/all_gather | solution.py:498
  233.6 7.8 convolution_convert_fusion.3.k_ref
  241.3 6.1 add_convert_fusion.3.v_ref
  250.1 16.6 %cross_attention.2 = (bf16[256,1024]{1,0:T(8,128)(2,1)}, f32[256,1024]{1,0:T(8,128)}, f32[256,1024]{1,0:T(8,128)}) custom-call(s32[2]{0:T(128)} %dynamic_slice.184.lens_ref, s32[4]{0:T(128)} %fusion.42.bases_ref, bf16[256,1024]{1,0:T(8,128)(2,1)} %fusion.25.q_ref, bf16[2048,1024]{1,0:T(8,128)(2,1)} %convolution_convert_fusion.3.k_ref, ...), custom_call_target="tpu_custom_call" | custom-call | flops 4294967296 | bytes 16777216 | tf_op jit(solution)/shard_map/cross_attention/pallas_call | solution.py:367
  268.8 8.9 %all-gather = bf16[8,1,512]{2,1,0:T(2,128)(2,1)S(1)} all-gather(bf16[1,1,512]{2,1,0:T(2,128)(2,1)S(1)} %reshape.122), channel_id=1, replica_groups=mesh['items'=8,'mem'=4] {'items'}, dimensions={0}, use_global_device_ids=true | all-gather | bytes 9216 | tf_op jit(solution)/shard_map/all_gather | solution.py:499
  278.1 5.5 multiply_convert_fusion
  288.7 4.2 convert_reduce_fusion.1
  297.7 25.0 %cross_attention.3 = (bf16[256,1024]{1,0:T(8,128)(2,1)}, bf16[2048,1024]{1,0:T(8,128)(2,1)}, bf16[2048,1024]{1,0:T(8,128)(2,1)}) custom-call(s32[2]{0:T(128)} %dynamic_slice.184.lens_ref, s32[4]{0:T(128)} %fusion.42.bases_ref, bf16[256,1024]{1,0:T(8,128)(2,1)} %fusion.25.q_ref, bf16[2048,1024]{1,0:T(8,128)(2,1)} %convolution_convert_fusion.3.k_ref, ...), custom_call_target="tpu_custom_call" | custom-call | flops 4294967296 | bytes 16777216 | tf_op jit(solution)/shard_map/cross_attention/pallas_call | solution.py:367
  328.1 13.1 %self_attention.3 = (bf16[256,1024]{1,0:T(8,128)(2,1)}, bf16[256,1024]{1,0:T(8,128)(2,1)}, bf16[256,1024]{1,0:T(8,128)(2,1)}) custom-call(s32[2]{0:T(128)} %dynamic_slice.183.lens_ref, s32[4]{0:T(128)} %fusion.42.bases_ref, bf16[256,1024]{1,0:T(8,128)(2,1)} %fusion.30.q_ref, bf16[256,1024]{1,0:T(8,128)(2,1)} %fusion.29.k_ref, ...), custom_call_target="tpu_custom_call" | custom-call | flops 536870912 | bytes 2097152 | tf_op jit(solution)/shard_map/self_attention/pallas_call | solution.py:367
  360.7 4.0 convolution_convert_fusion
  393.2 7.5 fusion.61
  400.7 7.2 add_convert_fusion.2
  418.5 6.6 convolution_convert_fusion.1
  427.6 11.5 %fusion.9 = bf16[1024,2048]{1,0:T(8,128)(2,1)} fusion(bf16[2048,1024]{1,0:T(8,128)(2,1)S(1)} %dynamic-slice_dynamic-update-slice_fusion, bf16[2048,1024]{1,0:T(8,128)(2,1)S(1)} %copy-done.12, bf16[2048,1024]{1,0:T(8,128)(2,1)S(1)} %copy-done.59), kind=kOutput, calls=%fused_computation.27 | convolution fusion | flops 8608808960 | bytes 16777216 | tf_op jit(solution)/shard_map/dot_general | solution.py:29
  440.2 4.5 convolution_convert_fusion.2
  444.7 3.3 convolution_add_fusion.3
  448.0 4.5 broadcast_in_dim.2
  455.3 4.8 slice.512
  461.5 4.0 slice.450
  465.5 15.1 %all-reduce.2.cloned.1.call-done = f32[136,128]{1,0:T(8,128)} async-done(((f32[136,128]{1,0:T(8,128)}), f32[136,128]{1,0:T(8,128)}) %all-reduce.2.cloned.1.call-update) | async-done | bytes 69648 | tf_op jit(solution)/shard_map/psum | solution.py:613
  498.8 57.6 %collective-permute-done.1 = bf16[2,256,1024]{2,1,0:T(8,128)(2,1)S(1)} collective-permute-done((bf16[2,256,1024]{2,1,0:T(8,128)(2,1)}, bf16[2,256,1024]{2,1,0:T(8,128)(2,1)S(1)}, u32[]{:S(2)}, u32[]{:S(2)}) %collective-permute-start.1) | collective-permute-done | bytes 1048608 | tf_op jit(solution)/shard_map/ppermute | solution.py:566
  561.5 9.6 %collective-permute-done.30 = bf16[256,1024]{1,0:T(8,128)(2,1)S(1)} collective-permute-done((bf16[256,1024]{1,0:T(8,128)(2,1)S(1)}, bf16[256,1024]{1,0:T(8,128)(2,1)S(1)}, u32[]{:S(2)}, u32[]{:S(2)}) %collective-permute-start.30) | collective-permute-done | bytes 524320 | tf_op jit(solution)/shard_map/ppermute | solution.py:428
  572.8 8.7 %collective-permute-done.18 = bf16[256,1024]{1,0:T(8,128)(2,1)S(1)} collective-permute-done((bf16[256,1024]{1,0:T(8,128)(2,1)S(1)}, bf16[256,1024]{1,0:T(8,128)(2,1)S(1)}, u32[]{:S(2)}, u32[]{:S(2)}) %collective-permute-start.18) | collective-permute-done | bytes 524320 | tf_op jit(solution)/shard_map/ppermute | solution.py:428
  585.1 5.7 collective-permute-done.31
  590.8 3.8 collective-permute-done.19
  596.2 5.0 collective-permute-done.14
  601.3 5.8 collective-permute-done.32
  607.2 5.8 collective-permute-done.20
  615.5 3.4 collective-permute-done.15
  619.0 4.6 collective-permute-done.33
  624.5 3.4 collective-permute-done.21
  628.8 7.5 collective-permute-done.23
  640.3 11.4 %collective-permute-done.24 = bf16[128,2048]{1,0:T(8,128)(2,1)S(1)} collective-permute-done((bf16[128,2048]{1,0:T(8,128)(2,1)S(1)}, bf16[128,2048]{1,0:T(8,128)(2,1)S(1)}, u32[]{:S(2)}, u32[]{:S(2)}) %collective-permute-start.24) | collective-permute-done | bytes 524320 | tf_op jit(solution)/shard_map/ppermute | solution.py:428
  664.0 4.3 add_convert_fusion
  670.8 14.8 %collective-permute-done.4 = bf16[256,3072]{1,0:T(8,128)(2,1)} collective-permute-done((bf16[256,3072]{1,0:T(8,128)(2,1)S(1)}, bf16[256,3072]{1,0:T(8,128)(2,1)}, u32[]{:S(2)}, u32[]{:S(2)}) %collective-permute-start.4) | collective-permute-done | bytes 1572896 | tf_op jit(solution)/shard_map/ppermute | solution.py:428
  689.1 3.7 add_convert_fusion.1
  695.5 12.6 %collective-permute-done.5 = bf16[128,3072]{1,0:T(8,128)(2,1)S(1)} collective-permute-done((bf16[128,3072]{1,0:T(8,128)(2,1)S(1)}, bf16[128,3072]{1,0:T(8,128)(2,1)S(1)}, u32[]{:S(2)}, u32[]{:S(2)}) %collective-permute-start.5) | collective-permute-done | bytes 786464 | tf_op jit(solution)/shard_map/ppermute | solution.py:428
  718.6 7.0 collective-permute-done.40
  728.1 25.0 %collective-permute-done.35 = bf16[256,4096]{1,0:T(8,128)(2,1)S(1)} collective-permute-done((bf16[256,4096]{1,0:T(8,128)(2,1)S(1)}, bf16[256,4096]{1,0:T(8,128)(2,1)S(1)}, u32[]{:S(2)}, u32[]{:S(2)}) %collective-permute-start.35) | collective-permute-done | bytes 2097184 | tf_op jit(solution)/shard_map/ppermute | solution.py:428
  757.4 7.8 collective-permute-done.41
  772.6 12.0 %collective-permute-done.42 = bf16[512,512]{1,0:T(8,128)(2,1)S(1)} collective-permute-done((bf16[512,512]{1,0:T(8,128)(2,1)S(1)}, bf16[512,512]{1,0:T(8,128)(2,1)S(1)}, u32[]{:S(2)}, u32[]{:S(2)}) %collective-permute-start.42) | collective-permute-done | bytes 524320 | tf_op jit(solution)/shard_map/ppermute | solution.py:439
  787.8 5.0 collective-permute-done.37
  794.2 4.2 collective-permute-done.43
  799.3 4.6 collective-permute-done.38
  (413 shorter events, 185.8 us)
Async XLA Ops:
  7.2 195.2 %copy-start.44 = (bf16[256,1024]{1,0:T(8,128)(2,1)S(1)}, bf16[256,1024]{1,0:T(8,128)(2,1)}, u32[]{:S(2)}) copy-start(bf16[256,1024]{1,0:T(8,128)(2,1)} %param.18) | copy-start | bytes 1572868
  7.2 473.5 %all-reduce.2.cloned.1.call-start = ((), (), s32[]{:S(2)}) async-start(), calls=%async_computation | async-start | bytes 139264 | tf_op jit(solution)/shard_map/psum | solution.py:613
  369.3 294.7 %collective-permute-start.39 = (bf16[2048,1024]{1,0:T(8,128)(2,1)}, bf16[2048,1024]{1,0:T(8,128)(2,1)}, u32[]{:S(2)}, u32[]{:S(2)}) collective-permute-start(bf16[2048,1024]{1,0:T(8,128)(2,1)} %slice.522), channel_id=1, source_target_pairs={{0,4},{4,0},{8,12},{12,8},{16,20},{20,16},{24,28},{28,24},{1,5},{5... | collective-permute-start | bytes 12582920 | tf_op jit(solution)/shard_map/ppermute | solution.py:428
  384.4 100.3 %collective-permute-start.29 = (bf16[512,1024]{1,0:T(8,128)(2,1)}, bf16[512,1024]{1,0:T(8,128)(2,1)}, u32[]{:S(2)}, u32[]{:S(2)}) collective-permute-start(bf16[512,1024]{1,0:T(8,128)(2,1)} %slice.502), channel_id=1, source_target_pairs={{0,4},{4,0},{8,12},{12,8},{16,20},{20,16},{24,28},{28,24},{1,5},{5... | collective-permute-start | bytes 3145736 | tf_op jit(solution)/shard_map/ppermute | solution.py:428
  386.7 102.8 %collective-permute-start.17 = (bf16[512,1024]{1,0:T(8,128)(2,1)}, bf16[512,1024]{1,0:T(8,128)(2,1)S(1)}, u32[]{:S(2)}, u32[]{:S(2)}) collective-permute-start(bf16[512,1024]{1,0:T(8,128)(2,1)} %slice.478), channel_id=1, source_target_pairs={{0,4},{4,0},{8,12},{12,8},{16,20},{20,16},{24,28},{28,24},{1,5},{5... | collective-permute-start | bytes 3145736 | tf_op jit(solution)/shard_map/ppermute | solution.py:428
  392.9 100.7 %collective-permute-start.12 = (bf16[512,1024]{1,0:T(8,128)(2,1)}, bf16[512,1024]{1,0:T(8,128)(2,1)}, u32[]{:S(2)}, u32[]{:S(2)}) collective-permute-start(bf16[512,1024]{1,0:T(8,128)(2,1)} %slice.468), channel_id=1, source_target_pairs={{0,4},{4,0},{8,12},{12,8},{16,20},{20,16},{24,28},{28,24},{1,5},{5... | collective-permute-start | bytes 3145736 | tf_op jit(solution)/shard_map/ppermute | solution.py:428
  411.6 83.8 %collective-permute-start = (bf16[2,256,1024]{2,1,0:T(8,128)(2,1)}, bf16[2,256,1024]{2,1,0:T(8,128)(2,1)}, u32[]{:S(2)}, u32[]{:S(2)}) collective-permute-start(bf16[2,256,1024]{2,1,0:T(8,128)(2,1)} %get-tuple-element.82), channel_id=1, source_target_pairs={{0,3},{1,0},{2,1},{3,2},{4,7},{5,4},{6,5},{7,6},{8,11},{9,8},{10,9... | collective-permute-start | bytes 3145736 | tf_op jit(solution)/shard_map/ppermute | solution.py:566
  484.7 71.6 %collective-permute-start.1 = (bf16[2,256,1024]{2,1,0:T(8,128)(2,1)}, bf16[2,256,1024]{2,1,0:T(8,128)(2,1)S(1)}, u32[]{:S(2)}, u32[]{:S(2)}) collective-permute-start(bf16[2,256,1024]{2,1,0:T(8,128)(2,1)} %get-tuple-element.81), channel_id=1, source_target_pairs={{0,2},{1,3},{2,0},{3,1},{4,6},{5,7},{6,4},{7,5},{8,10},{9,11},{10,... | collective-permute-start | bytes 3145736 | tf_op jit(solution)/shard_map/ppermute | solution.py:566
  489.5 69.9 %collective-permute-start.2 = (bf16[2,256,1024]{2,1,0:T(8,128)(2,1)}, bf16[2,256,1024]{2,1,0:T(8,128)(2,1)S(1)}, u32[]{:S(2)}, u32[]{:S(2)}) collective-permute-start(bf16[2,256,1024]{2,1,0:T(8,128)(2,1)} %get-tuple-element.80), channel_id=1, source_target_pairs={{0,1},{1,2},{2,3},{3,0},{4,5},{5,6},{6,7},{7,4},{8,9},{9,10},{10,1... | collective-permute-start | bytes 3145736 | tf_op jit(solution)/shard_map/ppermute | solution.py:566
  493.6 195.4 %collective-permute-start.34 = (bf16[512,4096]{1,0:T(8,128)(2,1)}, bf16[512,4096]{1,0:T(8,128)(2,1)}, u32[]{:S(2)}, u32[]{:S(2)}) collective-permute-start(bf16[512,4096]{1,0:T(8,128)(2,1)} %slice.512), channel_id=1, source_target_pairs={{0,4},{4,0},{8,12},{12,8},{16,20},{20,16},{24,28},{28,24},{1,5},{5... | collective-permute-start | bytes 12582920 | tf_op jit(solution)/shard_map/ppermute | solution.py:428
  495.4 117.6 %collective-permute-start.22 = (bf16[512,2048]{1,0:T(8,128)(2,1)S(1)}, bf16[512,2048]{1,0:T(8,128)(2,1)S(1)}, u32[]{:S(2)}, u32[]{:S(2)}) collective-permute-start(bf16[512,2048]{1,0:T(8,128)(2,1)S(1)} %copy-done.28), channel_id=1, source_target_pairs={{0,4},{4,0},{8,12},{12,8},{16,20},{20,16},{24,28},{28,24},{1,5},{5... | collective-permute-start | bytes 6291464 | tf_op jit(solution)/shard_map/ppermute | solution.py:428
  556.3 14.8 %collective-permute-start.30 = (bf16[256,1024]{1,0:T(8,128)(2,1)S(1)}, bf16[256,1024]{1,0:T(8,128)(2,1)S(1)}, u32[]{:S(2)}, u32[]{:S(2)}) collective-permute-start(bf16[256,1024]{1,0:T(8,128)(2,1)S(1)} %slice.504), channel_id=1, source_target_pairs={{0,16},{4,20},{8,24},{12,28},{16,0},{20,4},{24,8},{28,12},{1,17},{... | collective-permute-start | bytes 1572872 | tf_op jit(solution)/shard_map/ppermute | solution.py:428
  559.4 31.4 %copy-start.18 = (bf16[512,3072]{1,0:T(8,128)(2,1)S(1)}, bf16[512,3072]{1,0:T(8,128)(2,1)}, u32[]{:S(2)}) copy-start(bf16[512,3072]{1,0:T(8,128)(2,1)} %slice.450) | copy-start | bytes 9437188
  559.4 22.2 %collective-permute-start.18 = (bf16[256,1024]{1,0:T(8,128)(2,1)S(1)}, bf16[256,1024]{1,0:T(8,128)(2,1)S(1)}, u32[]{:S(2)}, u32[]{:S(2)}) collective-permute-start(bf16[256,1024]{1,0:T(8,128)(2,1)S(1)} %slice.480), channel_id=1, source_target_pairs={{0,16},{4,20},{8,24},{12,28},{16,0},{20,4},{24,8},{28,12},{1,17},{... | collective-permute-start | bytes 1572872 | tf_op jit(solution)/shard_map/ppermute | solution.py:428
  571.1 12.3 %collective-permute-start.13 = (bf16[256,1024]{1,0:T(8,128)(2,1)S(1)}, bf16[256,1024]{1,0:T(8,128)(2,1)S(1)}, u32[]{:S(2)}, u32[]{:S(2)}) collective-permute-start(bf16[256,1024]{1,0:T(8,128)(2,1)S(1)} %slice.470), channel_id=1, source_target_pairs={{0,8},{4,12},{8,0},{12,4},{16,24},{20,28},{24,16},{28,20},{1,9},{5... | collective-permute-start | bytes 1572872 | tf_op jit(solution)/shard_map/ppermute | solution.py:428
  572.8 40.3 %copy-start.10 = (bf16[1024,2048]{1,0:T(8,128)(2,1)S(1)}, bf16[1024,2048]{1,0:T(8,128)(2,1)}, u32[]{:S(2)}) copy-start(bf16[1024,2048]{1,0:T(8,128)(2,1)} %fusion.9) | copy-start | bytes 12582916
  581.5 9.2 %collective-permute-start.31 = (bf16[128,1024]{1,0:T(8,128)(2,1)S(1)}, bf16[128,1024]{1,0:T(8,128)(2,1)S(1)}, u32[]{:S(2)}, u32[]{:S(2)}) collective-permute-start(bf16[128,1024]{1,0:T(8,128)(2,1)S(1)} %slice.506), channel_id=1, source_target_pairs={{0,8},{4,12},{8,0},{12,4},{16,24},{20,28},{24,16},{28,20},{1,9},{5... | collective-permute-start | bytes 786440 | tf_op jit(solution)/shard_map/ppermute | solution.py:428
  583.4 11.2 %collective-permute-start.19 = (bf16[128,1024]{1,0:T(8,128)(2,1)S(1)}, bf16[128,1024]{1,0:T(8,128)(2,1)S(1)}, u32[]{:S(2)}, u32[]{:S(2)}) collective-permute-start(bf16[128,1024]{1,0:T(8,128)(2,1)S(1)} %slice.482), channel_id=1, source_target_pairs={{0,8},{4,12},{8,0},{12,4},{16,24},{20,28},{24,16},{28,20},{1,9},{5... | collective-permute-start | bytes 786440 | tf_op jit(solution)/shard_map/ppermute | solution.py:428
  590.8 47.0 %collective-permute-start.3 = (bf16[512,3072]{1,0:T(8,128)(2,1)S(1)}, bf16[512,3072]{1,0:T(8,128)(2,1)S(1)}, u32[]{:S(2)}, u32[]{:S(2)}) collective-permute-start(bf16[512,3072]{1,0:T(8,128)(2,1)S(1)} %copy-done.18), channel_id=1, source_target_pairs={{0,4},{4,0},{8,12},{12,8},{16,20},{20,16},{24,28},{28,24},{1,5},{5... | collective-permute-start | bytes 9437192 | tf_op jit(solution)/shard_map/ppermute | solution.py:428
  594.6 6.6 collective-permute-start.14
  601.2 5.9 collective-permute-start.32
  607.1 5.9 collective-permute-start.20
  612.9 6.0 collective-permute-start.15
  614.0 22.4 %collective-permute-start.23 = (bf16[256,2048]{1,0:T(8,128)(2,1)S(1)}, bf16[256,2048]{1,0:T(8,128)(2,1)S(1)}, u32[]{:S(2)}, u32[]{:S(2)}) collective-permute-start(bf16[256,2048]{1,0:T(8,128)(2,1)S(1)} %slice.490), channel_id=1, source_target_pairs={{0,8},{4,12},{8,0},{12,4},{16,24},{20,28},{24,16},{28,20},{1,9},{5... | collective-permute-start | bytes 3145736 | tf_op jit(solution)/shard_map/ppermute | solution.py:428
  618.9 4.7 collective-permute-start.33
  623.6 4.3 collective-permute-start.21
  627.9 26.7 %collective-permute-start.16 = (bf16[128,256]{1,0:T(8,128)(2,1)S(1)}, bf16[128,256]{1,0:T(8,128)(2,1)S(1)}, u32[]{:S(2)}, u32[]{:S(2)}) collective-permute-start(bf16[128,256]{1,0:T(8,128)(2,1)S(1)} %broadcast_select_fusion.16), channel_id=1, source_target_pairs={{0,1},{1,0},{2,3},{3,2},{4,5},{5,4},{6,7},{7,6},{8,9},{9,8},{10,11... | collective-permute-start | bytes 196616 | tf_op jit(solution)/shard_map/ppermute | solution.py:439
  636.8 14.9 %collective-permute-start.24 = (bf16[128,2048]{1,0:T(8,128)(2,1)S(1)}, bf16[128,2048]{1,0:T(8,128)(2,1)S(1)}, u32[]{:S(2)}, u32[]{:S(2)}) collective-permute-start(bf16[128,2048]{1,0:T(8,128)(2,1)S(1)} %slice.492), channel_id=1, source_target_pairs={{0,16},{4,20},{8,24},{12,28},{16,0},{20,4},{24,8},{28,12},{1,17},{... | collective-permute-start | bytes 1572872 | tf_op jit(solution)/shard_map/ppermute | solution.py:428
  639.1 46.4 %collective-permute-start.4 = (bf16[256,3072]{1,0:T(8,128)(2,1)S(1)}, bf16[256,3072]{1,0:T(8,128)(2,1)}, u32[]{:S(2)}, u32[]{:S(2)}) collective-permute-start(bf16[256,3072]{1,0:T(8,128)(2,1)S(1)} %slice.452), channel_id=1, source_target_pairs={{0,16},{4,20},{8,24},{12,28},{16,0},{20,4},{24,8},{28,12},{1,17},{... | collective-permute-start | bytes 4718600 | tf_op jit(solution)/shard_map/ppermute | solution.py:428
  651.9 6.1 collective-permute-start.25
  654.6 5.9 collective-permute-start.27
  661.3 32.7 %collective-permute-start.28 = (bf16[128,256]{1,0:T(8,128)(2,1)}, bf16[128,256]{1,0:T(8,128)(2,1)}, u32[]{:S(2)}, u32[]{:S(2)}) collective-permute-start(bf16[128,256]{1,0:T(8,128)(2,1)} %broadcast_select_fusion.13), channel_id=1, source_target_pairs={{0,1},{1,0},{2,3},{3,2},{4,5},{5,4},{6,7},{7,6},{8,9},{9,8},{10,11... | collective-permute-start | bytes 196616 | tf_op jit(solution)/shard_map/ppermute | solution.py:439
  662.0 49.4 %collective-permute-start.26 = (bf16[128,256]{1,0:T(8,128)(2,1)}, bf16[128,256]{1,0:T(8,128)(2,1)}, u32[]{:S(2)}, u32[]{:S(2)}) collective-permute-start(bf16[128,256]{1,0:T(8,128)(2,1)} %broadcast_select_fusion.14), channel_id=1, source_target_pairs={{0,1},{1,0},{2,3},{3,2},{4,5},{5,4},{6,7},{7,6},{8,9},{9,8},{10,11... | collective-permute-start | bytes 196616 | tf_op jit(solution)/shard_map/ppermute | solution.py:439
  669.8 55.8 %collective-permute-start.40 = (bf16[1024,1024]{1,0:T(8,128)(2,1)}, bf16[1024,1024]{1,0:T(8,128)(2,1)S(1)}, u32[]{:S(2)}, u32[]{:S(2)}) collective-permute-start(bf16[1024,1024]{1,0:T(8,128)(2,1)} %slice.524), channel_id=1, source_target_pairs={{0,16},{4,20},{8,24},{12,28},{16,0},{20,4},{24,8},{28,12},{1,17},{... | collective-permute-start | bytes 6291464 | tf_op jit(solution)/shard_map/ppermute | solution.py:428
  687.6 20.5 %collective-permute-start.5 = (bf16[128,3072]{1,0:T(8,128)(2,1)S(1)}, bf16[128,3072]{1,0:T(8,128)(2,1)S(1)}, u32[]{:S(2)}, u32[]{:S(2)}) collective-permute-start(bf16[128,3072]{1,0:T(8,128)(2,1)S(1)} %slice.454), channel_id=1, source_target_pairs={{0,8},{4,12},{8,0},{12,4},{16,24},{20,28},{24,16},{28,20},{1,9},{5... | collective-permute-start | bytes 2359304 | tf_op jit(solution)/shard_map/ppermute | solution.py:428
  693.3 59.8 %collective-permute-start.35 = (bf16[256,4096]{1,0:T(8,128)(2,1)S(1)}, bf16[256,4096]{1,0:T(8,128)(2,1)S(1)}, u32[]{:S(2)}, u32[]{:S(2)}) collective-permute-start(bf16[256,4096]{1,0:T(8,128)(2,1)S(1)} %slice.514), channel_id=1, source_target_pairs={{0,8},{4,12},{8,0},{12,4},{16,24},{20,28},{24,16},{28,20},{1,9},{5... | collective-permute-start | bytes 6291464 | tf_op jit(solution)/shard_map/ppermute | solution.py:428
  708.4 7.2 collective-permute-start.10
  711.1 5.9 collective-permute-start.6
  711.4 7.0 collective-permute-start.8
  718.5 38.2 %collective-permute-start.11 = (bf16[128,256]{1,0:T(8,128)(2,1)S(1)}, bf16[128,256]{1,0:T(8,128)(2,1)S(1)}, u32[]{:S(2)}, u32[]{:S(2)}) collective-permute-start(bf16[128,256]{1,0:T(8,128)(2,1)S(1)} %broadcast_select_fusion.17), channel_id=1, source_target_pairs={{0,1},{1,0},{2,3},{3,2},{4,5},{5,4},{6,7},{7,6},{8,9},{9,8},{10,11... | collective-permute-start | bytes 196616 | tf_op jit(solution)/shard_map/ppermute | solution.py:439
  726.7 38.4 %collective-permute-start.41 = (bf16[512,1024]{1,0:T(8,128)(2,1)S(1)}, bf16[512,1024]{1,0:T(8,128)(2,1)S(1)}, u32[]{:S(2)}, u32[]{:S(2)}) collective-permute-start(bf16[512,1024]{1,0:T(8,128)(2,1)S(1)} %slice.526), channel_id=1, source_target_pairs={{0,8},{4,12},{8,0},{12,4},{16,24},{20,28},{24,16},{28,20},{1,9},{5... | collective-permute-start | bytes 3145736 | tf_op jit(solution)/shard_map/ppermute | solution.py:428
  754.0 14.9 %collective-permute-start.36 = (bf16[128,4096]{1,0:T(8,128)(2,1)S(1)}, bf16[128,4096]{1,0:T(8,128)(2,1)S(1)}, u32[]{:S(2)}, u32[]{:S(2)}) collective-permute-start(bf16[128,4096]{1,0:T(8,128)(2,1)S(1)} %slice.516), channel_id=1, source_target_pairs={{0,16},{4,20},{8,24},{12,28},{16,0},{20,4},{24,8},{28,12},{1,17},{... | collective-permute-start | bytes 3145736 | tf_op jit(solution)/shard_map/ppermute | solution.py:428
  754.5 17.3 %collective-permute-start.9 = (bf16[128,256]{1,0:T(8,128)(2,1)S(1)}, bf16[128,256]{1,0:T(8,128)(2,1)S(1)}, u32[]{:S(2)}, u32[]{:S(2)}) collective-permute-start(bf16[128,256]{1,0:T(8,128)(2,1)S(1)} %broadcast_select_fusion.18), channel_id=1, source_target_pairs={{0,1},{1,0},{2,3},{3,2},{4,5},{5,4},{6,7},{7,6},{8,9},{9,8},{10,11... | collective-permute-start | bytes 196616 | tf_op jit(solution)/shard_map/ppermute | solution.py:439
  754.6 38.9 %collective-permute-start.7 = (bf16[128,256]{1,0:T(8,128)(2,1)S(1)}, bf16[128,256]{1,0:T(8,128)(2,1)S(1)}, u32[]{:S(2)}, u32[]{:S(2)}) collective-permute-start(bf16[128,256]{1,0:T(8,128)(2,1)S(1)} %broadcast_select_fusion.19), channel_id=1, source_target_pairs={{0,1},{1,0},{2,3},{3,2},{4,5},{5,4},{6,7},{7,6},{8,9},{9,8},{10,11... | collective-permute-start | bytes 196616 | tf_op jit(solution)/shard_map/ppermute | solution.py:439
  765.6 18.9 %collective-permute-start.42 = (bf16[512,512]{1,0:T(8,128)(2,1)S(1)}, bf16[512,512]{1,0:T(8,128)(2,1)S(1)}, u32[]{:S(2)}, u32[]{:S(2)}) collective-permute-start(bf16[512,512]{1,0:T(8,128)(2,1)S(1)} %broadcast_select_fusion), channel_id=1, source_target_pairs={{0,2},{1,3},{2,0},{3,1},{4,6},{5,7},{6,4},{7,5},{8,10},{9,11},{10,... | collective-permute-start | bytes 1572872 | tf_op jit(solution)/shard_map/ppermute | solution.py:439
  769.2 23.6 %collective-permute-start.37 = (bf16[128,2048]{1,0:T(8,128)(2,1)S(1)}, bf16[128,2048]{1,0:T(8,128)(2,1)S(1)}, u32[]{:S(2)}, u32[]{:S(2)}) collective-permute-start(bf16[128,2048]{1,0:T(8,128)(2,1)S(1)} %broadcast_select_fusion.1), channel_id=1, source_target_pairs={{0,2},{1,3},{2,0},{3,1},{4,6},{5,7},{6,4},{7,5},{8,10},{9,11},{10,... | collective-permute-start | bytes 1572872 | tf_op jit(solution)/shard_map/ppermute | solution.py:439
  784.8 13.6 %collective-permute-start.43 = (bf16[512,256]{1,0:T(8,128)(2,1)S(1)}, bf16[512,256]{1,0:T(8,128)(2,1)S(1)}, u32[]{:S(2)}, u32[]{:S(2)}) collective-permute-start(bf16[512,256]{1,0:T(8,128)(2,1)S(1)} %broadcast_select_fusion.2), channel_id=1, source_target_pairs={{0,1},{1,0},{2,3},{3,2},{4,5},{5,4},{6,7},{7,6},{8,9},{9,8},{10,11... | collective-permute-start | bytes 786440 | tf_op jit(solution)/shard_map/ppermute | solution.py:439
  793.1 10.8 %collective-permute-start.38 = (bf16[128,1024]{1,0:T(8,128)(2,1)S(1)}, bf16[128,1024]{1,0:T(8,128)(2,1)S(1)}, u32[]{:S(2)}, u32[]{:S(2)}) collective-permute-start(bf16[128,1024]{1,0:T(8,128)(2,1)S(1)} %broadcast_select_fusion.3), channel_id=1, source_target_pairs={{0,1},{1,0},{2,3},{3,2},{4,5},{5,4},{6,7},{7,6},{8,9},{9,8},{10,11... | collective-permute-start | bytes 786440 | tf_op jit(solution)/shard_map/ppermute | solution.py:439
  (67 other events, 621.6 us)
Sparse Core Ops, SparseCore 0:
  347.4 133.1 all-reduce.1

commit v2 on v1

--- a/solution.py
+++ b/solution.py
@@ -18,7 +18,9 @@
 MESH = pl.DeviceIdType.MESH
 F32 = jnp.float32
 BF16 = jnp.bfloat16
+Z_LAG, X_LAG, FIRST_PIECE, SPREAD = 1, 1, 3, 17
 ANY = pl.BlockSpec(memory_space=pl.ANY)
+VMEM = pl.BlockSpec(memory_space=pltpu.VMEM)
 
 
 def product(first_op, second_op):
@@ -61,9 +63,9 @@
 def gather_kernel(members, items_here, units, *refs):
     count = len(units)
     weights = 1 + max(unit[0] for unit in units)
-    shard_refs, memory_ref = refs[:weights], refs[weights]
-    whole_refs, items_ref = refs[weights + 1 : 2 * weights + 1], refs[2 * weights + 1]
-    send_sem, recv_sem, copy_sem, mem_send, mem_recv, mem_copy = refs[2 * weights + 2 :]
+    shard_refs, memory_ref, vector_ref = refs[:weights], refs[weights], refs[weights + 1]
+    whole_refs, items_ref, vectors_ref = refs[weights + 2 : 2 * weights + 2], refs[2 * weights + 2], refs[2 * weights + 3]
+    send_sem, recv_sem, copy_sem, mem_send, mem_recv, mem_copy, vec_send, vec_recv, bounce = refs[2 * weights + 4 :]
     row = lax.axis_index("items")
     member = lax.axis_index("mem")
     hops = members - 1
@@ -72,7 +74,7 @@
     ALONG_X, ALONG_Y, HALF_A, HALF_B, CORE = 2 * hops, 2 * hops + 1, 2 * hops + 2, 2 * hops + 3, 2 * hops + 4
 
     barrier = pltpu.get_barrier_semaphore()
-    partners = [(core_peer, member), (first_peer, member), (second_peer, member)]
+    partners = [(row ^ distance, member) for distance in range(1, 8)]
     partners += [(row, lax.rem(member + step, members)) for step in range(1, members)]
     for partner in partners:
         pl.semaphore_signal(barrier, inc=1, device_id=partner, device_id_type=MESH)
@@ -182,33 +184,49 @@
             device_id_type=MESH,
         )
 
-    local = pltpu.make_async_copy(
-        memory_ref.at[pl.ds(member * items_here, items_here)], items_ref.at[:, 0], mem_copy
-    )
-    local.start()
-
-    depth_ticks = hops + 3
-    for tick in range(max(count + depth_ticks, pieces)):
+    fetch = pltpu.make_async_copy(memory_ref.at[pl.ds(member * items_here, items_here)], bounce, mem_copy.at[0])
+    local = pltpu.make_async_copy(bounce, items_ref.at[:, 0], mem_copy.at[1])
+    fetch.start()
+    spot = vectors_ref.at[:, pl.ds(pl.multiple_of(row * 128, 128), 128)]
+    vector_copies = [
+        pltpu.make_async_remote_copy(
+            src_ref=vector_ref,
+            dst_ref=spot,
+            send_sem=vec_send.at[distance],
+            recv_sem=vec_recv.at[distance],
+            device_id=(row ^ distance, member),
+            device_id_type=MESH,
+        )
+        for distance in range(1, 8)
+    ]
+    vector_copies.append(pltpu.make_async_copy(vector_ref, spot, vec_send.at[0]))
+    for copy in vector_copies:
+        copy.start()
+
+    depth_ticks = Z_LAG * hops + 2 * X_LAG
+    due = [FIRST_PIECE + piece * SPREAD // pieces for piece in range(pieces)]
+    for tick in range(max(count + depth_ticks, due[-1] + 1)):
         unit = tick
         if unit < count:
             along_start(unit, 0)
             own_copy(unit).start()
-        if tick < pieces:
-            for step in range(1, members):
-                memory_send(tick, step).start()
+        for piece in range(pieces):
+            if due[piece] == tick:
+                for step in range(1, members):
+                    memory_send(piece, step).start()
         for hop in range(1, hops):
-            unit = tick - hop
+            unit = tick - Z_LAG * hop
             if 0 <= unit < count:
                 along_arrive(unit, hop - 1)
                 along_start(unit, hop)
-        unit = tick - hops
+        unit = tick - Z_LAG * hops
         if 0 <= unit < count:
             along_arrive(unit, hops - 1)
             own_copy(unit).wait()
             to_x(unit).start()
             to_y(unit).start()
             to_core(unit, 0).start()
-        unit = tick - hops - 1
+        unit = tick - Z_LAG * hops - X_LAG
         if 0 <= unit < count:
             to_x(unit).wait_recv()
             half_a(unit).start()
@@ -216,7 +234,7 @@
             to_y(unit).wait_recv()
             half_b(unit).start()
             to_core(unit, 2).start()
-        unit = tick - hops - 2
+        unit = tick - Z_LAG * hops - 2 * X_LAG
         if 0 <= unit < count:
             half_a(unit).wait_recv()
             half_b(unit).wait_recv()
@@ -233,10 +251,14 @@
     for piece in range(pieces):
         for step in range(1, members):
             memory_send(piece, step).wait()
+    fetch.wait()
+    local.start()
     local.wait()
-
-
-def gather_by_kernel(shards, memory, items_count, members):
+    for copy in vector_copies:
+        copy.wait()
+
+
+def gather_by_kernel(shards, memory, vector, items_count, members):
     items_here = memory.shape[0] // members
     units = []
     for weight, shard in enumerate(shards):
@@ -251,10 +273,11 @@
     out_shape.append(
         jax.ShapeDtypeStruct((items_here, members, memory.shape[1], memory.shape[2]), memory.dtype)
     )
+    out_shape.append(jax.ShapeDtypeStruct((vector.shape[0], vector.shape[1] * items_count), vector.dtype))
     outs = pl.pallas_call(
         functools.partial(gather_kernel, members, items_here, tuple(units)),
         out_shape=out_shape,
-        in_specs=[ANY] * (len(shards) + 1),
+        in_specs=[VMEM] * len(shards) + [ANY, VMEM],
         out_specs=[ANY] * len(out_shape),
         scratch_shapes=[
             pltpu.SemaphoreType.DMA((len(units), kinds)),
@@ -262,15 +285,18 @@
             pltpu.SemaphoreType.DMA((len(units),)),
             pltpu.SemaphoreType.DMA((pieces, members)),
             pltpu.SemaphoreType.DMA((pieces, members)),
-            pltpu.SemaphoreType.DMA,
+            pltpu.SemaphoreType.DMA((2,)),
+            pltpu.SemaphoreType.DMA((items_count,)),
+            pltpu.SemaphoreType.DMA((items_count,)),
+            pltpu.VMEM((items_here,) + memory.shape[1:], memory.dtype),
         ],
         compiler_params=pltpu.CompilerParams(collective_id=0, has_side_effects=True),
         name="gather_all",
-    )(*shards, memory)
-    return outs[:-1], outs[-1]
-
-
-def gather_by_collectives(shards, memory, items_count, members):
+    )(*shards, memory, vector)
+    return outs[:-2], outs[-2], outs[-1]
+
+
+def gather_by_collectives(shards, memory, vector, items_count, members):
     whole = []
     for shard in shards:
         cols = lax.all_gather(shard, "mem", axis=1, tiled=True)
@@ -284,7 +310,7 @@
         if step:
             part = lax.ppermute(part, "mem", [(a, (a + step) % members) for a in range(members)])
         parts.append(part)
-    return whole, jnp.stack(parts, 1)
+    return whole, jnp.stack(parts, 1), lax.all_gather(vector, "items", axis=1, tiled=True)
 
 
 def stack_pair(values, lane_low):
@@ -454,6 +480,313 @@
     return [
         reduce_columns(partial[:, k * width : (k + 1) * width], member, members) for k in range(len(grads))
     ]
+
+RING, KEPT, ROUND = 4, 6, 8
+S_LAG = 2
+
+
+def scatter_kernel(members, units, back_rows, *refs):
+    lefts = 1 + max(unit[0] for unit in units)
+    rights = 1 + max(unit[1] for unit in units)
+    outs = 1 + max(unit[2] for unit in units)
+    count = len(units)
+    left_refs, right_refs, part_ref = refs[:lefts], refs[lefts : lefts + rights], refs[lefts + rights]
+    refs = refs[lefts + rights + 1 :]
+    out_refs, back_ref = refs[:outs], refs[outs]
+    (
+        core_out, core_in, near_out, near_in, near_kept, far_out, far_in, own, hop_out, hop_in,
+        send_sem, recv_sem, back_send, back_recv, credit,
+    ) = refs[outs + 1 :]
+    row = lax.axis_index("items")
+    member = lax.axis_index("mem")
+    hops = members - 1
+    core_peer = row ^ 1
+
+    barrier = pltpu.get_barrier_semaphore()
+    partners = [(core_peer, member), (row ^ 2, member), (row ^ 4, member)]
+    partners += [(row, lax.rem(member + step, members)) for step in range(1, members)]
+    for partner in partners:
+        pl.semaphore_signal(barrier, inc=1, device_id=partner, device_id_type=MESH)
+    pl.semaphore_wait(barrier, len(partners))
+
+    def bits(unit):
+        return (2, 4) if unit % 2 == 0 else (4, 2)
+
+    def owners(unit, who):
+        near, far = bits(unit)
+        return (who ^ near, who ^ near ^ far, who ^ far, who)
+
+    def partial(unit, owner):
+        left, right, _, left_start, left_step, right_start, right_step = units[unit]
+        left_ref, right_ref = left_refs[left], right_refs[right]
+        cols = pl.ds(pl.multiple_of(owner * left_step + left_start, 128), 128)
+        depth = left_ref.shape[0]
+        chunk = min(depth, 512)
+
+        def term(start):
+            rows = pl.ds(start, chunk)
+            if right_step == 256:
+                right_value = right_ref[rows, :]
+            else:
+                right_value = jnp.concatenate(
+                    [
+                        right_ref[rows, pl.ds(right_start + k * right_step, 256)]
+                        for k in range(members)
+                    ],
+                    1,
+                )
+            return left_product(left_ref[rows, cols], right_value)
+
+        total = term(0)
+        if depth > chunk:
+            total = lax.fori_loop(
+                1, depth // chunk, lambda k, sums: sums + term(pl.multiple_of(k * chunk, chunk)), total
+            )
+        return total
+
+    def remote(unit, kind, src, dst, device):
+        return pltpu.make_async_remote_copy(
+            src_ref=src,
+            dst_ref=dst,
+            send_sem=send_sem.at[unit, kind],
+            recv_sem=recv_sem.at[unit, kind],
+            device_id=device,
+            device_id_type=MESH,
+        )
+
+    def core_copy(unit):
+        return remote(unit, 0, core_out.at[unit % 2], core_in.at[unit % RING], (core_peer, member))
+
+    def near_copy(unit):
+        return remote(unit, 1, near_out.at[unit % RING], near_in.at[unit % ROUND], (row ^ bits(unit)[0], member))
+
+    def far_copy(unit):
+        return remote(unit, 2, far_out.at[unit % RING], far_in.at[unit % ROUND], (row ^ bits(unit)[1], member))
+
+    def hop_copy(unit, hop, upward):
+        target = jnp.clip(member + 1 if upward else member - 1, 0, members - 1)
+        place = hop if upward else hops + hop
+        return remote(unit, 3 + place, hop_out.at[unit % RING, place], hop_in.at[unit, place], (row, target))
+
+    def hop_sends(hop, upward):
+        distance = members - 1 - hop
+        return (member + distance <= members - 1) if upward else (member - distance >= 0)
+
+    def hop_gets(hop, upward):
+        distance = members - 1 - hop
+        return (
+            ((member >= 1) & (member - 1 + distance <= members - 1))
+            if upward
+            else ((member <= members - 2) & (member + 1 - distance >= 0))
+        )
+
+    def core_stage(unit):
+        if unit >= 2:
+            core_copy(unit - 2).wait_send()
+        targets = owners(unit, core_peer)
+
+        def fill(spot, _):
+            owner = targets[3]
+            for k in range(3):
+                owner = jnp.where(spot == k, targets[k], owner)
+            core_out[unit % 2, spot] = partial(unit, owner).astype(BF16)
+            return 0
+
+        lax.fori_loop(0, 4, fill, 0)
+        if unit >= RING:
+            pl.semaphore_wait(credit, 1)
+        core_copy(unit).start()
+
+    def near_stage(unit):
+        core_copy(unit).wait_recv()
+        if unit >= RING:
+            near_copy(unit - RING).wait_send()
+        mine = owners(unit, row)
+
+        def give(spot, _):
+            total = partial(unit, jnp.where(spot == 0, mine[0], mine[1])) + core_in[unit % RING, spot].astype(F32)
+            near_out[unit % RING, spot] = total.astype(BF16)
+            return 0
+
+        lax.fori_loop(0, 2, give, 0)
+        near_copy(unit).start()
+
+        def keep(spot, _):
+            near_kept[unit % KEPT, spot] = partial(unit, jnp.where(spot == 0, mine[2], mine[3])) + core_in[
+                unit % RING, 2 + spot
+            ].astype(F32)
+            return 0
+
+        lax.fori_loop(0, 2, keep, 0)
+        if unit + RING < count:
+            pl.semaphore_signal(credit, inc=1, device_id=(core_peer, member), device_id_type=MESH)
+
+    def far_stage(unit):
+        near_copy(unit).wait_recv()
+        if unit >= RING:
+            far_copy(unit - RING).wait_send()
+        far_out[unit % RING] = (near_kept[unit % KEPT, 0] + near_in[unit % ROUND, 1].astype(F32)).astype(BF16)
+        far_copy(unit).start()
+
+    def hop_stage(unit, hop):
+        if hop == 0:
+            far_copy(unit).wait_recv()
+            own[unit % RING] = (
+                near_kept[unit % KEPT, 1] + near_in[unit % ROUND, 0].astype(F32) + far_in[unit % ROUND].astype(F32)
+            )
+        for upward in (True, False):
+            distance = members - 1 - hop
+            owner = jnp.clip(member + distance if upward else member - distance, 0, members - 1)
+            place = hop if upward else hops + hop
+            block = pl.ds(pl.multiple_of(owner * 256, 256), 256)
+            if unit >= RING:
+                @pl.when(hop_sends(hop, upward))
+                def _():
+                    hop_copy(unit - RING, hop, upward).wait_send()
+
+            if hop > 0:
+                @pl.when(hop_gets(hop - 1, upward))
+                def _():
+                    hop_copy(unit, hop - 1, upward).wait_recv()
+                    hop_out[unit % RING, place] = (
+                        own[unit % RING, :, block] + hop_in[unit, place - 1].astype(F32)
+                    ).astype(BF16)
+
+                @pl.when(hop_sends(hop, upward) & jnp.logical_not(hop_gets(hop - 1, upward)))
+                def _():
+                    hop_out[unit % RING, place] = own[unit % RING, :, block].astype(BF16)
+
+            else:
+                @pl.when(hop_sends(hop, upward))
+                def _():
+                    hop_out[unit % RING, place] = own[unit % RING, :, block].astype(BF16)
+
+            @pl.when(hop_sends(hop, upward))
+            def _():
+                hop_copy(unit, hop, upward).start()
+
+    def last_stage(unit):
+        _, _, out, left_start, left_step, right_start, right_step = units[unit]
+        rows, cols = pl.ds(left_start, 128), pl.ds(right_start, 256)
+        block = pl.ds(pl.multiple_of(member * 256, 256), 256)
+        out_refs[out][rows, cols] = own[unit % RING, :, block]
+        for upward in (True, False):
+            place = hops - 1 if upward else 2 * hops - 1
+
+            @pl.when(hop_gets(hops - 1, upward))
+            def _():
+                hop_copy(unit, hops - 1, upward).wait_recv()
+                out_refs[out][rows, cols] += hop_in[unit, place].astype(F32)
+
+    pieces = part_ref.shape[2] // back_rows * part_ref.shape[0]
+    items_here = part_ref.shape[0]
+
+    def back_copy(piece, step):
+        which, start = piece // (pieces // items_here), piece % (pieces // items_here) * back_rows
+        target = lax.rem(member - step + members, members)
+        return pltpu.make_async_remote_copy(
+            src_ref=part_ref.at[which, step, pl.ds(start, back_rows)],
+            dst_ref=back_ref.at[member * items_here + which, pl.ds(start, back_rows)],
+            send_sem=back_send.at[piece, step],
+            recv_sem=back_recv.at[piece, step],
+            device_id=(row, target),
+            device_id_type=MESH,
+        )
+
+    far_tick, hop_tick = 1 + S_LAG, 1 + 2 * S_LAG
+    last_tick = hop_tick + hops
+    for tick in range(max(count + last_tick, pieces)):
+        if tick < pieces:
+            for step in range(1, members):
+                back_copy(tick, step).start()
+        if 0 <= tick - far_tick < count:
+            far_stage(tick - far_tick)
+        for hop in range(hops):
+            if 0 <= tick - hop_tick - hop < count:
+                hop_stage(tick - hop_tick - hop, hop)
+        if 0 <= tick - last_tick < count:
+            last_stage(tick - last_tick)
+        if 0 <= tick < count:
+            core_stage(tick)
+        if 0 <= tick - 1 < count:
+            near_stage(tick - 1)
+    for unit in range(count - 2, count):
+        core_copy(unit).wait_send()
+    for unit in range(count - RING, count):
+        near_copy(unit).wait_send()
+        far_copy(unit).wait_send()
+        for hop in range(hops):
+            for upward in (True, False):
+                @pl.when(hop_sends(hop, upward))
+                def _():
+                    hop_copy(unit, hop, upward).wait_send()
+    for piece in range(pieces):
+        for step in range(1, members):
+            back_copy(piece, step).wait()
+
+
+def scatter_by_kernel(pairs, blocks, memory_part, members):
+    lefts, rights, units = [], [], []
+    for out, ((left, right), (height, width)) in enumerate(zip(pairs, blocks)):
+        spots = []
+        for value, found in ((left, lefts), (right, rights)):
+            for place, other in enumerate(found):
+                if other is value:
+                    spots.append(place)
+                    break
+            else:
+                spots.append(len(found))
+                found.append(value)
+        for left_start in range(0, height, 128):
+            for right_start in range(0, width, 256):
+                units.append((spots[0], spots[1], out, left_start, height, right_start, width))
+    count, hops = len(units), members - 1
+    items_here, _, mem_local, width = memory_part.shape
+    back_rows = 32
+    pieces = mem_local // back_rows * items_here
+    outs = pl.pallas_call(
+        functools.partial(scatter_kernel, members, tuple(units), back_rows),
+        out_shape=[jax.ShapeDtypeStruct(block, F32) for block in blocks]
+        + [jax.ShapeDtypeStruct((items_here * members, mem_local, width), BF16)],
+        in_specs=[VMEM] * (len(lefts) + len(rights)) + [ANY],
+        out_specs=[VMEM] * len(blocks) + [ANY],
+        scratch_shapes=[
+            pltpu.VMEM((2, 4, 128, 1024), BF16),
+            pltpu.VMEM((RING, 4, 128, 1024), BF16),
+            pltpu.VMEM((RING, 2, 128, 1024), BF16),
+            pltpu.VMEM((ROUND, 2, 128, 1024), BF16),
+            pltpu.VMEM((KEPT, 2, 128, 1024), F32),
+            pltpu.VMEM((RING, 128, 1024), BF16),
+            pltpu.VMEM((ROUND, 128, 1024), BF16),
+            pltpu.VMEM((RING, 128, 1024), F32),
+            pltpu.VMEM((RING, 2 * hops, 128, 256), BF16),
+            pltpu.VMEM((count, 2 * hops, 128, 256), BF16),
+            pltpu.SemaphoreType.DMA((count, 3 + 2 * hops)),
+            pltpu.SemaphoreType.DMA((count, 3 + 2 * hops)),
+            pltpu.SemaphoreType.DMA((pieces, members)),
+            pltpu.SemaphoreType.DMA((pieces, members)),
+            pltpu.SemaphoreType.REGULAR,
+        ],
+        compiler_params=pltpu.CompilerParams(
+            collective_id=1, has_side_effects=True, vmem_limit_bytes=60 * 1024 * 1024
+        ),
+        name="scatter_all",
+    )(*lefts, *rights, memory_part)
+    return outs[:-1], outs[-1]
+
+
+def scatter_by_collectives(pairs, blocks, memory_part, row, member, items_count, members):
+    grads = []
+    for place, (left, right) in enumerate(pairs):
+        ordered = order_columns(left, row, items_count, place % 2 == 1)
+        grads += weight_gradients(ordered, [right], items_count, member, members, place % 2 == 1)
+    items_here = memory_part.shape[0]
+    back = jnp.zeros((items_here * members,) + memory_part.shape[2:], BF16)
+    for step in range(1, members):
+        part = lax.ppermute(memory_part[:, step], "mem", [(a, (a - step) % members) for a in range(members)])
+        owner = lax.rem(member + step, members)
+        back = lax.dynamic_update_slice_in_dim(back, part, owner * items_here, 0)
+    return grads, back
 
 
 def body(
@@ -487,16 +820,23 @@
     shards = (
         self_query, self_key, self_value, self_out, cross_query, cross_key, cross_value, cross_out, feed_in, feed_out,
     )
-    gather = gather_by_kernel if (items_count, members) == (8, 4) else gather_by_collectives
-    whole, item_memory = gather(shards, memory, items_count, members)
+    by_kernel = (items_count, members) == (8, 4)
+    shift_width, bias_rows = shifts.shape[1], inner_bias.shape[0] // shifts.shape[1]
+    vector = jnp.concatenate([shifts, gains, inner_bias.reshape(bias_rows, shift_width)], 0)
+    gather = gather_by_kernel if by_kernel else gather_by_collectives
+    whole, item_memory, vectors = gather(shards, memory, vector, items_count, members)
     (
         query_self, key_self, value_self, output_self, query_cross, key_cross, value_cross, output_cross,
         feed_up, feed_down,
     ) = whole
     memory_flat = item_memory.reshape(-1, D)
-    shift_rows = lax.all_gather(shifts, "items", axis=1, tiled=True).astype(F32)
-    gain_rows = lax.all_gather(gains, "items", axis=1, tiled=True).astype(F32)
-    inner_shift = lax.all_gather(inner_bias, "items", axis=0, tiled=True).astype(F32)
+    vectors = vectors.astype(F32)
+    bias_start = shifts.shape[0] + gains.shape[0]
+    shift_rows = vectors[: shifts.shape[0]]
+    gain_rows = vectors[shifts.shape[0] : bias_start]
+    inner_shift = (
+        vectors[bias_start:].reshape(bias_rows, items_count, shift_width).transpose(1, 0, 2).reshape(-1)
+    )
 
     own_dec = lax.dynamic_slice_in_dim(dec_len, member * item_count, item_count)
     own_mem = lax.dynamic_slice_in_dim(mem_len, member * item_count, item_count)
@@ -532,23 +872,16 @@
     )
     grad_down = grad_three.astype(BF16)
 
-    def summed(values, grads, flipped):
-        ordered = order_columns(values, row, items_count, flipped)
-        return weight_gradients(ordered, grads, items_count, member, members, flipped)
-
-    (feed_down_grad,) = summed(active_low, [grad_down], False)
     out_bias_grad = column_sums(grad_down)
     grad_active = right_product(grad_down, feed_down)
     slope = cdf_part + inner_pre * jnp.exp(-0.5 * inner_pre * inner_pre) * normal_peak
     grad_inner = (grad_active * slope).astype(BF16)
-    (feed_up_grad,) = summed(hidden_two_low, [grad_inner], True)
     inner_bias_grad = column_sums(grad_inner)
     grad_hidden_two = grad_three + right_product(grad_inner, feed_up)
     grad_two, gain_grad_two, shift_grad_two = norm_backward(
         grad_hidden_two, normed_two, inverse_two, gain_rows[1]
     )
     grad_cross_branch = grad_two.astype(BF16)
-    (output_cross_grad,) = summed(mixed_two, [grad_cross_branch], False)
     cross_out_bias_grad = column_sums(grad_cross_branch)
     grad_mixed_two = right_product(grad_cross_branch, output_cross)
     query_grad_two, key_grad_two, value_grad_two = attend_backward(
@@ -559,32 +892,47 @@
     memory_part = (
         right_product(key_grad_two, key_cross) + right_product(value_grad_two, value_cross)
     ).astype(BF16).reshape(item_count, members, mem_local, D)
-    memory_grad = jnp.zeros((group_items, mem_local, D), F32)
-    for step in range(members):
-        part = memory_part[:, step]
-        if step:
-            part = lax.ppermute(part, "mem", [(a, (a - step) % members) for a in range(members)])
-        owner = lax.rem(member + step, members)
-        memory_grad = lax.dynamic_update_slice_in_dim(memory_grad, part.astype(F32), owner * item_count, 0)
-
-    key_cross_grad, value_cross_grad = summed(memory_flat, [key_grad_two, value_grad_two], True)
     cross_value_bias_grad = column_sums(value_grad_two)
-    (query_cross_grad,) = summed(hidden_one_low, [query_grad_two], False)
     cross_query_bias_grad = column_sums(query_grad_two)
     grad_hidden_one = grad_two + right_product(query_grad_two, query_cross)
     grad_one, gain_grad_one, shift_grad_one = norm_backward(
         grad_hidden_one, normed_one, inverse_one, gain_rows[0]
     )
     grad_self_branch = grad_one.astype(BF16)
-    (output_self_grad,) = summed(mixed_one, [grad_self_branch], True)
     self_out_bias_grad = column_sums(grad_self_branch)
     grad_mixed_one = right_product(grad_self_branch, output_self)
     query_grad_one, key_grad_one, value_grad_one = attend_backward(
         True, DEC, own_dec, bases, queries_one, keys_one, values_one, grad_mixed_one, exact_one, scale_one
     )
     query_grad_one = query_grad_one * jnp.asarray(0.125, BF16)
-    query_self_grad, key_self_grad, value_self_grad = summed(
-        tokens, [query_grad_one, key_grad_one, value_grad_one], False
+    pairs = (
+        (active_low, grad_down),
+        (hidden_two_low, grad_inner),
+        (mixed_two, grad_cross_branch),
+        (memory_flat, key_grad_two),
+        (memory_flat, value_grad_two),
+        (hidden_one_low, query_grad_two),
+        (mixed_one, grad_self_branch),
+        (tokens, query_grad_one),
+        (tokens, key_grad_one),
+        (tokens, value_grad_one),
+    )
+    blocks = tuple(
+        weight.shape
+        for weight in (
+            feed_out, feed_in, cross_out, cross_key, cross_value, cross_query, self_out, self_query, self_key, self_value,
+        )
+    )
+    if by_kernel:
+        grads, memory_back = scatter_by_kernel(pairs, blocks, memory_part, members)
+    else:
+        grads, memory_back = scatter_by_collectives(pairs, blocks, memory_part, row, member, items_count, members)
+    (
+        feed_down_grad, feed_up_grad, output_cross_grad, key_cross_grad, value_cross_grad, query_cross_grad,
+        output_self_grad, query_self_grad, key_self_grad, value_self_grad,
+    ) = grads
+    memory_grad = lax.dynamic_update_slice_in_dim(
+        memory_back.astype(F32), memory_part[:, 0].astype(F32), member * item_count, 0
     )
     tokens_grad = (
         grad_one

time: 821 us -> 549 us (0.67)
  waiting for transfers between devices: 249 us -> 0.02 us
  Pallas kernels: 249 us -> 417 us
  local copies, waits for them, and re-layouts: 71.7 us -> 16.8 us
  starting transfers between devices: 46.2 us -> 0.04 us
  matrix products: 100 us -> 68.8 us
  other arithmetic: 51.7 us -> 23.7 us
  blocking collectives: 28 us -> 0 us
    ppermute x44 -> x0, waiting for transfers between devices: 234 us -> none  [the longest x21 120 us: reduce_rows(): lax.ppermute(partial[half:], 'items', [(a, a ^ bit) for a in range(items_...]
    pallas_call x0 -> x1, Pallas kernels: none -> 183 us  [scatter_by_kernel(): pl.pallas_call(functools.partial(scatter_kernel, members, tuple(units), b...]
    ppermute x44 -> x0, starting transfers between devices: 46.2 us -> none  [the longest x20 21.7 us: reduce_columns(): lax.ppermute(jnp.where(high, left, right), 'mem', [(a, a ^ bit) for a in...]
    dot_general x7 -> x0, matrix products: 29.8 us -> none  [left_product(): lax.dot_general(first_op, second_op, (((0,), (0,)), ((), ())), preferred_...]
    all_gather x3 -> x0, blocking collectives: 28 us -> none  [the longest x1 10.5 us: body(): shift_rows = lax.all_gather(shifts, 'items', axis=1, tiled=True).astype(F32)]
    unnamed x201 -> x109, local copies, waits for them, and re-layouts: 37.5 us -> 9.69 us
    slice x22 -> x1, local copies, waits for them, and re-layouts: 18.5 us -> 0.77 us  [body(): vectors[bias_start:].reshape(bias_rows, items_count, shift_width)]
    psum x1, waiting for transfers between devices: 15.1 us -> 0.01 us  [body(): vectors = lax.psum(vectors.reshape(-1, 128), ('items', 'mem')).reshape(-1)]
  transfers between devices with their start and end apart: 45 -> 1, of which waited for: 29 -> 0; matrix products, arithmetic and copies ran while one was open for 19% -> 5% of each run, Pallas kernels for 0% -> 34%
where the time goes in v2:
time: 549 us; the launch traced here: 542 us
  Pallas kernels  417 us (76%)
  matrix products  68.8 us (13%)
  other arithmetic  23.7 us (4%)
  local copies, waits for them, and re-layouts  16.8 us (3%)
  between operations  15.2 us (3%)
    pallas_call x1, Pallas kernels, scatter_by_kernel(): pl.pallas_call(functools.partial(scatter_kernel, members, tuple(units), b...  183 us
    pallas_call x1, Pallas kernels, gather_by_kernel(): pl.pallas_call(functools.partial(gather_kernel, members, items_here, tupl...  168 us
    pallas_call x4, Pallas kernels, attention_call(): pl.pallas_call(functools.partial(kernel, causal, chunk), grid_spec=pltpu....  66.5 us
    dot_general x10, matrix products, product(): return jnp.dot(first_op, second_op, preferred_element_type=F32)  35.5 us
    dot_general x10, matrix products, right_product(): lax.dot_general(first_op, second_op, (((1,), (1,)), ((), ())), preferred_...  33.3 us
  transfers between devices with their start and end apart: 1, of which 0 were waited for; matrix products, arithmetic and copies ran while one was open for 5% of the time, Pallas kernels for 34%

profile of v2, /device:TPU:0, one launch (start us, length us, event | category | flops | bytes accessed | tf_op | source)
XLA Modules:
  0.0 541.8 jit_solution(7316369733627224682)
XLA Ops:
  7.2 1.4 pad_maximum_fusion.refs_11_
  8.6 168.3 %gather_all.1 = (bf16[1024,1024]{1,0:T(8,128)(2,1)}, bf16[1024,1024]{1,0:T(8,128)(2,1)}, bf16[1024,1024]{1,0:T(8,128)(2,1)}, bf16[1024,1024]{1,0:T(8,128)(2,1)},...) custom-call(bf16[128,256]{1,0:T(8,128)(2,1)} %refs_0_.1, ...), custom_call_target="tpu_custom_call" | custom-call | tf_op jit(solution)/shard_map/gather_all/pallas_call | solution.py:277
  176.9 1.1 fusion.29
  178.0 0.8 slice.106
  179.3 3.2 fusion.17.k_ref
  182.5 3.3 fusion.16.v_ref
  185.8 1.5 fusion.18.q_ref
  187.9 11.9 %self_attention.2 = (bf16[256,1024]{1,0:T(8,128)(2,1)}, f32[256,1024]{1,0:T(8,128)}, f32[256,1024]{1,0:T(8,128)}) custom-call(s32[2]{0:T(128)} %dynamic_slice.15.lens_ref, s32[4]{0:T(128)} %fusion.26.bases_ref, bf16[256,1024]{1,0:T(8,128)(2,1)} %fusion.18.q_ref, bf16[256,1024]{1,0:T(8,128)(2,1)} %fusion.17.k_ref, bf16[256,1024]{1,0:T(8,128)(2,1)} %fusion.16.v_ref), custom_call_target="tpu_custom_call" | custom-call | flops 536870912 | bytes 2097152 | tf_op jit(solution)/shard_map/self_attention/pallas_call | solution.py:393
  199.8 2.2 fusion.30
  202.9 7.8 %convolution_convert_fusion.k_ref = bf16[2048,1024]{1,0:T(8,128)(2,1)} fusion(bf16[2048,1024]{1,0:T(8,128)(2,1)S(1)} %bitcast.76, bf16[1024,1024]{1,0:T(8,128)(2,1)} %get-tuple-element.59), kind=kOutput, calls=%fused_computation.14 | convolution fusion | flops 4297064448 | bytes 10485760 | tf_op jit(solution)/shard_map/dot_general | solution.py:27
  210.7 6.0 %add_convert_fusion.1.v_ref = bf16[2048,1024]{1,0:T(8,128)(2,1)} fusion(f32[1024]{0:T(1024)S(1)} %bitcast.99, bf16[2048,1024]{1,0:T(8,128)(2,1)S(1)} %bitcast.77, bf16[1024,1024]{1,0:T(8,128)(2,1)S(1)} %copy-done.34), kind=kOutput, calls=%fused_computation.2 | convolution fusion | flops 4299161600 | bytes 10489856 | tf_op jit(solution)/shard_map/dot_general | solution.py:27
  217.0 0.8 copy-done.19
  217.8 1.5 fusion.13.q_ref
  219.3 16.5 %cross_attention.2 = (bf16[256,1024]{1,0:T(8,128)(2,1)}, f32[256,1024]{1,0:T(8,128)}, f32[256,1024]{1,0:T(8,128)}) custom-call(s32[2]{0:T(128)} %dynamic_slice.16.lens_ref, s32[4]{0:T(128)} %fusion.26.bases_ref, bf16[256,1024]{1,0:T(8,128)(2,1)} %fusion.13.q_ref, bf16[2048,1024]{1,0:T(8,128)(2,1)} %convolution_convert_fusion.k_ref, ...), custom_call_target="tpu_custom_call" | custom-call | flops 4294967296 | bytes 16777216 | tf_op jit(solution)/shard_map/cross_attention/pallas_call | solution.py:393
  235.9 1.9 fusion.31
  238.3 5.5 %multiply_convert_fusion = (bf16[256,4096]{1,0:T(8,128)(2,1)S(1)}, f32[256,4096]{1,0:T(8,128)S(1)}) fusion(f32[4096]{0:T(1024)S(1)} %bitcast.95, bf16[256,1024]{1,0:T(8,128)(2,1)S(1)} %fusion.24.refs_1_, bf16[1024,4096]{1,0:T(8,128)(2,1)} %get-tuple-element.63), kind=kOutput, calls=%fused_computation.12 | convolution fusion | flops 2153775104 | bytes 15220736 | tf_op jit(solution)/shard_map/dot_general | solution.py:27
  244.2 2.6 fusion.32
  247.6 1.4 convert_reduce_fusion.3
  249.0 6.6 %convert_reduce_fusion.1 = (f32[4096]{0:T(1024)S(1)}, bf16[256,4096]{1,0:T(8,128)(2,1)S(1)}) fusion(f32[256,4096]{1,0:T(8,128)S(1)} %get-tuple-element.125, bf16[256,1024]{1,0:T(8,128)(2,1)S(1)} %get-tuple-element.99.refs_7_, bf16[4096,1024]{1,0:T(8,128)(2,1)} %get-tuple-element.64), kind=kOutput, calls=%fused_computation.11 | convolution fusion | flops 2160062464 | bytes 15220736 | tf_op jit(solution)/shard_map/dot_general | solution.py:37
  255.7 3.0 multiply_reduce_fusion
  259.1 1.8 fusion.33.grad_ref
  260.9 24.9 %cross_attention.3 = (bf16[256,1024]{1,0:T(8,128)(2,1)}, bf16[2048,1024]{1,0:T(8,128)(2,1)}, bf16[2048,1024]{1,0:T(8,128)(2,1)}) custom-call(s32[2]{0:T(128)} %dynamic_slice.16.lens_ref, s32[4]{0:T(128)} %fusion.26.bases_ref, bf16[256,1024]{1,0:T(8,128)(2,1)} %fusion.13.q_ref, bf16[2048,1024]{1,0:T(8,128)(2,1)} %convolution_convert_fusion.k_ref, ...), custom_call_target="tpu_custom_call" | custom-call | flops 4294967296 | bytes 16777216 | tf_op jit(solution)/shard_map/cross_attention/pallas_call | solution.py:393
  285.7 1.2 convert_reduce_fusion.5
  286.9 3.0 multiply_reduce_fusion.1
  290.3 1.7 fusion.34.grad_ref
  292.1 13.2 %self_attention.3 = (bf16[256,1024]{1,0:T(8,128)(2,1)}, bf16[256,1024]{1,0:T(8,128)(2,1)}, bf16[256,1024]{1,0:T(8,128)(2,1)}) custom-call(s32[2]{0:T(128)} %dynamic_slice.15.lens_ref, s32[4]{0:T(128)} %fusion.26.bases_ref, bf16[256,1024]{1,0:T(8,128)(2,1)} %fusion.18.q_ref, bf16[256,1024]{1,0:T(8,128)(2,1)} %fusion.17.k_ref, ...), custom_call_target="tpu_custom_call" | custom-call | flops 536870912 | bytes 2097152 | tf_op jit(solution)/shard_map/self_attention/pallas_call | solution.py:393
  305.2 1.3 convert_reduce_fusion.8
  306.5 1.1 convert_reduce_fusion.7
  307.6 2.9 convert_reduce_fusion
  311.3 0.8 broadcast_multiply_fusion.refs_14_
  312.2 0.8 broadcast_multiply_fusion.1.refs_12_
  313.0 7.3 %fusion.35 = f32[2048,1024]{1,0:T(8,128)S(1)} fusion(bf16[2048,1024]{1,0:T(8,128)(2,1)} %get-tuple-element.73.refs_10_, bf16[1024,1024]{1,0:T(8,128)(2,1)} %get-tuple-element.59), kind=kOutput, calls=%fused_computation.118 | convolution fusion | flops 4294967296 | bytes 14680064 | tf_op jit(solution)/shard_map/dot_general | solution.py:37
  320.4 6.6 %add_convert_fusion = bf16[2048,1024]{1,0:T(8,128)(2,1)} fusion(f32[2048,1024]{1,0:T(8,128)S(1)} %fusion.35, bf16[2048,1024]{1,0:T(8,128)(2,1)S(1)} %copy-done, bf16[1024,1024]{1,0:T(8,128)(2,1)S(1)} %copy-done.35), kind=kOutput, calls=%fused_computation.1 | convolution fusion | flops 4299161600 | bytes 18874368 | tf_op jit(solution)/shard_map/dot_general | solution.py:37
  327.0 182.5 %scatter_all.1 = (f32[512,256]{1,0:T(8,128)}, f32[128,1024]{1,0:T(8,128)}, f32[128,256]{1,0:T(8,128)}, f32[128,256]{1,0:T(8,128)}, f32[128,256]{1,0:T(8,128)}, /...) custom-call(bf16[256,4096]{1,0:T(8,128)(2,1)} %copy-done.16, ...), custom_call_target="tpu_custom_call" | custom-call | tf_op jit(solution)/shard_map/scatter_all/pallas_call | solution.py:747
  509.5 6.8 %convert_element_type.110 = f32[8,256,1024]{2,1,0:T(8,128)} convert(bf16[8,256,1024]{2,1,0:T(8,128)(2,1)} %get-tuple-element.75) | non-fusion elementwise | flops 2097152 | bytes 12582912 | tf_op jit(solution)/shard_map/convert_element_type | solution.py:935
  516.3 0.8 convolution_add_fusion.5
  517.1 0.8 copy-done.11
  518.0 0.7 convolution_add_fusion.4
  518.9 1.8 convolution_add_fusion.3
  520.7 2.8 convert_dynamic-update-slice_fusion
  523.5 0.8 slice.111
  524.3 0.7 slice.112
  526.2 0.7 slice_bitcast_fusion.1
  528.9 0.7 copy.71
  529.6 0.7 copy.72
  530.2 0.7 copy.73
  532.9 0.8 copy.77
  533.7 0.8 copy.78
  (135 shorter events, 10.8 us)
Async XLA Ops:
  7.2 172.1 %copy-start.24 = (bf16[256,1024]{1,0:T(8,128)(2,1)S(1)}, bf16[256,1024]{1,0:T(8,128)(2,1)}, u32[]{:S(2)}) copy-start(bf16[256,1024]{1,0:T(8,128)(2,1)} %refs_6_.3) | copy-start | bytes 1572868
  7.2 516.3 %all-reduce.2.cloned.1.call-start = ((), (), s32[]{:S(2)}) async-start(), calls=%async_computation | async-start | bytes 139264 | tf_op jit(solution)/shard_map/psum | solution.py:961
  179.3 6.5 %copy-start.12 = (bf16[1024,1024]{1,0:T(8,128)(2,1)S(1)}, bf16[1024,1024]{1,0:T(8,128)(2,1)}, u32[]{:S(2)}) copy-start(bf16[1024,1024]{1,0:T(8,128)(2,1)} %get-tuple-element.51) | copy-start | bytes 6291460
  182.5 4.8 copy-start.37
  182.5 17.3 %copy-start.6 = (bf16[1024,1024]{1,0:T(8,128)(2,1)S(1)}, bf16[1024,1024]{1,0:T(8,128)(2,1)}, u32[]{:S(2)}) copy-start(bf16[1024,1024]{1,0:T(8,128)(2,1)} %get-tuple-element.56) | copy-start | bytes 6291460
  187.3 15.0 %copy-start.38 = (s32[8]{0:T(128)S(1)}, s32[8]{0:T(128)}, u32[]{:S(2)}) copy-start(s32[8]{0:T(128)} %param.21) | copy-start | bytes 100
  199.8 3.1 copy-start.5
  202.9 7.8 %copy-start.34 = (bf16[1024,1024]{1,0:T(8,128)(2,1)S(1)}, bf16[1024,1024]{1,0:T(8,128)(2,1)}, u32[]{:S(2)}) copy-start(bf16[1024,1024]{1,0:T(8,128)(2,1)} %get-tuple-element.60) | copy-start | bytes 6291460
  210.7 7.1 %copy-start.36 = (bf16[1024,1024]{1,0:T(8,128)(2,1)S(1)}, bf16[1024,1024]{1,0:T(8,128)(2,1)}, u32[]{:S(2)}) copy-start(bf16[1024,1024]{1,0:T(8,128)(2,1)} %get-tuple-element.57) | copy-start | bytes 6291460
  217.0 0.8 copy-start.19
  219.3 16.6 %copy-start.8 = (bf16[1024,1024]{1,0:T(8,128)(2,1)S(1)}, bf16[1024,1024]{1,0:T(8,128)(2,1)}, u32[]{:S(2)}) copy-start(bf16[1024,1024]{1,0:T(8,128)(2,1)} %get-tuple-element.62) | copy-start | bytes 6291460
  238.0 5.9 %slice-start.2 = ((s8[8388608]{0:T(1024)(128)(4,1)}), s8[4194304]{0:T(1024)(128)(4,1)S(1)}, s32[]{:S(2)}) async-start(s8[8388608]{0:T(1024)(128)(4,1)} %bitcast.106), calls=%async_computation.3 | async-start | bytes 8388608
  238.3 5.6 %copy-start.20 = (bf16[256,1024]{1,0:T(8,128)(2,1)}, bf16[256,1024]{1,0:T(8,128)(2,1)S(1)}, u32[]{:S(2)}) copy-start(bf16[256,1024]{1,0:T(8,128)(2,1)S(1)} %fusion.24.refs_1_) | copy-start | bytes 1572868
  238.3 5.9 %slice-start.3 = ((s8[8388608]{0:T(1024)(128)(4,1)}), s8[4194304]{0:T(1024)(128)(4,1)S(1)}, s32[]{:S(2)}) async-start(s8[8388608]{0:T(1024)(128)(4,1)} %bitcast.106), calls=%async_computation.4 | async-start | bytes 8388608
  243.9 2.9 copy-start.16
  244.2 2.9 copy-start.14
  247.6 8.1 %slice-start = ((s8[8388608]{0:T(1024)(128)(4,1)}), s8[4194304]{0:T(1024)(128)(4,1)S(1)}, s32[]{:S(2)}) async-start(s8[8388608]{0:T(1024)(128)(4,1)} %bitcast.104), calls=%async_computation.1 | async-start | bytes 8388608
  249.0 6.6 %copy-start.21 = (bf16[256,1024]{1,0:T(8,128)(2,1)}, bf16[256,1024]{1,0:T(8,128)(2,1)S(1)}, u32[]{:S(2)}) copy-start(bf16[256,1024]{1,0:T(8,128)(2,1)S(1)} %get-tuple-element.99.refs_7_) | copy-start | bytes 1572868
  249.0 6.6 %slice-start.1 = ((s8[8388608]{0:T(1024)(128)(4,1)}), s8[4194304]{0:T(1024)(128)(4,1)S(1)}, s32[]{:S(2)}) async-start(s8[8388608]{0:T(1024)(128)(4,1)} %bitcast.104), calls=%async_computation.2 | async-start | bytes 8388608
  255.6 3.0 copy-start.17
  255.7 3.4 copy-start.9
  259.1 26.7 %copy-start.3 = (bf16[256,1024]{1,0:T(8,128)(2,1)}, bf16[256,1024]{1,0:T(8,128)(2,1)S(1)}, u32[]{:S(2)}) copy-start(bf16[256,1024]{1,0:T(8,128)(2,1)S(1)} %get-tuple-element.101.refs_9_) | copy-start | bytes 1572868
  286.9 3.4 copy-start.7
  290.3 14.9 %copy-start.4 = (bf16[256,1024]{1,0:T(8,128)(2,1)}, bf16[256,1024]{1,0:T(8,128)(2,1)S(1)}, u32[]{:S(2)}) copy-start(bf16[256,1024]{1,0:T(8,128)(2,1)S(1)} %get-tuple-element.104.refs_13_) | copy-start | bytes 1572868
  305.2 6.1 %copy-start.1 = (bf16[256,1024]{1,0:T(8,128)(2,1)S(1)}, bf16[256,1024]{1,0:T(8,128)(2,1)}, u32[]{:S(2)}) copy-start(bf16[256,1024]{1,0:T(8,128)(2,1)} %get-tuple-element.70) | copy-start | bytes 1572868
  305.2 6.9 %copy-start.15 = (bf16[256,1024]{1,0:T(8,128)(2,1)S(1)}, bf16[256,1024]{1,0:T(8,128)(2,1)}, u32[]{:S(2)}) copy-start(bf16[256,1024]{1,0:T(8,128)(2,1)} %get-tuple-element.67) | copy-start | bytes 1572868
  310.6 0.6 copy-start.33
  313.0 7.4 %copy-start = (bf16[2048,1024]{1,0:T(8,128)(2,1)S(1)}, bf16[2048,1024]{1,0:T(8,128)(2,1)}, u32[]{:S(2)}) copy-start(bf16[2048,1024]{1,0:T(8,128)(2,1)} %get-tuple-element.74.refs_11_) | copy-start | bytes 12582916
  313.0 7.4 %copy-start.35 = (bf16[1024,1024]{1,0:T(8,128)(2,1)S(1)}, bf16[1024,1024]{1,0:T(8,128)(2,1)}, u32[]{:S(2)}) copy-start(bf16[1024,1024]{1,0:T(8,128)(2,1)} %get-tuple-element.60) | copy-start | bytes 6291460
  509.5 6.8 %copy-start.13 = (bf16[1024,1024]{1,0:T(8,128)(2,1)S(1)}, bf16[1024,1024]{1,0:T(8,128)(2,1)}, u32[]{:S(2)}) copy-start(bf16[1024,1024]{1,0:T(8,128)(2,1)} %get-tuple-element.51) | copy-start | bytes 6291460
  516.3 1.6 copy-start.11
  516.3 1.7 copy-start.18
  516.3 2.4 copy-start.2
  516.3 2.5 copy-start.10
  518.8 8.8 %copy-start.32 = (f32[128,256]{1,0:T(8,128)S(1)}, f32[128,256]{1,0:T(8,128)}, u32[]{:S(2)}) copy-start(f32[128,256]{1,0:T(8,128)} %get-tuple-element.153) | copy-start | bytes 393220
  518.8 9.4 %copy-start.31 = (f32[128,256]{1,0:T(8,128)S(1)}, f32[128,256]{1,0:T(8,128)}, u32[]{:S(2)}) copy-start(f32[128,256]{1,0:T(8,128)} %get-tuple-element.154) | copy-start | bytes 393220
  518.8 10.1 %copy-start.30 = (f32[128,256]{1,0:T(8,128)S(1)}, f32[128,256]{1,0:T(8,128)}, u32[]{:S(2)}) copy-start(f32[128,256]{1,0:T(8,128)} %get-tuple-element.155) | copy-start | bytes 393220
  518.8 10.7 %copy-start.29 = (f32[128,256]{1,0:T(8,128)S(1)}, f32[128,256]{1,0:T(8,128)}, u32[]{:S(2)}) copy-start(f32[128,256]{1,0:T(8,128)} %get-tuple-element.156) | copy-start | bytes 393220
  518.8 11.4 %copy-start.28 = (f32[128,256]{1,0:T(8,128)S(1)}, f32[128,256]{1,0:T(8,128)}, u32[]{:S(2)}) copy-start(f32[128,256]{1,0:T(8,128)} %get-tuple-element.157) | copy-start | bytes 393220
  518.9 12.0 %copy-start.27 = (f32[128,256]{1,0:T(8,128)S(1)}, f32[128,256]{1,0:T(8,128)}, u32[]{:S(2)}) copy-start(f32[128,256]{1,0:T(8,128)} %get-tuple-element.158) | copy-start | bytes 393220
  518.9 12.7 %copy-start.26 = (f32[128,256]{1,0:T(8,128)S(1)}, f32[128,256]{1,0:T(8,128)}, u32[]{:S(2)}) copy-start(f32[128,256]{1,0:T(8,128)} %get-tuple-element.159) | copy-start | bytes 393220
  518.9 13.3 %copy-start.25 = (f32[128,256]{1,0:T(8,128)S(1)}, f32[128,256]{1,0:T(8,128)}, u32[]{:S(2)}) copy-start(f32[128,256]{1,0:T(8,128)} %get-tuple-element.160) | copy-start | bytes 393220
  518.9 14.0 %copy-start.23 = (f32[128,1024]{1,0:T(8,128)S(1)}, f32[128,1024]{1,0:T(8,128)}, u32[]{:S(2)}) copy-start(f32[128,1024]{1,0:T(8,128)} %get-tuple-element.161) | copy-start | bytes 1572868
  520.7 13.0 %copy-start.22 = (f32[512,256]{1,0:T(8,128)S(1)}, f32[512,256]{1,0:T(8,128)}, u32[]{:S(2)}) copy-start(f32[512,256]{1,0:T(8,128)} %get-tuple-element.162) | copy-start | bytes 1572868
Sparse Core Ops, SparseCore 0:
  311.4 120.4 all-reduce.1

commit v3 on v2

--- a/solution.py
+++ b/solution.py
@@ -60,12 +60,16 @@
     return (grad_in, jnp.sum(grad_out * normed, 0), jnp.sum(grad_out, 0))
 
 
-def gather_kernel(members, items_here, units, *refs):
+def gather_kernel(members, items_here, units, forward, *refs):
     count = len(units)
     weights = 1 + max(unit[0] for unit in units)
-    shard_refs, memory_ref, vector_ref = refs[:weights], refs[weights], refs[weights + 1]
-    whole_refs, items_ref, vectors_ref = refs[weights + 2 : 2 * weights + 2], refs[2 * weights + 2], refs[2 * weights + 3]
-    send_sem, recv_sem, copy_sem, mem_send, mem_recv, mem_copy, vec_send, vec_recv, bounce = refs[2 * weights + 4 :]
+    shard_refs = refs[:weights]
+    memory_ref, vector_ref, tokens_ref, limits_ref = refs[weights : weights + 4]
+    refs = refs[weights + 4 :]
+    whole_refs, items_ref, vectors_ref = refs[:weights], refs[weights], refs[weights + 1]
+    refs = refs[weights + 2 :]
+    outs, refs = refs[: forward.outs], refs[forward.outs :]
+    send_sem, recv_sem, copy_sem, mem_send, mem_recv, mem_copy, vec_send, vec_recv, bounce = refs[:9]
     row = lax.axis_index("items")
     member = lax.axis_index("mem")
     hops = members - 1
@@ -203,9 +207,14 @@
     for copy in vector_copies:
         copy.start()
 
-    depth_ticks = Z_LAG * hops + 2 * X_LAG
     due = [FIRST_PIECE + piece * SPREAD // pieces for piece in range(pieces)]
-    for tick in range(max(count + depth_ticks, due[-1] + 1)):
+    done_lag = Z_LAG * hops + 2 * X_LAG + 1
+    jobs = forward.jobs(
+        members, items_here, member, tokens_ref, limits_ref, whole_refs, items_ref, vectors_ref, outs, refs[9:],
+        done_lag, due,
+    )
+    last = max([count - 1 + done_lag, due[-1] + 2] + list(jobs))
+    for tick in range(last + 1):
         unit = tick
         if unit < count:
             along_start(unit, 0)
@@ -239,6 +248,23 @@
             half_a(unit).wait_recv()
             half_b(unit).wait_recv()
             to_core(unit, 3).start()
+        if tick == 1:
+            fetch.wait()
+            local.start()
+        if tick == 3:
+            local.wait()
+            for copy in vector_copies:
+                copy.wait()
+        unit = tick - done_lag
+        if 0 <= unit < count:
+            for which in range(4):
+                to_core(unit, which).wait_recv()
+        for piece in range(pieces):
+            if due[piece] + 2 == tick:
+                for step in range(1, members):
+                    memory_send(piece, step).wait_recv()
+        for job in jobs.get(tick, ()):
+            job()
     for unit in range(count):
         for hop in range(hops):
             along_sent(unit, hop)
@@ -247,18 +273,224 @@
         half_a(unit).wait_send()
         half_b(unit).wait_send()
         for which in range(4):
-            to_core(unit, which).wait()
+            to_core(unit, which).wait_send()
     for piece in range(pieces):
         for step in range(1, members):
-            memory_send(piece, step).wait()
-    fetch.wait()
-    local.start()
-    local.wait()
-    for copy in vector_copies:
-        copy.wait()
-
-
-def gather_by_kernel(shards, memory, vector, items_count, members):
+            memory_send(piece, step).wait_send()
+    forward.finish()
+
+
+def attend_pair(queries, keys_at, values_at, allowed_at, chunks):
+    lane_low = low_lanes(DEC)
+    q2 = stack_pair(queries, lane_low)
+    numer, total = None, None
+    for step in range(chunks):
+        scores = right_product(q2, keys_at(step))
+        exp_scores = jnp.where(allowed_at(step), jnp.exp(scores), 0.0)
+        part = jnp.sum(exp_scores, -1, keepdims=True)
+        term = product(exp_scores.astype(BF16), values_at(step))
+        total = part if total is None else total + part
+        numer = term if numer is None else numer + term
+    numer = jnp.where(lane_low, numer[:DEC], numer[DEC:])
+    scale = 1.0 / jnp.where(lane_low, total[:DEC], total[DEC:])
+    return numer * scale, scale
+
+
+class Forward:
+    outs = 15
+
+    def __init__(self, rows, items_here, members, mem_local):
+        self.rows, self.items_here, self.members, self.mem_local = rows, items_here, members, mem_local
+        self.slots = members * mem_local
+
+    def out_shapes(self):
+        wide, low = jax.ShapeDtypeStruct((self.rows, D), F32), jax.ShapeDtypeStruct((self.rows, D), BF16)
+        keys = jax.ShapeDtypeStruct((self.items_here, self.members, self.mem_local, D), BF16)
+        inverse = jax.ShapeDtypeStruct((self.rows, 1), F32)
+        return [low, low, low, low, wide, wide, wide, wide, inverse, low, low, wide, wide, keys, keys]
+
+    def out_specs(self):
+        return [VMEM] * 13 + [ANY] * 2
+
+    def scratch(self):
+        return [
+            pltpu.VMEM((2, D, D), BF16),
+            pltpu.VMEM((2, D, D), BF16),
+            pltpu.VMEM((2, self.members, self.mem_local // 4, D), BF16),
+            pltpu.VMEM((self.items_here, self.members, self.mem_local, D), BF16),
+            pltpu.VMEM((self.items_here, self.members, self.mem_local, D), BF16),
+            pltpu.SemaphoreType.DMA((16,)),
+        ]
+
+    def jobs(
+        self, members, items_here, member, tokens_ref, limits_ref, whole_refs, items_ref, vectors_ref, outs, scratch,
+        done_lag, due,
+    ):
+        (
+            q_one, k_one, v_one, mixed_one, exact_one, scale_one, hidden_one, normed_one, inverse_one, q_two, mixed_two,
+            exact_two, scale_two, keys_out, values_out,
+        ) = outs
+        weight_buf, cross_buf, rows_buf, keys, values, sems = scratch
+        part = self.mem_local // 4
+        schedule = {}
+
+        def at(tick, job):
+            schedule.setdefault(tick, []).append(job)
+
+        def vector(index):
+            return vectors_ref[...].astype(F32)[index : index + 1]
+
+        def fetch_weight(unit, slot):
+            return pltpu.make_async_copy(whole_refs[unit], weight_buf.at[slot], sems.at[slot])
+
+        def fetch_cross(unit):
+            return pltpu.make_async_copy(whole_refs[unit], cross_buf.at[unit], sems.at[2 + unit])
+
+        def fetch_rows(which, chunk):
+            slot = chunk % 2
+            return pltpu.make_async_copy(
+                items_ref.at[which, :, pl.ds(chunk * part, part)], rows_buf.at[slot], sems.at[4 + slot]
+            )
+
+        def store(which, value):
+            source, target = ((keys, keys_out), (values, values_out))[value]
+            return pltpu.make_async_copy(source.at[which], target.at[which], sems.at[6 + 2 * which + value])
+
+        self.pending = []
+
+        def project(slot, unit, result, shift, scale):
+            def job():
+                fetch_weight(unit, slot).wait()
+                total = product(tokens_ref[...], weight_buf[slot])
+                if shift is not None:
+                    total = total + vector(shift)
+                if scale is not None:
+                    total = total * scale
+                result[...] = total.astype(BF16)
+
+            return job
+
+        def self_attend(which):
+            def job():
+                limit = limits_ref[0:1, which : which + 1]
+                slot = lax.broadcasted_iota(jnp.int32, (2 * DEC, DEC), 1)
+                query = lax.broadcasted_iota(jnp.int32, (2 * DEC, DEC), 0) % DEC
+                allowed = (slot <= query) & (slot < limit)
+                rows = pl.ds(which * DEC, DEC)
+
+                def pair(p, _):
+                    cols = pl.ds(pl.multiple_of(p * PAIR, PAIR), PAIR)
+                    exact, scale = attend_pair(
+                        q_one[rows, cols], lambda _: k_one[rows, cols], lambda _: v_one[rows, cols], lambda _: allowed, 1
+                    )
+                    mixed_one[rows, cols] = exact.astype(BF16)
+                    exact_one[rows, cols] = exact
+                    scale_one[rows, cols] = scale
+                    return 0
+
+                lax.fori_loop(0, PAIRS, pair, 0)
+
+            return job
+
+        def first_norm(slot, unit):
+            def job():
+                fetch_weight(unit, slot).wait()
+                resid = tokens_ref[...].astype(F32) + product(mixed_one[...], weight_buf[slot]) + vector(2)
+                hidden, normed, inverse = norm_forward(resid, vector(10), vector(7))
+                hidden_one[...] = hidden
+                normed_one[...] = normed
+                inverse_one[...] = inverse
+
+            return job
+
+        def cross_query(slot, unit):
+            def job():
+                fetch_weight(unit, slot).wait()
+                total = (product(hidden_one[...].astype(BF16), weight_buf[slot]) + vector(3)) * 0.125
+                q_two[...] = total.astype(BF16)
+
+            return job
+
+        def project_rows(which, chunk):
+            def job():
+                fetch_rows(which, chunk).wait()
+                rows = rows_buf[chunk % 2].reshape(members * part, D)
+                new_keys = product(rows, cross_buf[0]).astype(BF16).reshape(members, part, D)
+                new_values = (product(rows, cross_buf[1]) + vector(4)).astype(BF16).reshape(members, part, D)
+                keys[which, :, pl.ds(chunk * part, part)] = new_keys
+                values[which, :, pl.ds(chunk * part, part)] = new_values
+                if chunk == 3:
+                    store(which, 0).start()
+                    store(which, 1).start()
+
+            return job
+
+        def cross_attend(which, low, high):
+            def job():
+                rows = pl.ds(which * DEC, DEC)
+                limit = limits_ref[1:2, which : which + 1]
+                slot = lax.broadcasted_iota(jnp.int32, (2 * DEC, self.mem_local), 1)
+
+                def allowed(step):
+                    return slot < limit - lax.rem(member - step + members, members) * self.mem_local
+
+                def pair(p, _):
+                    cols = pl.ds(pl.multiple_of(p * PAIR, PAIR), PAIR)
+                    exact, scale = attend_pair(
+                        q_two[rows, cols],
+                        lambda step: keys[which, step, :, cols],
+                        lambda step: values[which, step, :, cols],
+                        allowed,
+                        members,
+                    )
+                    mixed_two[rows, cols] = exact.astype(BF16)
+                    exact_two[rows, cols] = exact
+                    scale_two[rows, cols] = scale
+                    return 0
+
+                lax.fori_loop(low, high, pair, 0)
+
+            return job
+
+        for unit in range(2):
+            at(unit + done_lag, fetch_cross(unit).start)
+        for unit in range(2, 7):
+            at(unit + done_lag, fetch_weight(unit, unit % 2).start)
+        at(1 + done_lag + 1, fetch_cross(0).wait)
+        at(1 + done_lag + 1, fetch_cross(1).wait)
+        start = 2 + done_lag + 1
+        at(start, project(0, 2, q_one, 0, 0.125))
+        at(start + 1, project(1, 3, k_one, None, None))
+        at(start + 2, project(0, 4, v_one, 1, None))
+        at(start + 2, self_attend(0))
+        at(start + 3, self_attend(1))
+        at(start + 3, first_norm(1, 5))
+        at(start + 4, cross_query(0, 6))
+        previous = 1 + done_lag
+        per_item = len(due) // items_here
+        for which in range(items_here):
+            for chunk in range(4):
+                ready = due[which * per_item + (chunk + 1) * per_item // 4 - 1] + 2
+                begin = max(ready, previous)
+                at(begin, fetch_rows(which, chunk).start)
+                late = begin if which == items_here - 1 and chunk == 3 else begin + 1
+                at(late, project_rows(which, chunk))
+                previous = begin + 1
+            begin = max(previous, start + 5)
+            if which < items_here - 1:
+                for quarter in range(4):
+                    at(begin + quarter, cross_attend(which, 2 * quarter, 2 * quarter + 2))
+            else:
+                at(late, cross_attend(which, 0, PAIRS))
+        self.pending = [store(which, value) for which in range(items_here) for value in range(2)]
+        return schedule
+
+    def finish(self):
+        for copy in self.pending:
+            copy.wait()
+
+
+def gather_by_kernel(shards, memory, vector, tokens, limits, items_count, members):
     items_here = memory.shape[0] // members
     units = []
     for weight, shard in enumerate(shards):
@@ -266,6 +498,7 @@
         depth = height * 256 // max(height * width // 128, 256)
         for start in range(0, height, depth):
             units.append((weight, start, depth, height))
+    forward = Forward(tokens.shape[0], items_here, members, memory.shape[1])
     pieces = memory.shape[1] // 32 * items_here
     hops = members - 1
     kinds = 2 * hops + 8
@@ -274,11 +507,13 @@
         jax.ShapeDtypeStruct((items_here, members, memory.shape[1], memory.shape[2]), memory.dtype)
     )
     out_shape.append(jax.ShapeDtypeStruct((vector.shape[0], vector.shape[1] * items_count), vector.dtype))
+    gathered = len(out_shape)
+    out_shape += forward.out_shapes()
     outs = pl.pallas_call(
-        functools.partial(gather_kernel, members, items_here, tuple(units)),
+        functools.partial(gather_kernel, members, items_here, tuple(units), forward),
         out_shape=out_shape,
-        in_specs=[VMEM] * len(shards) + [ANY, VMEM],
-        out_specs=[ANY] * len(out_shape),
+        in_specs=[VMEM] * len(shards) + [ANY, VMEM, VMEM, VMEM],
+        out_specs=[ANY] * (gathered - 1) + [VMEM] + forward.out_specs(),
         scratch_shapes=[
             pltpu.SemaphoreType.DMA((len(units), kinds)),
             pltpu.SemaphoreType.DMA((len(units), kinds)),
@@ -289,11 +524,14 @@
             pltpu.SemaphoreType.DMA((items_count,)),
             pltpu.SemaphoreType.DMA((items_count,)),
             pltpu.VMEM((items_here,) + memory.shape[1:], memory.dtype),
-        ],
-        compiler_params=pltpu.CompilerParams(collective_id=0, has_side_effects=True),
+        ]
+        + forward.scratch(),
+        compiler_params=pltpu.CompilerParams(
+            collective_id=0, has_side_effects=True, vmem_limit_bytes=60 * 1024 * 1024
+        ),
         name="gather_all",
-    )(*shards, memory, vector)
-    return outs[:-2], outs[-2], outs[-1]
+    )(*shards, memory, vector, tokens, limits)
+    return outs[: gathered - 2], outs[gathered - 2], outs[gathered - 1], outs[gathered:]
 
 
 def gather_by_collectives(shards, memory, vector, items_count, members):
@@ -818,15 +1056,21 @@
     group_items = memory.shape[0]
     mem_local = memory.shape[1]
     shards = (
-        self_query, self_key, self_value, self_out, cross_query, cross_key, cross_value, cross_out, feed_in, feed_out,
+        cross_key, cross_value, self_query, self_key, self_value, self_out, cross_query, cross_out, feed_in, feed_out,
     )
     by_kernel = (items_count, members) == (8, 4)
     shift_width, bias_rows = shifts.shape[1], inner_bias.shape[0] // shifts.shape[1]
     vector = jnp.concatenate([shifts, gains, inner_bias.reshape(bias_rows, shift_width)], 0)
-    gather = gather_by_kernel if by_kernel else gather_by_collectives
-    whole, item_memory, vectors = gather(shards, memory, vector, items_count, members)
+    own_dec = lax.dynamic_slice_in_dim(dec_len, member * item_count, item_count)
+    own_mem = lax.dynamic_slice_in_dim(mem_len, member * item_count, item_count)
+    if by_kernel:
+        whole, item_memory, vectors, forward = gather_by_kernel(
+            shards, memory, vector, tokens, jnp.stack([own_dec, own_mem]), items_count, members
+        )
+    else:
+        whole, item_memory, vectors = gather_by_collectives(shards, memory, vector, items_count, members)
     (
-        query_self, key_self, value_self, output_self, query_cross, key_cross, value_cross, output_cross,
+        key_cross, value_cross, query_self, key_self, value_self, output_self, query_cross, output_cross,
         feed_up, feed_down,
     ) = whole
     memory_flat = item_memory.reshape(-1, D)
@@ -838,26 +1082,32 @@
         vectors[bias_start:].reshape(bias_rows, items_count, shift_width).transpose(1, 0, 2).reshape(-1)
     )
 
-    own_dec = lax.dynamic_slice_in_dim(dec_len, member * item_count, item_count)
-    own_mem = lax.dynamic_slice_in_dim(mem_len, member * item_count, item_count)
     bases = lax.rem(member - jnp.arange(members, dtype=jnp.int32) + members, members) * mem_local
 
-    tokens_float = tokens.astype(F32)
-    queries_one = ((product(tokens, query_self) + shift_rows[0]) * 0.125).astype(BF16)
-    keys_one = product(tokens, key_self).astype(BF16)
-    values_one = (product(tokens, value_self) + shift_rows[1]).astype(BF16)
-    mixed_one, exact_one, scale_one = attend_forward(
-        True, DEC, own_dec, bases, queries_one, keys_one, values_one
-    )
-    resid_one = tokens_float + product(mixed_one, output_self) + shift_rows[2]
-    hidden_one, normed_one, inverse_one = norm_forward(resid_one, gain_rows[0], shift_rows[7])
-    hidden_one_low = hidden_one.astype(BF16)
-    queries_two = ((product(hidden_one_low, query_cross) + shift_rows[3]) * 0.125).astype(BF16)
-    keys_two = product(memory_flat, key_cross).astype(BF16)
-    values_two = (product(memory_flat, value_cross) + shift_rows[4]).astype(BF16)
-    mixed_two, exact_two, scale_two = attend_forward(
-        False, mem_local, own_mem, bases, queries_two, keys_two, values_two
-    )
+    if by_kernel:
+        (
+            queries_one, keys_one, values_one, mixed_one, exact_one, scale_one, hidden_one, normed_one, inverse_one,
+            queries_two, mixed_two, exact_two, scale_two, keys_two, values_two,
+        ) = forward
+        hidden_one_low = hidden_one.astype(BF16)
+        keys_two, values_two = keys_two.reshape(-1, D), values_two.reshape(-1, D)
+    else:
+        tokens_float = tokens.astype(F32)
+        queries_one = ((product(tokens, query_self) + shift_rows[0]) * 0.125).astype(BF16)
+        keys_one = product(tokens, key_self).astype(BF16)
+        values_one = (product(tokens, value_self) + shift_rows[1]).astype(BF16)
+        mixed_one, exact_one, scale_one = attend_forward(
+            True, DEC, own_dec, bases, queries_one, keys_one, values_one
+        )
+        resid_one = tokens_float + product(mixed_one, output_self) + shift_rows[2]
+        hidden_one, normed_one, inverse_one = norm_forward(resid_one, gain_rows[0], shift_rows[7])
+        hidden_one_low = hidden_one.astype(BF16)
+        queries_two = ((product(hidden_one_low, query_cross) + shift_rows[3]) * 0.125).astype(BF16)
+        keys_two = product(memory_flat, key_cross).astype(BF16)
+        values_two = (product(memory_flat, value_cross) + shift_rows[4]).astype(BF16)
+        mixed_two, exact_two, scale_two = attend_forward(
+            False, mem_local, own_mem, bases, queries_two, keys_two, values_two
+        )
     resid_two = hidden_one + product(mixed_two, output_cross) + shift_rows[5]
     hidden_two, normed_two, inverse_two = norm_forward(resid_two, gain_rows[1], shift_rows[8])
     hidden_two_low = hidden_two.astype(BF16)

time: 549 us -> 508 us (0.925)
  matrix products: 68.8 us -> 44.1 us
  Pallas kernels: 417 us -> 400 us
    pallas_call x4 -> x2, Pallas kernels: 66.5 us -> 38.4 us  [attention_call(): pl.pallas_call(functools.partial(kernel, causal, chunk), grid_spec=pltpu....]
    dot_general x10 -> x3, matrix products: 35.5 us -> 10.9 us  [product(): return jnp.dot(first_op, second_op, preferred_element_type=F32)]
    pallas_call x1, Pallas kernels: 168 us -> 177 us  [gather_by_kernel(): pl.pallas_call(functools.partial(gather_kernel, members, items_here, tupl...]
  transfers between devices with their start and end apart: 1 -> 1, of which waited for: 0 -> 0; matrix products, arithmetic and copies ran while one was open for 5% -> 6% of each run, Pallas kernels for 34% -> 37%
where the time goes in v3:
time: 508 us; the launch traced here: 502 us
  Pallas kernels  400 us (79%)
  matrix products  44.1 us (9%)
  other arithmetic  23.9 us (5%)
  local copies, waits for them, and re-layouts  19.3 us (4%)
  between operations  14.9 us (3%)
    pallas_call x1, Pallas kernels, scatter_by_kernel(): pl.pallas_call(functools.partial(scatter_kernel, members, tuple(units), b...  184 us
    pallas_call x1, Pallas kernels, gather_by_kernel(): pl.pallas_call(functools.partial(gather_kernel, members, items_here, tupl...  177 us
    pallas_call x2, Pallas kernels, attention_call(): pl.pallas_call(functools.partial(kernel, causal, chunk), grid_spec=pltpu....  38.4 us
    dot_general x10, matrix products, right_product(): lax.dot_general(first_op, second_op, (((1,), (1,)), ((), ())), preferred_...  33.2 us
    dot_general x3, matrix products, product(): return jnp.dot(first_op, second_op, preferred_element_type=F32)  10.9 us
  transfers between devices with their start and end apart: 1, of which 0 were waited for; matrix products, arithmetic and copies ran while one was open for 6% of the time, Pallas kernels for 37%

profile of v3, /device:TPU:0, one launch (start us, length us, event | category | flops | bytes accessed | tf_op | source)
XLA Modules:
  0.0 502.2 jit_solution(987510216706462513)
XLA Ops:
  7.8 0.7 dynamic-slice_bitcast_fusion.1
  8.5 1.2 dynamic_slice.16.lens_ref
  9.7 0.7 dynamic-slice_bitcast_fusion
  10.4 1.2 dynamic_slice.15.lens_ref
  12.2 1.3 pad_maximum_fusion.refs_11_
  13.6 177.2 %gather_all.1 = (bf16[1024,1024]{1,0:T(8,128)(2,1)}, bf16[1024,1024]{1,0:T(8,128)(2,1)}, bf16[1024,1024]{1,0:T(8,128)(2,1)}, bf16[1024,1024]{1,0:T(8,128)(2,1)},...) custom-call(bf16[128,256]{1,0:T(8,128)(2,1)} %refs_0_.1, ...), custom_call_target="tpu_custom_call" | custom-call | tf_op jit(solution)/shard_map/gather_all/pallas_call | solution.py:512
  190.8 0.8 slice.68
  191.6 0.9 fusion.21
  192.5 2.8 fusion.22
  195.9 5.6 %multiply_convert_fusion = (bf16[256,4096]{1,0:T(8,128)(2,1)S(1)}, f32[256,4096]{1,0:T(8,128)S(1)}) fusion(f32[4096]{0:T(1024)S(1)} %bitcast.71, bf16[256,1024]{1,0:T(8,128)(2,1)S(1)} %fusion.14.refs_1_, bf16[1024,4096]{1,0:T(8,128)(2,1)} %get-tuple-element.64), kind=kOutput, calls=%fused_computation.11 | convolution fusion | flops 2153775104 | bytes 15220736 | tf_op jit(solution)/shard_map/dot_general | solution.py:27
  201.7 2.5 fusion.23
  205.1 1.4 convert_reduce_fusion.3
  206.6 6.8 %convert_reduce_fusion.1 = (f32[4096]{0:T(1024)S(1)}, bf16[256,4096]{1,0:T(8,128)(2,1)S(1)}) fusion(f32[256,4096]{1,0:T(8,128)S(1)} %get-tuple-element.134, bf16[256,1024]{1,0:T(8,128)(2,1)S(1)} %get-tuple-element.117.refs_7_, bf16[4096,1024]{1,0:T(8,128)(2,1)} %get-tuple-element.65), kind=kOutput, calls=%fused_computation.10 | convolution fusion | flops 2160062464 | bytes 15220736 | tf_op jit(solution)/shard_map/dot_general | solution.py:37
  213.4 2.9 multiply_reduce_fusion
  216.8 1.7 fusion.24.grad_ref
  218.5 25.0 %cross_attention.1 = (bf16[256,1024]{1,0:T(8,128)(2,1)}, bf16[2048,1024]{1,0:T(8,128)(2,1)}, bf16[2048,1024]{1,0:T(8,128)(2,1)}) custom-call(s32[2]{0:T(128)} %dynamic_slice.16.lens_ref, s32[4]{0:T(128)} %fusion.16.bases_ref, bf16[256,1024]{1,0:T(8,128)(2,1)} %get-tuple-element.67.q_ref, bf16[2048,1024]{1,0:T(8,128)(2,1)} %bitcast.78, ...), custom_call_target="tpu_custom_call" | custom-call | flops 4294967296 | bytes 16777216 | tf_op jit(solution)/shard_map/cross_attention/pallas_call | solution.py:631
  243.5 1.3 convert_reduce_fusion.5
  244.8 2.9 multiply_reduce_fusion.1
  247.7 0.7 convert_reduce_fusion
  248.8 0.8 copy-done.8
  249.6 3.3 fusion.25.grad_ref
  252.9 13.4 %self_attention.1 = (bf16[256,1024]{1,0:T(8,128)(2,1)}, bf16[256,1024]{1,0:T(8,128)(2,1)}, bf16[256,1024]{1,0:T(8,128)(2,1)}) custom-call(s32[2]{0:T(128)} %dynamic_slice.15.lens_ref, s32[4]{0:T(128)} %fusion.16.bases_ref, bf16[256,1024]{1,0:T(8,128)(2,1)} %get-tuple-element.75.q_ref, bf16[256,1024]{1,0:T(8,128)(2,1)} %get-tuple-element.76.k_ref, ...), custom_call_target="tpu_custom_call" | custom-call | flops 536870912 | bytes 2097152 | tf_op jit(solution)/shard_map/self_attention/pallas_call | solution.py:631
  266.4 1.2 convert_reduce_fusion.8
  267.6 1.1 convert_reduce_fusion.7
  269.6 2.3 convert_element_type.71.refs_4_
  271.8 0.8 broadcast_multiply_fusion.1.refs_12_
  272.7 0.8 broadcast_multiply_fusion.refs_14_
  273.5 1.8 convolution_add_fusion.3
  275.3 4.6 fusion.26
  280.0 6.7 %add_convert_fusion = bf16[2048,1024]{1,0:T(8,128)(2,1)} fusion(f32[2048,1024]{1,0:T(8,128)S(1)} %fusion.26, bf16[2048,1024]{1,0:T(8,128)(2,1)S(1)} %copy-done.1, bf16[1024,1024]{1,0:T(8,128)(2,1)S(1)} %copy-done.32), kind=kOutput, calls=%fused_computation.1 | convolution fusion | flops 4299161600 | bytes 18874368 | tf_op jit(solution)/shard_map/dot_general | solution.py:37
  286.6 184.2 %scatter_all.1 = (f32[512,256]{1,0:T(8,128)}, f32[128,1024]{1,0:T(8,128)}, f32[128,256]{1,0:T(8,128)}, f32[128,256]{1,0:T(8,128)}, f32[128,256]{1,0:T(8,128)}, /...) custom-call(bf16[256,4096]{1,0:T(8,128)(2,1)} %copy-done.15, ...), custom_call_target="tpu_custom_call" | custom-call | tf_op jit(solution)/shard_map/scatter_all/pallas_call | solution.py:985
  470.9 6.8 %convert_element_type.73 = f32[8,256,1024]{2,1,0:T(8,128)} convert(bf16[8,256,1024]{2,1,0:T(8,128)(2,1)} %get-tuple-element.93) | non-fusion elementwise | flops 2097152 | bytes 12582912 | tf_op jit(solution)/shard_map/convert_element_type | solution.py:1185
  477.7 0.7 convolution_add_fusion.2
  478.8 0.7 copy-done.12
  479.5 1.7 convolution_add_fusion.1
  481.3 2.8 convert_dynamic-update-slice_fusion
  484.1 0.7 slice.75
  484.8 0.8 slice.74
  486.8 0.7 slice_bitcast_fusion.1
  488.2 0.7 copy.60
  488.8 0.7 copy.61
  489.5 0.7 copy.62
  490.2 0.7 copy.63
  490.8 0.7 copy.64
  491.5 0.7 copy.65
  492.1 0.7 copy.66
  493.5 0.8 copy.68
  494.2 0.8 copy.69
  (117 shorter events, 7.1 us)
Async XLA Ops:
  7.2 476.9 %all-reduce.2.cloned.1.call-start = ((), (), s32[]{:S(2)}) async-start(), calls=%async_computation | async-start | bytes 139264 | tf_op jit(solution)/shard_map/psum | solution.py:1211
  195.6 5.9 %slice-start.2 = ((s8[8388608]{0:T(1024)(128)(4,1)}), s8[4194304]{0:T(1024)(128)(4,1)S(1)}, s32[]{:S(2)}) async-start(s8[8388608]{0:T(1024)(128)(4,1)} %bitcast.76), calls=%async_computation.3 | async-start | bytes 8388608
  195.9 5.6 %copy-start.18 = (bf16[256,1024]{1,0:T(8,128)(2,1)}, bf16[256,1024]{1,0:T(8,128)(2,1)S(1)}, u32[]{:S(2)}) copy-start(bf16[256,1024]{1,0:T(8,128)(2,1)S(1)} %fusion.14.refs_1_) | copy-start | bytes 1572868
  195.9 5.9 %slice-start.3 = ((s8[8388608]{0:T(1024)(128)(4,1)}), s8[4194304]{0:T(1024)(128)(4,1)S(1)}, s32[]{:S(2)}) async-start(s8[8388608]{0:T(1024)(128)(4,1)} %bitcast.76), calls=%async_computation.4 | async-start | bytes 8388608
  201.5 2.8 copy-start.15
  201.7 2.8 copy-start.14
  205.1 8.2 %slice-start = ((s8[8388608]{0:T(1024)(128)(4,1)}), s8[4194304]{0:T(1024)(128)(4,1)S(1)}, s32[]{:S(2)}) async-start(s8[8388608]{0:T(1024)(128)(4,1)} %bitcast.74), calls=%async_computation.1 | async-start | bytes 8388608
  206.6 6.8 %copy-start.19 = (bf16[256,1024]{1,0:T(8,128)(2,1)}, bf16[256,1024]{1,0:T(8,128)(2,1)S(1)}, u32[]{:S(2)}) copy-start(bf16[256,1024]{1,0:T(8,128)(2,1)S(1)} %get-tuple-element.117.refs_7_) | copy-start | bytes 1572868
  206.6 6.8 %slice-start.1 = ((s8[8388608]{0:T(1024)(128)(4,1)}), s8[4194304]{0:T(1024)(128)(4,1)S(1)}, s32[]{:S(2)}) async-start(s8[8388608]{0:T(1024)(128)(4,1)} %bitcast.74), calls=%async_computation.2 | async-start | bytes 8388608
  213.3 3.0 copy-start.16
  213.4 3.4 copy-start.3
  216.7 1.7 copy-start.7
  218.5 26.3 %copy-start.2 = (f32[256,1024]{1,0:T(8,128)S(1)}, f32[256,1024]{1,0:T(8,128)}, u32[]{:S(2)}) copy-start(f32[256,1024]{1,0:T(8,128)} %get-tuple-element.74) | copy-start | bytes 3145732
  243.5 4.2 copy-start
  244.8 3.6 copy-start.22
  248.8 0.8 copy-start.8
  252.9 18.9 %copy-start.4 = (bf16[256,1024]{1,0:T(8,128)(2,1)S(1)}, bf16[256,1024]{1,0:T(8,128)(2,1)}, u32[]{:S(2)}) copy-start(bf16[256,1024]{1,0:T(8,128)(2,1)} %get-tuple-element.72) | copy-start | bytes 1572868
  266.4 6.3 %copy-start.5 = (bf16[256,1024]{1,0:T(8,128)(2,1)S(1)}, bf16[256,1024]{1,0:T(8,128)(2,1)}, u32[]{:S(2)}) copy-start(bf16[256,1024]{1,0:T(8,128)(2,1)} %get-tuple-element.81) | copy-start | bytes 1572868
  268.9 0.6 copy-start.31
  269.6 4.0 copy-start.11
  271.8 3.5 copy-start.10
  271.8 3.5 copy-start.33
  275.3 4.6 copy-start.1
  275.3 4.6 copy-start.32
  470.9 6.8 %copy-start.9 = (f32[256,1024]{1,0:T(8,128)S(1)}, f32[256,1024]{1,0:T(8,128)}, u32[]{:S(2)}) copy-start(f32[256,1024]{1,0:T(8,128)} %convolution_add_fusion.3) | copy-start | bytes 3145732
  470.9 6.8 %copy-start.13 = (bf16[1024,1024]{1,0:T(8,128)(2,1)S(1)}, bf16[1024,1024]{1,0:T(8,128)(2,1)}, u32[]{:S(2)}) copy-start(bf16[1024,1024]{1,0:T(8,128)(2,1)} %get-tuple-element.84) | copy-start | bytes 6291460
  470.9 6.8 %copy-start.17 = (bf16[256,1024]{1,0:T(8,128)(2,1)S(1)}, bf16[256,1024]{1,0:T(8,128)(2,1)}, u32[]{:S(2)}) copy-start(bf16[256,1024]{1,0:T(8,128)(2,1)} %get-tuple-element.83.refs_15_) | copy-start | bytes 1572868
  477.7 1.0 copy-start.6
  477.7 1.8 copy-start.12
  478.5 9.7 %copy-start.30 = (f32[128,256]{1,0:T(8,128)S(1)}, f32[128,256]{1,0:T(8,128)}, u32[]{:S(2)}) copy-start(f32[128,256]{1,0:T(8,128)} %get-tuple-element.162) | copy-start | bytes 393220
  479.5 9.4 %copy-start.29 = (f32[128,256]{1,0:T(8,128)S(1)}, f32[128,256]{1,0:T(8,128)}, u32[]{:S(2)}) copy-start(f32[128,256]{1,0:T(8,128)} %get-tuple-element.163) | copy-start | bytes 393220
  479.5 10.0 %copy-start.28 = (f32[128,256]{1,0:T(8,128)S(1)}, f32[128,256]{1,0:T(8,128)}, u32[]{:S(2)}) copy-start(f32[128,256]{1,0:T(8,128)} %get-tuple-element.164) | copy-start | bytes 393220
  479.5 10.7 %copy-start.27 = (f32[128,256]{1,0:T(8,128)S(1)}, f32[128,256]{1,0:T(8,128)}, u32[]{:S(2)}) copy-start(f32[128,256]{1,0:T(8,128)} %get-tuple-element.165) | copy-start | bytes 393220
  479.5 11.3 %copy-start.26 = (f32[128,256]{1,0:T(8,128)S(1)}, f32[128,256]{1,0:T(8,128)}, u32[]{:S(2)}) copy-start(f32[128,256]{1,0:T(8,128)} %get-tuple-element.166) | copy-start | bytes 393220
  479.5 12.0 %copy-start.25 = (f32[128,256]{1,0:T(8,128)S(1)}, f32[128,256]{1,0:T(8,128)}, u32[]{:S(2)}) copy-start(f32[128,256]{1,0:T(8,128)} %get-tuple-element.167) | copy-start | bytes 393220
  479.5 12.6 %copy-start.24 = (f32[128,256]{1,0:T(8,128)S(1)}, f32[128,256]{1,0:T(8,128)}, u32[]{:S(2)}) copy-start(f32[128,256]{1,0:T(8,128)} %get-tuple-element.168) | copy-start | bytes 393220
  479.5 13.3 %copy-start.23 = (f32[128,256]{1,0:T(8,128)S(1)}, f32[128,256]{1,0:T(8,128)}, u32[]{:S(2)}) copy-start(f32[128,256]{1,0:T(8,128)} %get-tuple-element.169) | copy-start | bytes 393220
  479.5 13.9 %copy-start.21 = (f32[128,1024]{1,0:T(8,128)S(1)}, f32[128,1024]{1,0:T(8,128)}, u32[]{:S(2)}) copy-start(f32[128,1024]{1,0:T(8,128)} %get-tuple-element.170) | copy-start | bytes 1572868
  481.3 13.0 %copy-start.20 = (f32[512,256]{1,0:T(8,128)S(1)}, f32[512,256]{1,0:T(8,128)}, u32[]{:S(2)}) copy-start(f32[512,256]{1,0:T(8,128)} %get-tuple-element.171) | copy-start | bytes 1572868
Sparse Core Ops, SparseCore 0:
  269.7 125.1 all-reduce.1

commit v4 on v3

--- a/solution.py
+++ b/solution.py
@@ -18,7 +18,7 @@
 MESH = pl.DeviceIdType.MESH
 F32 = jnp.float32
 BF16 = jnp.bfloat16
-Z_LAG, X_LAG, FIRST_PIECE, SPREAD = 1, 1, 3, 17
+X_LAG, FIRST_PIECE, SPREAD, STRAIGHT = 1, 2, 16, 3
 ANY = pl.BlockSpec(memory_space=pl.ANY)
 VMEM = pl.BlockSpec(memory_space=pltpu.VMEM)
 
@@ -116,6 +116,23 @@
             unit, (UP if upward else DOWN) + hop, shard(unit) if hop == 0 else piece, piece, (row, target)
         )
 
+    straight = range(STRAIGHT)
+
+    def straight_copy(unit, hop, upward):
+        target = jnp.clip(member + hop + 1 if upward else member - hop - 1, 0, members - 1)
+        piece = whole_refs[units[unit][0]].at[place(unit, row), cols(unit, member)]
+        return remote(unit, (UP if upward else DOWN) + hop, shard(unit), piece, (row, target))
+
+    def straight_each(unit, act):
+        for hop in range(hops):
+            @pl.when(member + hop + 1 <= members - 1)
+            def _():
+                act(straight_copy(unit, hop, True))
+
+            @pl.when(member - hop - 1 >= 0)
+            def _():
+                act(straight_copy(unit, hop, False))
+
     def along_start(unit, hop):
         @pl.when((member >= hop) & (member < members - 1))
         def _():
@@ -208,34 +225,38 @@
         copy.start()
 
     due = [FIRST_PIECE + piece * SPREAD // pieces for piece in range(pieces)]
-    done_lag = Z_LAG * hops + 2 * X_LAG + 1
+    plane_lag = 1
+    done_lag = plane_lag + 2 * X_LAG + 1
     jobs = forward.jobs(
         members, items_here, member, tokens_ref, limits_ref, whole_refs, items_ref, vectors_ref, outs, refs[9:],
         done_lag, due,
     )
     last = max([count - 1 + done_lag, due[-1] + 2] + list(jobs))
     for tick in range(last + 1):
-        unit = tick
-        if unit < count:
-            along_start(unit, 0)
-            own_copy(unit).start()
+        if tick in straight:
+            straight_each(tick, lambda copy: copy.start())
+            own_copy(tick).start()
+        for hop in range(hops):
+            unit = tick + hops - plane_lag - hop
+            if unit not in straight and 0 <= unit < count:
+                if hop == 0:
+                    own_copy(unit).start()
+                else:
+                    along_arrive(unit, hop - 1)
+                along_start(unit, hop)
         for piece in range(pieces):
             if due[piece] == tick:
                 for step in range(1, members):
                     memory_send(piece, step).start()
-        for hop in range(1, hops):
-            unit = tick - Z_LAG * hop
-            if 0 <= unit < count:
-                along_arrive(unit, hop - 1)
-                along_start(unit, hop)
-        unit = tick - Z_LAG * hops
+        unit = tick - plane_lag
         if 0 <= unit < count:
-            along_arrive(unit, hops - 1)
+            for hop in range(hops) if unit in straight else (hops - 1,):
+                along_arrive(unit, hop)
             own_copy(unit).wait()
             to_x(unit).start()
             to_y(unit).start()
             to_core(unit, 0).start()
-        unit = tick - Z_LAG * hops - X_LAG
+        unit = tick - plane_lag - X_LAG
         if 0 <= unit < count:
             to_x(unit).wait_recv()
             half_a(unit).start()
@@ -243,7 +264,7 @@
             to_y(unit).wait_recv()
             half_b(unit).start()
             to_core(unit, 2).start()
-        unit = tick - Z_LAG * hops - 2 * X_LAG
+        unit = tick - plane_lag - 2 * X_LAG
         if 0 <= unit < count:
             half_a(unit).wait_recv()
             half_b(unit).wait_recv()
@@ -266,8 +287,11 @@
         for job in jobs.get(tick, ()):
             job()
     for unit in range(count):
-        for hop in range(hops):
-            along_sent(unit, hop)
+        if unit in straight:
+            straight_each(unit, lambda copy: copy.wait_send())
+        else:
+            for hop in range(hops):
+                along_sent(unit, hop)
         to_x(unit).wait_send()
         to_y(unit).wait_send()
         half_a(unit).wait_send()
@@ -297,7 +321,7 @@
 
 
 class Forward:
-    outs = 15
+    outs = 16
 
     def __init__(self, rows, items_here, members, mem_local):
         self.rows, self.items_here, self.members, self.mem_local = rows, items_here, members, mem_local
@@ -307,10 +331,10 @@
         wide, low = jax.ShapeDtypeStruct((self.rows, D), F32), jax.ShapeDtypeStruct((self.rows, D), BF16)
         keys = jax.ShapeDtypeStruct((self.items_here, self.members, self.mem_local, D), BF16)
         inverse = jax.ShapeDtypeStruct((self.rows, 1), F32)
-        return [low, low, low, low, wide, wide, wide, wide, inverse, low, low, wide, wide, keys, keys]
+        return [low, low, low, low, wide, wide, wide, low, wide, inverse, low, low, wide, wide, keys, keys]
 
     def out_specs(self):
-        return [VMEM] * 13 + [ANY] * 2
+        return [VMEM] * 14 + [ANY] * 2
 
     def scratch(self):
         return [
@@ -327,8 +351,8 @@
         done_lag, due,
     ):
         (
-            q_one, k_one, v_one, mixed_one, exact_one, scale_one, hidden_one, normed_one, inverse_one, q_two, mixed_two,
-            exact_two, scale_two, keys_out, values_out,
+            q_one, k_one, v_one, mixed_one, exact_one, scale_one, hidden_one, hidden_low, normed_one, inverse_one, q_two,
+            mixed_two, exact_two, scale_two, keys_out, values_out,
         ) = outs
         weight_buf, cross_buf, rows_buf, keys, values, sems = scratch
         part = self.mem_local // 4
@@ -398,6 +422,7 @@
                 resid = tokens_ref[...].astype(F32) + product(mixed_one[...], weight_buf[slot]) + vector(2)
                 hidden, normed, inverse = norm_forward(resid, vector(10), vector(7))
                 hidden_one[...] = hidden
+                hidden_low[...] = hidden.astype(BF16)
                 normed_one[...] = normed
                 inverse_one[...] = inverse
 
@@ -406,7 +431,7 @@
         def cross_query(slot, unit):
             def job():
                 fetch_weight(unit, slot).wait()
-                total = (product(hidden_one[...].astype(BF16), weight_buf[slot]) + vector(3)) * 0.125
+                total = (product(hidden_low[...], weight_buf[slot]) + vector(3)) * 0.125
                 q_two[...] = total.astype(BF16)
 
             return job
@@ -719,34 +744,133 @@
         reduce_columns(partial[:, k * width : (k + 1) * width], member, members) for k in range(len(grads))
     ]
 
-RING, KEPT, ROUND = 4, 6, 8
-S_LAG = 2
-
-
-def scatter_kernel(members, units, back_rows, *refs):
-    lefts = 1 + max(unit[0] for unit in units)
-    rights = 1 + max(unit[1] for unit in units)
-    outs = 1 + max(unit[2] for unit in units)
-    count = len(units)
-    left_refs, right_refs, part_ref = refs[:lefts], refs[lefts : lefts + rights], refs[lefts + rights]
-    refs = refs[lefts + rights + 1 :]
-    out_refs, back_ref = refs[:outs], refs[outs]
+RING, KEPT, ROUND, CORES = 4, 6, 10, 3
+BACK_PIECES, BACK_WEIGHT, DIRECT = 8, 4, 0
+S_LAG = 3
+
+
+def total_grads(weighted):
+    weighted = jnp.transpose(weighted)
+    return -jnp.concatenate(
+        [jnp.sum(weighted[:HEAD_DIM], 0, keepdims=True), jnp.sum(weighted[HEAD_DIM:], 0, keepdims=True)], 1
+    )
+
+
+def attend_back_chunk(q2, gn2, grad_total, keys, values, allowed):
+    exp_scores = jnp.where(allowed, jnp.exp(right_product(keys, q2)), 0.0)
+    grad_exp = right_product(values, gn2) + grad_total
+    grad_scores = (exp_scores * grad_exp).astype(BF16)
+    return product(grad_scores, q2), product(exp_scores.astype(BF16), gn2), left_product(grad_scores, keys)
+
+
+class Given:
     (
+        active, grad_down, hidden_two, slope, feed_down, feed_up, grad_three, normed_two, mixed_two, q_two, exact_two,
+        scale_two, tokens, mixed_one, hidden_one, normed_one, q_one, k_one, v_one, keys, values, memory, exact_one,
+        scale_one, output_cross, key_cross, value_cross, query_cross, output_self, query_self, key_self, value_self,
+    ) = range(32)
+    count = 32
+
+
+class Small:
+    inverse_one, inverse_two, gains, limits, vectors = range(5)
+    count = 5
+
+
+class Block:
+    fo, fi, co, ck, cv, cq, so, sq, sk, sv = range(10)
+    count = 10
+
+
+def scatter_kernel(members, items_here, mem_local, *refs):
+    big, refs = refs[: Given.count], refs[Given.count :]
+    small, refs = refs[: Small.count], refs[Small.count :]
+    out_refs, refs = refs[: Block.count], refs[Block.count :]
+    tokens_grad, vector_out, part_ref, back_ref = refs[:4]
+    (
+        wide, grad_down, hidden_two, mixed_two, grad_cross, q_two, tokens, mixed_one, hidden_one, normed_one,
+        grad_mixed, exact, scale, grad_numer_low, grad_total, key_buf, value_buf, gk_two, gv_two,
+        gq_two, weight_buf,
+        grad_self, stage, vector_sum, vector_in, vector_far,
         core_out, core_in, near_out, near_in, near_kept, far_out, far_in, own, hop_out, hop_in,
-        send_sem, recv_sem, back_send, back_recv, credit,
-    ) = refs[outs + 1 :]
+        send_sem, recv_sem, back_send, back_recv, credit, load_sem, kv_sem, stage_sem, vec_send, vec_recv,
+    ) = refs[4:]
+    gq_one, q_one, k_one, v_one = key_buf.at[0], key_buf.at[1], value_buf.at[0], value_buf.at[1]
+    gk_one, gv_one = stage.at[0], stage.at[1]
     row = lax.axis_index("items")
     member = lax.axis_index("mem")
     hops = members - 1
     core_peer = row ^ 1
+    slots = members * mem_local
+
+    loads = {}
+
+    def load(name, source, target):
+        loads[name] = pltpu.make_async_copy(source, target, load_sem.at[len(loads)])
+        loads[name].start()
+
+    def loaded(*names):
+        for name in names:
+            loads[name].wait()
+
+    def whole(name, target):
+        load(name, big[name], target)
+
+    def down_load(k):
+        load((Given.feed_down, k), big[Given.feed_down].at[pl.ds(k * D, D)], weight_buf.at[0])
+
+    def up_load(k):
+        load((Given.feed_up, k), big[Given.feed_up].at[:, pl.ds(k * D, D)], weight_buf.at[1])
+
+    def slope_load(k):
+        load((Given.slope, k), big[Given.slope].at[:, pl.ds(k * D, D)], (exact, scale)[k % 2])
+
+    whole(Given.grad_down, grad_down)
+    for k in range(4):
+        load((Given.active, k), big[Given.active].at[:, pl.ds(k * D, D)], wide.at[pl.ds(k * 256, 256)])
+    down_load(0)
+    slope_load(0)
+    up_load(0)
+    slope_load(1)
+    whole(Given.grad_three, tokens_grad)
+    whole(Given.normed_two, normed_one)
+    whole(Given.q_two, q_two)
+    whole(Given.hidden_two, hidden_two)
+    whole(Given.mixed_two, mixed_two)
+    whole(Given.hidden_one, hidden_one)
+    whole(Given.mixed_one, mixed_one)
+    whole(Given.tokens, tokens)
 
     barrier = pltpu.get_barrier_semaphore()
-    partners = [(core_peer, member), (row ^ 2, member), (row ^ 4, member)]
+    partners = [(row ^ distance, member) for distance in range(1, 8)]
     partners += [(row, lax.rem(member + step, members)) for step in range(1, members)]
     for partner in partners:
         pl.semaphore_signal(barrier, inc=1, device_id=partner, device_id_type=MESH)
     pl.semaphore_wait(barrier, len(partners))
 
+    units = [(Block.fo, k) for k in range(4)] + [(Block.fi, k) for k in range(4)]
+    units += [(name, 0) for name in range(Block.co, Block.count)]
+    count = len(units)
+    factors = {
+        Block.co: (mixed_two, grad_cross),
+        Block.ck: (wide, gk_two),
+        Block.cv: (wide, gv_two),
+        Block.cq: (hidden_one, gq_two),
+        Block.so: (mixed_one, grad_self),
+        Block.sq: (tokens, gq_one),
+        Block.sk: (tokens, gk_one),
+        Block.sv: (tokens, gv_one),
+    }
+    needs = {
+        0: (Given.grad_down,) + tuple((Given.active, k) for k in range(4)),
+        4: (Given.hidden_two,),
+        8: (Given.mixed_two,),
+        9: (Given.memory,),
+        11: (Given.hidden_one,),
+        12: (Given.mixed_one,),
+        13: (Given.tokens,),
+    }
+
     def bits(unit):
         return (2, 4) if unit % 2 == 0 else (4, 2)
 
@@ -754,33 +878,29 @@
         near, far = bits(unit)
         return (who ^ near, who ^ near ^ far, who ^ far, who)
 
+    def lanes(start, size):
+        return pl.ds(pl.multiple_of(start, 128), size)
+
     def partial(unit, owner):
-        left, right, _, left_start, left_step, right_start, right_step = units[unit]
-        left_ref, right_ref = left_refs[left], right_refs[right]
-        cols = pl.ds(pl.multiple_of(owner * left_step + left_start, 128), 128)
-        depth = left_ref.shape[0]
-        chunk = min(depth, 512)
-
-        def term(start):
-            rows = pl.ds(start, chunk)
-            if right_step == 256:
-                right_value = right_ref[rows, :]
-            else:
-                right_value = jnp.concatenate(
-                    [
-                        right_ref[rows, pl.ds(right_start + k * right_step, 256)]
-                        for k in range(members)
-                    ],
-                    1,
-                )
-            return left_product(left_ref[rows, cols], right_value)
-
-        total = term(0)
-        if depth > chunk:
-            total = lax.fori_loop(
-                1, depth // chunk, lambda k, sums: sums + term(pl.multiple_of(k * chunk, chunk)), total
+        name, k = units[unit]
+        if name == Block.fo:
+            left = wide[pl.ds(pl.multiple_of(owner // 2 * 256, 256), 256), lanes(owner % 2 * 512 + k * 128, 128)]
+            return left_product(left, grad_down[...])
+        if name == Block.fi:
+            right = jnp.concatenate(
+                [wide[pl.ds(D + part * 256, 256), pl.ds(k * 256, 256)] for part in range(members)], 1
             )
-        return total
+            return left_product(hidden_two[:, lanes(owner * 128, 128)], right)
+        left_ref, right_ref = factors[name]
+        depth = right_ref.shape[0]
+        if depth <= 512:
+            return left_product(left_ref[:, lanes(owner * 128, 128)], right_ref[...])
+
+        def term(spot, sums):
+            rows = pl.ds(pl.multiple_of(spot * 512, 512), 512)
+            return sums + left_product(left_ref[rows, lanes(owner * 128, 128)], right_ref[rows, :])
+
+        return lax.fori_loop(0, depth // 512, term, jnp.zeros((128, D), F32))
 
     def remote(unit, kind, src, dst, device):
         return pltpu.make_async_remote_copy(
@@ -793,25 +913,34 @@
         )
 
     def core_copy(unit):
-        return remote(unit, 0, core_out.at[unit % 2], core_in.at[unit % RING], (core_peer, member))
+        return remote(unit, 0, core_out.at[unit % 2], core_in.at[unit % CORES], (core_peer, member))
 
     def near_copy(unit):
-        return remote(unit, 1, near_out.at[unit % RING], near_in.at[unit % ROUND], (row ^ bits(unit)[0], member))
+        return remote(
+            unit, 1, near_out.at[unit % RING], near_in.at[unit % ROUND], (row ^ bits(unit)[0], member)
+        )
 
     def far_copy(unit):
         return remote(unit, 2, far_out.at[unit % RING], far_in.at[unit % ROUND], (row ^ bits(unit)[1], member))
 
+    direct = range(count - DIRECT, count)
+
     def hop_copy(unit, hop, upward):
-        target = jnp.clip(member + 1 if upward else member - 1, 0, members - 1)
+        reach = members - 1 - hop if unit in direct else 1
+        target = jnp.clip(member + reach if upward else member - reach, 0, members - 1)
         place = hop if upward else hops + hop
-        return remote(unit, 3 + place, hop_out.at[unit % RING, place], hop_in.at[unit, place], (row, target))
+        return remote(
+            unit, 3 + place, hop_out.at[unit % RING, place], hop_in.at[unit % ROUND, place], (row, target)
+        )
 
     def hop_sends(hop, upward):
         distance = members - 1 - hop
         return (member + distance <= members - 1) if upward else (member - distance >= 0)
 
-    def hop_gets(hop, upward):
+    def hop_gets(unit, hop, upward):
         distance = members - 1 - hop
+        if unit in direct:
+            return (member >= distance) if upward else (member <= members - 1 - distance)
         return (
             ((member >= 1) & (member - 1 + distance <= members - 1))
             if upward
@@ -819,6 +948,7 @@
         )
 
     def core_stage(unit):
+        loaded(*needs.get(unit, ()))
         if unit >= 2:
             core_copy(unit - 2).wait_send()
         targets = owners(unit, core_peer)
@@ -831,7 +961,7 @@
             return 0
 
         lax.fori_loop(0, 4, fill, 0)
-        if unit >= RING:
+        if unit >= CORES:
             pl.semaphore_wait(credit, 1)
         core_copy(unit).start()
 
@@ -842,7 +972,7 @@
         mine = owners(unit, row)
 
         def give(spot, _):
-            total = partial(unit, jnp.where(spot == 0, mine[0], mine[1])) + core_in[unit % RING, spot].astype(F32)
+            total = partial(unit, jnp.where(spot == 0, mine[0], mine[1])) + core_in[unit % CORES, spot].astype(F32)
             near_out[unit % RING, spot] = total.astype(BF16)
             return 0
 
@@ -850,47 +980,52 @@
         near_copy(unit).start()
 
         def keep(spot, _):
-            near_kept[unit % KEPT, spot] = partial(unit, jnp.where(spot == 0, mine[2], mine[3])) + core_in[
-                unit % RING, 2 + spot
-            ].astype(F32)
+            total = partial(unit, jnp.where(spot == 0, mine[2], mine[3])) + core_in[unit % CORES, 2 + spot].astype(F32)
+            near_kept[unit % KEPT, spot] = total.astype(BF16)
             return 0
 
         lax.fori_loop(0, 2, keep, 0)
-        if unit + RING < count:
+        if unit + CORES < count:
             pl.semaphore_signal(credit, inc=1, device_id=(core_peer, member), device_id_type=MESH)
 
     def far_stage(unit):
         near_copy(unit).wait_recv()
         if unit >= RING:
             far_copy(unit - RING).wait_send()
-        far_out[unit % RING] = (near_kept[unit % KEPT, 0] + near_in[unit % ROUND, 1].astype(F32)).astype(BF16)
+        far_out[unit % RING] = (
+            near_kept[unit % KEPT, 0].astype(F32) + near_in[unit % ROUND, 1].astype(F32)
+        ).astype(BF16)
         far_copy(unit).start()
 
     def hop_stage(unit, hop):
         if hop == 0:
             far_copy(unit).wait_recv()
             own[unit % RING] = (
-                near_kept[unit % KEPT, 1] + near_in[unit % ROUND, 0].astype(F32) + far_in[unit % ROUND].astype(F32)
+                near_kept[unit % KEPT, 1].astype(F32)
+                + near_in[unit % ROUND, 0].astype(F32)
+                + far_in[unit % ROUND].astype(F32)
             )
         for upward in (True, False):
             distance = members - 1 - hop
             owner = jnp.clip(member + distance if upward else member - distance, 0, members - 1)
             place = hop if upward else hops + hop
-            block = pl.ds(pl.multiple_of(owner * 256, 256), 256)
+            block = lanes(owner * 256, 256)
             if unit >= RING:
                 @pl.when(hop_sends(hop, upward))
                 def _():
                     hop_copy(unit - RING, hop, upward).wait_send()
 
-            if hop > 0:
-                @pl.when(hop_gets(hop - 1, upward))
+            if hop > 0 and unit not in direct:
+                arrived = hop_gets(unit, hop - 1, upward)
+
+                @pl.when(arrived)
                 def _():
                     hop_copy(unit, hop - 1, upward).wait_recv()
                     hop_out[unit % RING, place] = (
-                        own[unit % RING, :, block] + hop_in[unit, place - 1].astype(F32)
+                        own[unit % RING, :, block] + hop_in[unit % ROUND, place - 1].astype(F32)
                     ).astype(BF16)
 
-                @pl.when(hop_sends(hop, upward) & jnp.logical_not(hop_gets(hop - 1, upward)))
+                @pl.when(hop_sends(hop, upward) & jnp.logical_not(arrived))
                 def _():
                     hop_out[unit % RING, place] = own[unit % RING, :, block].astype(BF16)
 
@@ -904,50 +1039,339 @@
                 hop_copy(unit, hop, upward).start()
 
     def last_stage(unit):
-        _, _, out, left_start, left_step, right_start, right_step = units[unit]
-        rows, cols = pl.ds(left_start, 128), pl.ds(right_start, 256)
-        block = pl.ds(pl.multiple_of(member * 256, 256), 256)
-        out_refs[out][rows, cols] = own[unit % RING, :, block]
+        name, k = units[unit]
+        rows = pl.ds(k * 128 if name == Block.fo else 0, 128)
+        cols = pl.ds(k * 256 if name == Block.fi else 0, 256)
+        out_refs[name][rows, cols] = own[unit % RING, :, lanes(member * 256, 256)]
         for upward in (True, False):
-            place = hops - 1 if upward else 2 * hops - 1
-
-            @pl.when(hop_gets(hops - 1, upward))
-            def _():
-                hop_copy(unit, hops - 1, upward).wait_recv()
-                out_refs[out][rows, cols] += hop_in[unit, place].astype(F32)
-
-    pieces = part_ref.shape[2] // back_rows * part_ref.shape[0]
-    items_here = part_ref.shape[0]
-
-    def back_copy(piece, step):
-        which, start = piece // (pieces // items_here), piece % (pieces // items_here) * back_rows
+            for hop in range(hops) if unit in direct else (hops - 1,):
+                place = hop if upward else hops + hop
+
+                @pl.when(hop_gets(unit, hop, upward))
+                def _():
+                    hop_copy(unit, hop, upward).wait_recv()
+                    out_refs[name][rows, cols] += hop_in[unit % ROUND, place].astype(F32)
+
+    vector_sum[...] = small[Small.vectors][...]
+
+    def add_vector(index, cols, values):
+        vector_sum[index : index + 1, cols] += jnp.sum(values, 0, keepdims=True)
+
+    chunks = [(which, step % members) for which in range(items_here) for step in range(1, members + 1)]
+
+    def key_load(order):
+        which, step = chunks[order]
+        rows, slot = pl.ds(which * slots + step * mem_local, mem_local), order % 2
+        return (
+            pltpu.make_async_copy(big[Given.keys].at[rows], key_buf.at[slot], kv_sem.at[0, slot]),
+            pltpu.make_async_copy(big[Given.values].at[rows], value_buf.at[slot], kv_sem.at[1, slot]),
+        )
+
+    for copy in key_load(0):
+        copy.start()
+
+    def feed_back(k):
+        def job():
+            loaded((Given.feed_down, k), (Given.slope, k))
+            grad_active = right_product(grad_down[...], weight_buf[0])
+            if k < 3:
+                down_load(k + 1)
+            else:
+                whole(Given.output_cross, weight_buf.at[0])
+            grad = (grad_active * (exact, scale)[k % 2][...]).astype(BF16)
+            if k < 2:
+                slope_load(k + 2)
+            wide[pl.ds(D + k * 256, 256), :] = grad
+            sums = jnp.sum(grad.astype(F32), 0, keepdims=True)
+            for part in range(8):
+                target, place = 2 * k + part // 4, part % 4
+                vector_sum[13 + place : 14 + place, target * 128 : target * 128 + 128] = sums[
+                    :, part * 128 : part * 128 + 128
+                ]
+            loaded((Given.feed_up, k))
+            if k == 0:
+                loaded(Given.grad_three)
+            tokens_grad[...] += right_product(grad, weight_buf[1])
+            if k < 3:
+                up_load(k + 1)
+            else:
+                whole(Given.key_cross, weight_buf.at[1])
+
+        return job
+
+    def middle_norm_back():
+        loaded(Given.normed_two)
+        grad_in, gain_grad, shift_grad = norm_backward(
+            tokens_grad[...], normed_one[...], small[Small.inverse_two][...], small[Small.gains][1:2]
+        )
+        whole(Given.normed_one, normed_one)
+        whole(Given.exact_two, exact)
+        whole(Given.scale_two, scale)
+        vector_sum[11:12, :] = gain_grad.reshape(1, D)
+        vector_sum[8:9, :] = shift_grad.reshape(1, D)
+        tokens_grad[...] = grad_in
+        grad_cross[...] = grad_in.astype(BF16)
+        add_vector(5, pl.ds(0, D), grad_in)
+        loaded(Given.output_cross)
+        grad_mixed[...] = right_product(grad_cross[...], weight_buf[0])
+        whole(Given.value_cross, weight_buf.at[0])
+        loaded(Given.q_two, Given.exact_two, Given.scale_two)
+
+    def cross_prepare():
+        def pair(p, _):
+            cols = lanes(p * PAIR, PAIR)
+            for which in range(items_here):
+                rows = pl.ds(which * DEC, DEC)
+                grad_numer = grad_mixed[rows, cols] * scale[rows, cols]
+                grad_numer_low[rows, cols] = grad_numer.astype(BF16)
+                grad_total[which, pl.ds(p, 1), :] = total_grads(grad_numer * exact[rows, cols])
+            return 0
+
+        lax.fori_loop(0, PAIRS, pair, 0)
+
+    def cross_chunk(order):
+        which, step = chunks[order]
+
+        def job():
+            for copy in key_load(order):
+                copy.wait()
+            if order + 1 < len(chunks):
+                for copy in key_load(order + 1):
+                    copy.start()
+            rows, slot = pl.ds(which * DEC, DEC), order % 2
+            limit = small[Small.limits][1:2, which : which + 1] - lax.rem(member - step + members, members) * mem_local
+            allowed = lax.broadcasted_iota(jnp.int32, (mem_local, 2 * DEC), 0) < limit
+            lane_low = low_lanes(DEC)
+            at_rows = pl.ds(which * slots + step * mem_local, mem_local)
+
+            def pair(p, _):
+                cols = lanes(p * PAIR, PAIR)
+                q2 = stack_pair(q_two[rows, cols], lane_low)
+                gn2 = stack_pair(grad_numer_low[rows, cols], lane_low)
+                gk, gv, gq2 = attend_back_chunk(
+                    q2, gn2, grad_total[which, pl.ds(p, 1), :], key_buf[slot, :, cols], value_buf[slot, :, cols], allowed
+                )
+                gk_two[at_rows, cols] = gk.astype(BF16)
+                gv_two[at_rows, cols] = gv.astype(BF16)
+                add_vector(4, cols, gv)
+                grad = jnp.where(lane_low, gq2[:DEC], gq2[DEC:]) * 0.125
+                if step == 1:
+                    grad_mixed[rows, cols] = grad
+                else:
+                    grad_mixed[rows, cols] += grad
+                return 0
+
+            lax.fori_loop(0, PAIRS, pair, 0)
+            if step == 0:
+                gq_two[rows, :] = grad_mixed[rows, :].astype(BF16)
+                add_vector(3, pl.ds(0, D), grad_mixed[rows, :])
+
+        return job
+
+    def stage_copy(order):
+        which, step = chunks[order]
+        own_place = back_ref.at[member * items_here + which]
+        target = own_place if step == 0 else part_ref.at[which, step]
+        return pltpu.make_async_copy(stage.at[order % 2], target, stage_sem.at[order % 2])
+
+    def memory_part(order):
+        which, step = chunks[order]
+
+        def job():
+            if order == 0:
+                loaded(Given.key_cross, Given.value_cross)
+            rows = pl.ds(which * slots + step * mem_local, mem_local)
+            total = right_product(gk_two[rows, :], weight_buf[1]) + right_product(gv_two[rows, :], weight_buf[0])
+            stage[order % 2] = total.astype(BF16)
+            stage_copy(order).start()
+            if order == len(chunks) - 1:
+                whole(Given.query_cross, weight_buf.at[1])
+                whole(Given.output_self, weight_buf.at[0])
+                whole(Given.exact_one, exact)
+                whole(Given.scale_one, scale)
+                whole(Given.q_one, q_one)
+                whole(Given.k_one, k_one)
+                whole(Given.v_one, v_one)
+
+        return job
+
+    def norm_back():
+        loaded(Given.query_cross, Given.normed_one)
+        grad = tokens_grad[...] + right_product(gq_two[...], weight_buf[1])
+        whole(Given.query_self, weight_buf.at[1])
+        grad_in, gain_grad, shift_grad = norm_backward(
+            grad, normed_one[...], small[Small.inverse_one][...], small[Small.gains][0:1]
+        )
+        vector_sum[10:11, :] = gain_grad.reshape(1, D)
+        vector_sum[7:8, :] = shift_grad.reshape(1, D)
+        tokens_grad[...] = grad_in
+        grad_self[...] = grad_in.astype(BF16)
+        add_vector(2, pl.ds(0, D), grad_in)
+        loaded(Given.output_self)
+        grad_mixed[...] = right_product(grad_self[...], weight_buf[0])
+        whole(Given.key_self, weight_buf.at[0])
+        loaded(Given.exact_one, Given.scale_one, Given.q_one, Given.k_one, Given.v_one)
+
+    def self_back(which, low, high):
+        def job():
+            rows = pl.ds(which * DEC, DEC)
+            limit = small[Small.limits][0:1, which : which + 1]
+            slot = lax.broadcasted_iota(jnp.int32, (DEC, 2 * DEC), 0)
+            query = lax.broadcasted_iota(jnp.int32, (DEC, 2 * DEC), 1) % DEC
+            allowed = (slot <= query) & (slot < limit)
+
+            def pair(p, _):
+                cols = lanes(p * PAIR, PAIR)
+
+                lane_low = low_lanes(DEC)
+                grad_numer = grad_mixed[rows, cols] * scale[rows, cols]
+                gk, gv, gq2 = attend_back_chunk(
+                    stack_pair(q_one[rows, cols], lane_low),
+                    stack_pair(grad_numer.astype(BF16), lane_low),
+                    total_grads(grad_numer * exact[rows, cols]),
+                    k_one[rows, cols],
+                    v_one[rows, cols],
+                    allowed,
+                )
+                gk_one[rows, cols] = gk.astype(BF16)
+                gv_one[rows, cols] = gv.astype(BF16)
+                add_vector(1, cols, gv)
+                grad = jnp.where(lane_low, gq2[:DEC], gq2[DEC:]) * 0.125
+                gq_one[rows, cols] = grad.astype(BF16)
+                add_vector(0, cols, grad)
+                return 0
+
+            lax.fori_loop(low, high, pair, 0)
+
+        return job
+
+    def token_term(name, slot, grads, following=None):
+        def job():
+            loaded(name)
+            tokens_grad[...] += right_product(grads[...], weight_buf[slot])
+            if following:
+                whole(following, weight_buf.at[slot])
+
+        return job
+
+    def plane_vector(distance):
+        return pltpu.make_async_remote_copy(
+            src_ref=vector_sum.at[:, lanes((row ^ distance) * 128, 128)],
+            dst_ref=vector_in.at[distance],
+            send_sem=vec_send.at[0, distance],
+            recv_sem=vec_recv.at[0, distance],
+            device_id=(row ^ distance, member),
+            device_id_type=MESH,
+        )
+
+    def line_vector(step):
+        return pltpu.make_async_remote_copy(
+            src_ref=vector_in.at[0],
+            dst_ref=vector_far.at[step],
+            send_sem=vec_send.at[1, step],
+            recv_sem=vec_recv.at[1, step],
+            device_id=(row, lax.rem(member + step, members)),
+            device_id_type=MESH,
+        )
+
+    def vectors_start():
+        for distance in range(1, 8):
+            plane_vector(distance).start()
+
+    def vectors_pass():
+        total = vector_sum[:, lanes(row * 128, 128)]
+        for distance in range(1, 8):
+            plane_vector(distance).wait()
+            total = total + vector_in[distance]
+        vector_in[0] = total
+        for step in range(1, members):
+            line_vector(step).start()
+
+    def vectors_end():
+        total = vector_in[0]
+        for step in range(1, members):
+            line_vector(step).wait()
+            total = total + vector_far[step]
+        vector_out[...] = total
+
+    back_rows = mem_local // BACK_PIECES
+
+    def back_copy(which, step, piece):
         target = lax.rem(member - step + members, members)
+        rows = pl.ds(piece * back_rows, back_rows)
+        place = (which * members + step) * BACK_PIECES + piece
         return pltpu.make_async_remote_copy(
-            src_ref=part_ref.at[which, step, pl.ds(start, back_rows)],
-            dst_ref=back_ref.at[member * items_here + which, pl.ds(start, back_rows)],
-            send_sem=back_send.at[piece, step],
-            recv_sem=back_recv.at[piece, step],
+            src_ref=part_ref.at[which, step, rows],
+            dst_ref=back_ref.at[member * items_here + which, rows],
+            send_sem=back_send.at[place],
+            recv_sem=back_recv.at[place],
             device_id=(row, target),
             device_id_type=MESH,
         )
 
+    schedule = {}
+
+    def at(tick, *jobs):
+        schedule.setdefault(tick, []).extend(jobs)
+
+    steps = {}
+    for tick, orders in enumerate(((0,), (1,), (2, 3), (4,), (5,), (6,), (7,)), 2):
+        for order in orders:
+            steps[order] = tick
+    at(0, feed_back(0), feed_back(1))
+    at(1, feed_back(2), feed_back(3), middle_norm_back)
+    at(2, cross_prepare)
+    for order in range(len(chunks)):
+        at(steps[order], cross_chunk(order))
+        if order:
+            at(steps[order], stage_copy(order - 1).wait)
+        at(steps[order], memory_part(order))
+    at(steps[len(chunks) - 1], stage_copy(len(chunks) - 1).wait)
+    at(9, norm_back)
+    at(10, self_back(0, 0, 8))
+    at(11, self_back(1, 0, 4))
+    at(12, self_back(1, 4, 8), vectors_start)
+    at(14, token_term(Given.query_self, 1, gq_one, Given.value_self), vectors_pass)
+    at(15, token_term(Given.key_self, 0, gk_one))
+    at(16, token_term(Given.value_self, 1, gv_one), vectors_end)
+    moves, tick, weight = [], 0, 0
+    for order, (which, step) in enumerate(chunks):
+        if step == 0:
+            continue
+        for piece in range(BACK_PIECES):
+            ready = steps[min(order + 1, len(chunks) - 1)]
+            if ready > tick:
+                tick, weight = ready, 0
+            elif weight >= BACK_WEIGHT:
+                tick, weight = tick + 1, 0
+            weight += 2 if step == members // 2 else 1
+            moves.append((which, step, piece))
+            at(tick, back_copy(which, step, piece).start)
     far_tick, hop_tick = 1 + S_LAG, 1 + 2 * S_LAG
     last_tick = hop_tick + hops
-    for tick in range(max(count + last_tick, pieces)):
-        if tick < pieces:
-            for step in range(1, members):
-                back_copy(tick, step).start()
+    end = count + last_tick
+
+    for tick in range(end):
         if 0 <= tick - far_tick < count:
             far_stage(tick - far_tick)
         for hop in range(hops):
-            if 0 <= tick - hop_tick - hop < count:
+            if 0 <= tick - hop_tick - hop < count and tick - hop_tick - hop not in direct:
                 hop_stage(tick - hop_tick - hop, hop)
-        if 0 <= tick - last_tick < count:
+        if tick - hop_tick in direct:
+            for hop in range(hops):
+                hop_stage(tick - hop_tick, hop)
+        if 0 <= tick - last_tick < count and tick - last_tick not in direct:
             last_stage(tick - last_tick)
+        if tick - hop_tick - 1 in direct:
+            last_stage(tick - hop_tick - 1)
+        if 0 <= tick - 1 < count:
+            near_stage(tick - 1)
+        if tick == 8:
+            whole(Given.memory, wide)
         if 0 <= tick < count:
             core_stage(tick)
-        if 0 <= tick - 1 < count:
-            near_stage(tick - 1)
+        for job in schedule.get(tick, ()):
+            job()
     for unit in range(count - 2, count):
         core_copy(unit).wait_send()
     for unit in range(count - RING, count):
@@ -958,59 +1382,73 @@
                 @pl.when(hop_sends(hop, upward))
                 def _():
                     hop_copy(unit, hop, upward).wait_send()
-    for piece in range(pieces):
-        for step in range(1, members):
-            back_copy(piece, step).wait()
-
-
-def scatter_by_kernel(pairs, blocks, memory_part, members):
-    lefts, rights, units = [], [], []
-    for out, ((left, right), (height, width)) in enumerate(zip(pairs, blocks)):
-        spots = []
-        for value, found in ((left, lefts), (right, rights)):
-            for place, other in enumerate(found):
-                if other is value:
-                    spots.append(place)
-                    break
-            else:
-                spots.append(len(found))
-                found.append(value)
-        for left_start in range(0, height, 128):
-            for right_start in range(0, width, 256):
-                units.append((spots[0], spots[1], out, left_start, height, right_start, width))
-    count, hops = len(units), members - 1
-    items_here, _, mem_local, width = memory_part.shape
-    back_rows = 32
-    pieces = mem_local // back_rows * items_here
+    for move in moves:
+        back_copy(*move).wait()
+
+
+def scatter_by_kernel(big, small, blocks, members, items_here, mem_local):
+    count, hops = 16, members - 1
+    rows = big[Given.tokens].shape[0]
+    low = pltpu.VMEM((rows, D), BF16)
+    high = pltpu.VMEM((rows, D), F32)
+    slots = items_here * members * mem_local
+    out_shape = [jax.ShapeDtypeStruct(block, F32) for block in blocks]
+    out_shape += [
+        jax.ShapeDtypeStruct((rows, D), F32),
+        jax.ShapeDtypeStruct((small[Small.vectors].shape[0], 128), F32),
+        jax.ShapeDtypeStruct((items_here, members, mem_local, D), BF16),
+        jax.ShapeDtypeStruct((items_here * members, mem_local, D), BF16),
+    ]
     outs = pl.pallas_call(
-        functools.partial(scatter_kernel, members, tuple(units), back_rows),
-        out_shape=[jax.ShapeDtypeStruct(block, F32) for block in blocks]
-        + [jax.ShapeDtypeStruct((items_here * members, mem_local, width), BF16)],
-        in_specs=[VMEM] * (len(lefts) + len(rights)) + [ANY],
-        out_specs=[VMEM] * len(blocks) + [ANY],
+        functools.partial(scatter_kernel, members, items_here, mem_local),
+        out_shape=out_shape,
+        in_specs=[ANY] * Given.count + [VMEM] * Small.count,
+        out_specs=[VMEM] * (len(blocks) + 2) + [ANY, ANY],
         scratch_shapes=[
-            pltpu.VMEM((2, 4, 128, 1024), BF16),
-            pltpu.VMEM((RING, 4, 128, 1024), BF16),
-            pltpu.VMEM((RING, 2, 128, 1024), BF16),
-            pltpu.VMEM((ROUND, 2, 128, 1024), BF16),
-            pltpu.VMEM((KEPT, 2, 128, 1024), F32),
-            pltpu.VMEM((RING, 128, 1024), BF16),
-            pltpu.VMEM((ROUND, 128, 1024), BF16),
-            pltpu.VMEM((RING, 128, 1024), F32),
+            pltpu.VMEM((2 * D, D), BF16),
+            low, low, low, low, low, low, low, low,
+            high,
+            high, high, high,
+            low,
+            pltpu.VMEM((items_here, PAIRS, 2 * DEC), F32),
+            pltpu.VMEM((2, mem_local, D), BF16),
+            pltpu.VMEM((2, mem_local, D), BF16),
+            pltpu.VMEM((slots, D), BF16),
+            pltpu.VMEM((slots, D), BF16),
+            low,
+            pltpu.VMEM((2, D, D), BF16),
+            low,
+            pltpu.VMEM((2, mem_local, D), BF16),
+            pltpu.VMEM(small[Small.vectors].shape, F32),
+            pltpu.VMEM((8, small[Small.vectors].shape[0], 128), F32),
+            pltpu.VMEM((members, small[Small.vectors].shape[0], 128), F32),
+            pltpu.VMEM((2, 4, 128, D), BF16),
+            pltpu.VMEM((CORES, 4, 128, D), BF16),
+            pltpu.VMEM((RING, 2, 128, D), BF16),
+            pltpu.VMEM((ROUND, 2, 128, D), BF16),
+            pltpu.VMEM((KEPT, 2, 128, D), BF16),
+            pltpu.VMEM((RING, 128, D), BF16),
+            pltpu.VMEM((ROUND, 128, D), BF16),
+            pltpu.VMEM((RING, 128, D), F32),
             pltpu.VMEM((RING, 2 * hops, 128, 256), BF16),
-            pltpu.VMEM((count, 2 * hops, 128, 256), BF16),
+            pltpu.VMEM((ROUND, 2 * hops, 128, 256), BF16),
             pltpu.SemaphoreType.DMA((count, 3 + 2 * hops)),
             pltpu.SemaphoreType.DMA((count, 3 + 2 * hops)),
-            pltpu.SemaphoreType.DMA((pieces, members)),
-            pltpu.SemaphoreType.DMA((pieces, members)),
+            pltpu.SemaphoreType.DMA((items_here * members * BACK_PIECES,)),
+            pltpu.SemaphoreType.DMA((items_here * members * BACK_PIECES,)),
             pltpu.SemaphoreType.REGULAR,
+            pltpu.SemaphoreType.DMA((48,)),
+            pltpu.SemaphoreType.DMA((2, 2)),
+            pltpu.SemaphoreType.DMA((2,)),
+            pltpu.SemaphoreType.DMA((2, 8)),
+            pltpu.SemaphoreType.DMA((2, 8)),
         ],
         compiler_params=pltpu.CompilerParams(
-            collective_id=1, has_side_effects=True, vmem_limit_bytes=60 * 1024 * 1024
+            collective_id=1, has_side_effects=True, vmem_limit_bytes=62 * 1024 * 1024
         ),
         name="scatter_all",
-    )(*lefts, *rights, memory_part)
-    return outs[:-1], outs[-1]
+    )(*big, *small)
+    return outs[: len(blocks)], outs[len(blocks)], outs[len(blocks) + 1], outs[len(blocks) + 3]
 
 
 def scatter_by_collectives(pairs, blocks, memory_part, row, member, items_count, members):
@@ -1086,10 +1524,9 @@
 
     if by_kernel:
         (
-            queries_one, keys_one, values_one, mixed_one, exact_one, scale_one, hidden_one, normed_one, inverse_one,
-            queries_two, mixed_two, exact_two, scale_two, keys_two, values_two,
+            queries_one, keys_one, values_one, mixed_one, exact_one, scale_one, hidden_one, hidden_one_low, normed_one,
+            inverse_one, queries_two, mixed_two, exact_two, scale_two, keys_two, values_two,
         ) = forward
-        hidden_one_low = hidden_one.astype(BF16)
         keys_two, values_two = keys_two.reshape(-1, D), values_two.reshape(-1, D)
     else:
         tokens_float = tokens.astype(F32)
@@ -1123,50 +1560,7 @@
     grad_down = grad_three.astype(BF16)
 
     out_bias_grad = column_sums(grad_down)
-    grad_active = right_product(grad_down, feed_down)
     slope = cdf_part + inner_pre * jnp.exp(-0.5 * inner_pre * inner_pre) * normal_peak
-    grad_inner = (grad_active * slope).astype(BF16)
-    inner_bias_grad = column_sums(grad_inner)
-    grad_hidden_two = grad_three + right_product(grad_inner, feed_up)
-    grad_two, gain_grad_two, shift_grad_two = norm_backward(
-        grad_hidden_two, normed_two, inverse_two, gain_rows[1]
-    )
-    grad_cross_branch = grad_two.astype(BF16)
-    cross_out_bias_grad = column_sums(grad_cross_branch)
-    grad_mixed_two = right_product(grad_cross_branch, output_cross)
-    query_grad_two, key_grad_two, value_grad_two = attend_backward(
-        False, mem_local, own_mem, bases, queries_two, keys_two, values_two, grad_mixed_two, exact_two, scale_two
-    )
-    query_grad_two = query_grad_two * jnp.asarray(0.125, BF16)
-
-    memory_part = (
-        right_product(key_grad_two, key_cross) + right_product(value_grad_two, value_cross)
-    ).astype(BF16).reshape(item_count, members, mem_local, D)
-    cross_value_bias_grad = column_sums(value_grad_two)
-    cross_query_bias_grad = column_sums(query_grad_two)
-    grad_hidden_one = grad_two + right_product(query_grad_two, query_cross)
-    grad_one, gain_grad_one, shift_grad_one = norm_backward(
-        grad_hidden_one, normed_one, inverse_one, gain_rows[0]
-    )
-    grad_self_branch = grad_one.astype(BF16)
-    self_out_bias_grad = column_sums(grad_self_branch)
-    grad_mixed_one = right_product(grad_self_branch, output_self)
-    query_grad_one, key_grad_one, value_grad_one = attend_backward(
-        True, DEC, own_dec, bases, queries_one, keys_one, values_one, grad_mixed_one, exact_one, scale_one
-    )
-    query_grad_one = query_grad_one * jnp.asarray(0.125, BF16)
-    pairs = (
-        (active_low, grad_down),
-        (hidden_two_low, grad_inner),
-        (mixed_two, grad_cross_branch),
-        (memory_flat, key_grad_two),
-        (memory_flat, value_grad_two),
-        (hidden_one_low, query_grad_two),
-        (mixed_one, grad_self_branch),
-        (tokens, query_grad_one),
-        (tokens, key_grad_one),
-        (tokens, value_grad_one),
-    )
     blocks = tuple(
         weight.shape
         for weight in (
@@ -1174,51 +1568,114 @@
         )
     )
     if by_kernel:
-        grads, memory_back = scatter_by_kernel(pairs, blocks, memory_part, members)
+        vector_rows = (
+            jnp.zeros((24, D), F32).at[6].set(out_bias_grad).at[9].set(shift_grad_three).at[12].set(gain_grad_three)
+        )
+        big = (
+            active_low, grad_down, hidden_two_low, slope, feed_down, feed_up, grad_three, normed_two, mixed_two,
+            queries_two, exact_two, scale_two, tokens, mixed_one, hidden_one_low, normed_one, queries_one, keys_one,
+            values_one, keys_two, values_two, memory_flat, exact_one, scale_one, output_cross, key_cross, value_cross,
+            query_cross, output_self, query_self, key_self, value_self,
+        )
+        small = (inverse_one, inverse_two, gain_rows, jnp.stack([own_dec, own_mem]), vector_rows)
+        grads, tokens_grad, sums, memory_back = scatter_by_kernel(
+            big, small, blocks, members, item_count, mem_local
+        )
+        memory_grad = memory_back.astype(F32)
+        (
+            feed_down_grad, feed_up_grad, output_cross_grad, key_cross_grad, value_cross_grad, query_cross_grad,
+            output_self_grad, query_self_grad, key_self_grad, value_self_grad,
+        ) = grads
+        shifts_grad = sums[: shifts.shape[0]]
+        gains_grad = sums[shifts.shape[0] : bias_start]
+        bias_grad = sums[bias_start : bias_start + bias_rows].reshape(-1)
     else:
+        grad_active = right_product(grad_down, feed_down)
+        grad_inner = (grad_active * slope).astype(BF16)
+        inner_bias_grad = column_sums(grad_inner)
+        grad_hidden_two = grad_three + right_product(grad_inner, feed_up)
+        grad_two, gain_grad_two, shift_grad_two = norm_backward(
+            grad_hidden_two, normed_two, inverse_two, gain_rows[1]
+        )
+        grad_cross_branch = grad_two.astype(BF16)
+        cross_out_bias_grad = column_sums(grad_cross_branch)
+        grad_mixed_two = right_product(grad_cross_branch, output_cross)
+        query_grad_two, key_grad_two, value_grad_two = attend_backward(
+            False, mem_local, own_mem, bases, queries_two, keys_two, values_two, grad_mixed_two, exact_two, scale_two
+        )
+        query_grad_two = query_grad_two * jnp.asarray(0.125, BF16)
+
+        memory_part = (
+            right_product(key_grad_two, key_cross) + right_product(value_grad_two, value_cross)
+        ).astype(BF16).reshape(item_count, members, mem_local, D)
+        cross_value_bias_grad = column_sums(value_grad_two)
+        cross_query_bias_grad = column_sums(query_grad_two)
+        grad_hidden_one = grad_two + right_product(query_grad_two, query_cross)
+        grad_one, gain_grad_one, shift_grad_one = norm_backward(
+            grad_hidden_one, normed_one, inverse_one, gain_rows[0]
+        )
+        grad_self_branch = grad_one.astype(BF16)
+        self_out_bias_grad = column_sums(grad_self_branch)
+        grad_mixed_one = right_product(grad_self_branch, output_self)
+        query_grad_one, key_grad_one, value_grad_one = attend_backward(
+            True, DEC, own_dec, bases, queries_one, keys_one, values_one, grad_mixed_one, exact_one, scale_one
+        )
+        query_grad_one = query_grad_one * jnp.asarray(0.125, BF16)
+        pairs = (
+            (active_low, grad_down),
+            (hidden_two_low, grad_inner),
+            (mixed_two, grad_cross_branch),
+            (memory_flat, key_grad_two),
+            (memory_flat, value_grad_two),
+            (hidden_one_low, query_grad_two),
+            (mixed_one, grad_self_branch),
+            (tokens, query_grad_one),
+            (tokens, key_grad_one),
+            (tokens, value_grad_one),
+        )
         grads, memory_back = scatter_by_collectives(pairs, blocks, memory_part, row, member, items_count, members)
-    (
-        feed_down_grad, feed_up_grad, output_cross_grad, key_cross_grad, value_cross_grad, query_cross_grad,
-        output_self_grad, query_self_grad, key_self_grad, value_self_grad,
-    ) = grads
-    memory_grad = lax.dynamic_update_slice_in_dim(
-        memory_back.astype(F32), memory_part[:, 0].astype(F32), member * item_count, 0
-    )
-    tokens_grad = (
-        grad_one
-        + right_product(query_grad_one, query_self)
-        + right_product(key_grad_one, key_self)
-        + right_product(value_grad_one, value_self)
-    )
-    vectors = jnp.concatenate(
-        [
-            column_sums(query_grad_one),
-            column_sums(value_grad_one),
-            self_out_bias_grad,
-            cross_query_bias_grad,
-            cross_value_bias_grad,
-            cross_out_bias_grad,
-            out_bias_grad,
-            shift_grad_one,
-            shift_grad_two,
-            shift_grad_three,
-            gain_grad_one,
-            gain_grad_two,
-            gain_grad_three,
-            inner_bias_grad,
-        ]
-    )
-    vectors = lax.psum(vectors.reshape(-1, 128), ("items", "mem")).reshape(-1)
-    shift_count = shifts.shape[0] * D
-    gain_count = gains.shape[0] * D
-    shift_width, gain_width, bias_width = shifts.shape[1], gains.shape[1], inner_bias.shape[0]
-    shifts_grad = lax.dynamic_slice_in_dim(
-        vectors[:shift_count].reshape(-1, D), row * shift_width, shift_width, 1
-    )
-    gains_grad = lax.dynamic_slice_in_dim(
-        vectors[shift_count : shift_count + gain_count].reshape(-1, D), row * gain_width, gain_width, 1
-    )
-    bias_grad = lax.dynamic_slice_in_dim(vectors[shift_count + gain_count :], row * bias_width, bias_width)
+        (
+            feed_down_grad, feed_up_grad, output_cross_grad, key_cross_grad, value_cross_grad, query_cross_grad,
+            output_self_grad, query_self_grad, key_self_grad, value_self_grad,
+        ) = grads
+        memory_grad = lax.dynamic_update_slice_in_dim(
+            memory_back.astype(F32), memory_part[:, 0].astype(F32), member * item_count, 0
+        )
+        tokens_grad = (
+            grad_one
+            + right_product(query_grad_one, query_self)
+            + right_product(key_grad_one, key_self)
+            + right_product(value_grad_one, value_self)
+        )
+        vectors = jnp.concatenate(
+            [
+                column_sums(query_grad_one),
+                column_sums(value_grad_one),
+                self_out_bias_grad,
+                cross_query_bias_grad,
+                cross_value_bias_grad,
+                cross_out_bias_grad,
+                out_bias_grad,
+                shift_grad_one,
+                shift_grad_two,
+                shift_grad_three,
+                gain_grad_one,
+                gain_grad_two,
+                gain_grad_three,
+                inner_bias_grad,
+            ]
+        )
+        vectors = lax.psum(vectors.reshape(-1, 128), ("items", "mem")).reshape(-1)
+        shift_count = shifts.shape[0] * D
+        gain_count = gains.shape[0] * D
+        shift_width, gain_width, bias_width = shifts.shape[1], gains.shape[1], inner_bias.shape[0]
+        shifts_grad = lax.dynamic_slice_in_dim(
+            vectors[:shift_count].reshape(-1, D), row * shift_width, shift_width, 1
+        )
+        gains_grad = lax.dynamic_slice_in_dim(
+            vectors[shift_count : shift_count + gain_count].reshape(-1, D), row * gain_width, gain_width, 1
+        )
+        bias_grad = lax.dynamic_slice_in_dim(vectors[shift_count + gain_count :], row * bias_width, bias_width)
     return (
         layer_out,
         tokens_grad,

time: 508 us -> 435 us (0.86)
  matrix products: 44.1 us -> 13.5 us
  Pallas kernels: 400 us -> 386 us
  between operations: 14.9 us -> 1.11 us
  other arithmetic: 23.9 us -> 12 us
    dot_general x10 -> x0, matrix products: 33.2 us -> none  [right_product(): lax.dot_general(first_op, second_op, (((1,), (1,)), ((), ())), preferred_...]
    pallas_call x3 -> x1, Pallas kernels: 223 us -> 212 us  [scatter_by_kernel(): pl.pallas_call(functools.partial(scatter_kernel, members, items_here, mem...]
  transfers between devices with their start and end apart: 1 -> 0, of which waited for: 0 -> 0; matrix products, arithmetic and copies ran while one was open for 6% -> 0% of each run, Pallas kernels for 37% -> 0%
where the time goes in v4:
time: 435 us; the launch traced here: 430 us
  Pallas kernels  386 us (89%)
  local copies, waits for them, and re-layouts  17.1 us (4%)
  matrix products  13.5 us (3%)
  other arithmetic  12 us (3%)
    pallas_call x1, Pallas kernels, scatter_by_kernel(): pl.pallas_call(functools.partial(scatter_kernel, members, items_here, mem...  212 us
    pallas_call x1, Pallas kernels, gather_by_kernel(): pl.pallas_call(functools.partial(gather_kernel, members, items_here, tupl...  175 us
    dot_general x3, matrix products, product(): return jnp.dot(first_op, second_op, preferred_element_type=F32)  13.5 us

profile of v4, /device:TPU:0, one launch (start us, length us, event | category | flops | bytes accessed | tf_op | source)
XLA Modules:
  0.0 430.0 jit_solution(17161875390203817067)
XLA Ops:
  0.7 0.8 dynamic-slice_bitcast_fusion
  1.4 0.6 pad_add_fusion.refs_13_.refs_35_
  2.0 1.3 pad_maximum_fusion.refs_11_
  3.3 174.6 %gather_all.1 = (bf16[1024,1024]{1,0:T(8,128)(2,1)}, bf16[1024,1024]{1,0:T(8,128)(2,1)}, bf16[1024,1024]{1,0:T(8,128)(2,1)}, bf16[1024,1024]{1,0:T(8,128)(2,1)},...) custom-call(bf16[128,256]{1,0:T(8,128)(2,1)} %refs_0_.1, ...), custom_call_target="tpu_custom_call" | custom-call | tf_op jit(solution)/shard_map/gather_all/pallas_call | solution.py:537
  177.9 0.8 slice.99
  178.6 1.3 slice.103.refs_34_
  180.0 0.9 fusion.15
  180.8 2.8 fusion.16
  183.7 0.3 multiply_reduce_fusion.1
  183.9 0.8 copy.35.refs_33_
  184.8 0.3 fusion.13
  185.0 0.0 copy-start.1
  185.0 0.0 copy-start
  185.0 0.0 slice-start.1
  185.1 8.3 %fusion.3 = (f32[256,4096]{1,0:T(8,128)}, bf16[256,4096]{1,0:T(8,128)(2,1)S(1)}) fusion(f32[4096]{0:T(1024)S(1)} %bitcast.45, bf16[256,1024]{1,0:T(8,128)(2,1)S(1)} %get-tuple-element.141.refs_2_, bf16[1024,4096]{1,0:T(8,128)(2,1)} %get-tuple-element.97.refs_5_), kind=kOutput, calls=%fused_computation.5 | convolution fusion | flops 2159017984 | bytes 15220736 | tf_op jit(solution)/shard_map/dot_general | solution.py:27
  193.3 0.0 copy-done.1
  193.3 0.0 copy-done
  193.3 0.0 slice-done
  193.4 0.0 slice-done.1
  193.4 0.0 copy-start.3
  193.4 2.4 fusion.17
  195.8 0.0 copy-done.2
  195.9 0.2 multiply_reduce_fusion
  196.1 0.0 copy-done.3
  196.1 0.5 fusion.12
  196.7 2.0 convert_reduce_fusion.1
  198.7 0.1 scatter.11
  198.8 0.1 scatter.14.refs_36_
  198.9 0.0 copy-start.7
  198.9 0.6 copy-done.7
  199.6 211.7 %scatter_all.1 = (f32[512,256]{1,0:T(8,128)}, f32[128,1024]{1,0:T(8,128)}, f32[128,256]{1,0:T(8,128)}, f32[128,256]{1,0:T(8,128)}, f32[128,256]{1,0:T(8,128)}, /...) custom-call(bf16[256,4096]{1,0:T(8,128)(2,1)} %copy-done.2, ...), custom_call_target="tpu_custom_call" | custom-call | tf_op jit(solution)/shard_map/scatter_all/pallas_call | solution.py:1402
  411.3 1.3 slice_bitcast_fusion
  412.5 1.3 slice.94
  413.8 1.3 slice.93
  415.1 0.0 copy-start.12
  415.2 6.8 %convert_element_type.27 = f32[8,256,1024]{2,1,0:T(8,128)} convert(bf16[8,256,1024]{2,1,0:T(8,128)(2,1)} %get-tuple-element.122) | non-fusion elementwise | flops 2097152 | bytes 12582912 | tf_op jit(solution)/shard_map/convert_element_type | solution.py:1584
  421.9 0.0 copy-done.4
  422.0 1.0 copy.49
  422.9 0.7 copy.50
  423.6 0.7 copy.51
  424.2 0.7 copy.52
  424.9 0.7 copy.53
  425.6 0.7 copy.54
  426.2 0.7 copy.55
  426.9 0.7 copy.56
  427.5 0.7 copy.57
  428.2 0.8 copy.58
  429.0 0.8 copy.59
  (30 shorter events, 0.1 us)
Async XLA Ops:
  184.7 8.6 %slice-start = ((s8[8388608]{0:T(1024)(128)(4,1)}), s8[4194304]{0:T(1024)(128)(4,1)S(1)}, s32[]{:S(2)}) async-start(s8[8388608]{0:T(1024)(128)(4,1)} %bitcast.31), calls=%async_computation | async-start | bytes 8388608
  185.0 8.3 %copy-start.1 = (bf16[256,1024]{1,0:T(8,128)(2,1)}, bf16[256,1024]{1,0:T(8,128)(2,1)S(1)}, u32[]{:S(2)}) copy-start(bf16[256,1024]{1,0:T(8,128)(2,1)S(1)} %get-tuple-element.141.refs_2_) | copy-start | bytes 1572868
  185.0 8.3 %copy-start = (f32[256,1024]{1,0:T(8,128)}, f32[256,1024]{1,0:T(8,128)S(1)}, u32[]{:S(2)}) copy-start(f32[256,1024]{1,0:T(8,128)S(1)} %get-tuple-element.142.refs_7_) | copy-start | bytes 3145732
  185.0 8.3 %slice-start.1 = ((s8[8388608]{0:T(1024)(128)(4,1)}), s8[4194304]{0:T(1024)(128)(4,1)S(1)}, s32[]{:S(2)}) async-start(s8[8388608]{0:T(1024)(128)(4,1)} %bitcast.31), calls=%async_computation.1 | async-start | bytes 8388608
  193.3 2.5 copy-start.2
  193.4 2.7 copy-start.3
  198.9 0.6 copy-start.7
  415.1 6.8 %copy-start.4 = (f32[256,1024]{1,0:T(8,128)S(1)}, f32[256,1024]{1,0:T(8,128)}, u32[]{:S(2)}) copy-start(f32[256,1024]{1,0:T(8,128)} %get-tuple-element.175) | copy-start | bytes 3145732
  415.1 7.8 %copy-start.15 = (f32[128,256]{1,0:T(8,128)S(1)}, f32[128,256]{1,0:T(8,128)}, u32[]{:S(2)}) copy-start(f32[128,256]{1,0:T(8,128)} %get-tuple-element.177) | copy-start | bytes 393220
  415.1 8.5 %copy-start.14 = (f32[128,256]{1,0:T(8,128)S(1)}, f32[128,256]{1,0:T(8,128)}, u32[]{:S(2)}) copy-start(f32[128,256]{1,0:T(8,128)} %get-tuple-element.178) | copy-start | bytes 393220
  415.1 9.1 %copy-start.13 = (f32[128,256]{1,0:T(8,128)S(1)}, f32[128,256]{1,0:T(8,128)}, u32[]{:S(2)}) copy-start(f32[128,256]{1,0:T(8,128)} %get-tuple-element.179) | copy-start | bytes 393220
  415.1 9.8 %copy-start.12 = (f32[128,256]{1,0:T(8,128)S(1)}, f32[128,256]{1,0:T(8,128)}, u32[]{:S(2)}) copy-start(f32[128,256]{1,0:T(8,128)} %get-tuple-element.180) | copy-start | bytes 393220
  415.1 10.4 %copy-start.11 = (f32[128,256]{1,0:T(8,128)S(1)}, f32[128,256]{1,0:T(8,128)}, u32[]{:S(2)}) copy-start(f32[128,256]{1,0:T(8,128)} %get-tuple-element.181) | copy-start | bytes 393220
  415.1 11.1 %copy-start.10 = (f32[128,256]{1,0:T(8,128)S(1)}, f32[128,256]{1,0:T(8,128)}, u32[]{:S(2)}) copy-start(f32[128,256]{1,0:T(8,128)} %get-tuple-element.182) | copy-start | bytes 393220
  415.1 11.7 %copy-start.9 = (f32[128,256]{1,0:T(8,128)S(1)}, f32[128,256]{1,0:T(8,128)}, u32[]{:S(2)}) copy-start(f32[128,256]{1,0:T(8,128)} %get-tuple-element.183) | copy-start | bytes 393220
  415.2 12.4 %copy-start.8 = (f32[128,256]{1,0:T(8,128)S(1)}, f32[128,256]{1,0:T(8,128)}, u32[]{:S(2)}) copy-start(f32[128,256]{1,0:T(8,128)} %get-tuple-element.184) | copy-start | bytes 393220
  421.9 6.2 %copy-start.6 = (f32[128,1024]{1,0:T(8,128)S(1)}, f32[128,1024]{1,0:T(8,128)}, u32[]{:S(2)}) copy-start(f32[128,1024]{1,0:T(8,128)} %get-tuple-element.185) | copy-start | bytes 1572868
  422.0 7.0 %copy-start.5 = (f32[512,256]{1,0:T(8,128)S(1)}, f32[512,256]{1,0:T(8,128)}, u32[]{:S(2)}) copy-start(f32[512,256]{1,0:T(8,128)} %get-tuple-element.186) | copy-start | bytes 1572868

commit v5 on v4

--- a/solution.py
+++ b/solution.py
@@ -233,6 +233,14 @@
     )
     last = max([count - 1 + done_lag, due[-1] + 2] + list(jobs))
     for tick in range(last + 1):
+        unit = tick - plane_lag
+        if 0 <= unit < count:
+            for hop in range(hops) if unit in straight else (hops - 1,):
+                along_arrive(unit, hop)
+            own_copy(unit).wait()
+            to_x(unit).start()
+            to_y(unit).start()
+            to_core(unit, 0).start()
         if tick in straight:
             straight_each(tick, lambda copy: copy.start())
             own_copy(tick).start()
@@ -248,14 +256,6 @@
             if due[piece] == tick:
                 for step in range(1, members):
                     memory_send(piece, step).start()
-        unit = tick - plane_lag
-        if 0 <= unit < count:
-            for hop in range(hops) if unit in straight else (hops - 1,):
-                along_arrive(unit, hop)
-            own_copy(unit).wait()
-            to_x(unit).start()
-            to_y(unit).start()
-            to_core(unit, 0).start()
         unit = tick - plane_lag - X_LAG
         if 0 <= unit < count:
             to_x(unit).wait_recv()
@@ -304,7 +304,7 @@
     forward.finish()
 
 
-def attend_pair(queries, keys_at, values_at, allowed_at, chunks):
+def attend_parts(queries, keys_at, values_at, allowed_at, chunks):
     lane_low = low_lanes(DEC)
     q2 = stack_pair(queries, lane_low)
     numer, total = None, None
@@ -315,8 +315,12 @@
         term = product(exp_scores.astype(BF16), values_at(step))
         total = part if total is None else total + part
         numer = term if numer is None else numer + term
-    numer = jnp.where(lane_low, numer[:DEC], numer[DEC:])
-    scale = 1.0 / jnp.where(lane_low, total[:DEC], total[DEC:])
+    return jnp.where(lane_low, numer[:DEC], numer[DEC:]), jnp.where(lane_low, total[:DEC], total[DEC:])
+
+
+def attend_pair(queries, keys_at, values_at, allowed_at, chunks):
+    numer, total = attend_parts(queries, keys_at, values_at, allowed_at, chunks)
+    scale = 1.0 / total
     return numer * scale, scale
 
 
@@ -331,35 +335,37 @@
         wide, low = jax.ShapeDtypeStruct((self.rows, D), F32), jax.ShapeDtypeStruct((self.rows, D), BF16)
         keys = jax.ShapeDtypeStruct((self.items_here, self.members, self.mem_local, D), BF16)
         inverse = jax.ShapeDtypeStruct((self.rows, 1), F32)
-        return [low, low, low, low, wide, wide, wide, low, wide, inverse, low, low, wide, wide, keys, keys]
+        return [low, low, low, low, wide, wide, wide, low, wide, low, inverse, low, wide, wide, keys, keys]
 
     def out_specs(self):
-        return [VMEM] * 14 + [ANY] * 2
+        return [ANY] * 10 + [VMEM] * 4 + [ANY] * 2
 
     def scratch(self):
-        return [
+        return [pltpu.VMEM(shape.shape, shape.dtype) for shape in self.out_shapes()[:10]] + [
             pltpu.VMEM((2, D, D), BF16),
             pltpu.VMEM((2, D, D), BF16),
             pltpu.VMEM((2, self.members, self.mem_local // 4, D), BF16),
             pltpu.VMEM((self.items_here, self.members, self.mem_local, D), BF16),
             pltpu.VMEM((self.items_here, self.members, self.mem_local, D), BF16),
-            pltpu.SemaphoreType.DMA((16,)),
+            pltpu.SemaphoreType.DMA((20,)),
         ]
 
     def jobs(
         self, members, items_here, member, tokens_ref, limits_ref, whole_refs, items_ref, vectors_ref, outs, scratch,
         done_lag, due,
     ):
-        (
-            q_one, k_one, v_one, mixed_one, exact_one, scale_one, hidden_one, hidden_low, normed_one, inverse_one, q_two,
-            mixed_two, exact_two, scale_two, keys_out, values_out,
-        ) = outs
-        weight_buf, cross_buf, rows_buf, keys, values, sems = scratch
+        early, (inverse_one, mixed_two, exact_two, scale_two, keys_out, values_out) = outs[:10], outs[10:]
+        q_one, k_one, v_one, mixed_one, exact_one, scale_one, hidden_one, hidden_low, normed_one, q_two = scratch[:10]
+        weight_buf, cross_buf, rows_buf, keys, values, sems = scratch[10:]
+        early_copies = [
+            pltpu.make_async_copy(source, target, sems.at[10 + place])
+            for place, (source, target) in enumerate(zip(scratch[:10], early))
+        ]
         part = self.mem_local // 4
         schedule = {}
 
-        def at(tick, job):
-            schedule.setdefault(tick, []).append(job)
+        def at(tick, *jobs):
+            schedule.setdefault(tick, []).extend(jobs)
 
         def vector(index):
             return vectors_ref[...].astype(F32)[index : index + 1]
@@ -450,27 +456,35 @@
 
             return job
 
-        def cross_attend(which, low, high):
+        def cross_attend(which, low, high, first, size, begin, end):
             def job():
                 rows = pl.ds(which * DEC, DEC)
-                limit = limits_ref[1:2, which : which + 1]
-                slot = lax.broadcasted_iota(jnp.int32, (2 * DEC, self.mem_local), 1)
+                limit = limits_ref[1:2, which : which + 1] - first
+                slot = lax.broadcasted_iota(jnp.int32, (2 * DEC, size), 1)
 
                 def allowed(step):
                     return slot < limit - lax.rem(member - step + members, members) * self.mem_local
 
                 def pair(p, _):
                     cols = pl.ds(pl.multiple_of(p * PAIR, PAIR), PAIR)
-                    exact, scale = attend_pair(
+                    numer, total = attend_parts(
                         q_two[rows, cols],
-                        lambda step: keys[which, step, :, cols],
-                        lambda step: values[which, step, :, cols],
+                        lambda step: keys[which, step, pl.ds(first, size), cols],
+                        lambda step: values[which, step, pl.ds(first, size), cols],
                         allowed,
                         members,
                     )
-                    mixed_two[rows, cols] = exact.astype(BF16)
-                    exact_two[rows, cols] = exact
-                    scale_two[rows, cols] = scale
+                    if not begin:
+                        numer, total = numer + exact_two[rows, cols], total + scale_two[rows, cols]
+                    if end:
+                        scale = 1.0 / total
+                        exact = numer * scale
+                        mixed_two[rows, cols] = exact.astype(BF16)
+                        exact_two[rows, cols] = exact
+                        scale_two[rows, cols] = scale
+                    else:
+                        exact_two[rows, cols] = numer
+                        scale_two[rows, cols] = total
                     return 0
 
                 lax.fori_loop(low, high, pair, 0)
@@ -491,6 +505,7 @@
         at(start + 3, self_attend(1))
         at(start + 3, first_norm(1, 5))
         at(start + 4, cross_query(0, 6))
+        at(start + 5, *[copy.start for copy in early_copies])
         previous = 1 + done_lag
         per_item = len(due) // items_here
         for which in range(items_here):
@@ -504,10 +519,11 @@
             begin = max(previous, start + 5)
             if which < items_here - 1:
                 for quarter in range(4):
-                    at(begin + quarter, cross_attend(which, 2 * quarter, 2 * quarter + 2))
+                    at(begin + quarter, cross_attend(which, 2 * quarter, 2 * quarter + 2, 0, self.mem_local, True, True))
             else:
-                at(late, cross_attend(which, 0, PAIRS))
-        self.pending = [store(which, value) for which in range(items_here) for value in range(2)]
+                at(late - 1, cross_attend(which, 0, PAIRS, 0, 3 * part, True, False))
+                at(late, cross_attend(which, 0, PAIRS, 3 * part, part, False, True))
+        self.pending = early_copies + [store(which, value) for which in range(items_here) for value in range(2)]
         return schedule
 
     def finish(self):
@@ -745,8 +761,8 @@
     ]
 
 RING, KEPT, ROUND, CORES = 4, 6, 10, 3
-BACK_PIECES, BACK_WEIGHT, DIRECT = 8, 4, 0
-S_LAG = 3
+BACK_PIECES, BACK_EARLY, BACK_LATE, DIRECT = 8, 6, 3, 0
+S_LAG = 2
 
 
 def total_grads(weighted):
@@ -1334,6 +1350,7 @@
     at(14, token_term(Given.query_self, 1, gq_one, Given.value_self), vectors_pass)
     at(15, token_term(Given.key_self, 0, gk_one))
     at(16, token_term(Given.value_self, 1, gv_one), vectors_end)
+    far_tick, hop_tick = 1 + S_LAG, 1 + 2 * S_LAG
     moves, tick, weight = [], 0, 0
     for order, (which, step) in enumerate(chunks):
         if step == 0:
@@ -1342,18 +1359,23 @@
             ready = steps[min(order + 1, len(chunks) - 1)]
             if ready > tick:
                 tick, weight = ready, 0
-            elif weight >= BACK_WEIGHT:
+            elif weight >= (BACK_EARLY if tick < hop_tick else BACK_LATE):
                 tick, weight = tick + 1, 0
             weight += 2 if step == members // 2 else 1
             moves.append((which, step, piece))
             at(tick, back_copy(which, step, piece).start)
-    far_tick, hop_tick = 1 + S_LAG, 1 + 2 * S_LAG
     last_tick = hop_tick + hops
     end = count + last_tick
 
     for tick in range(end):
         if 0 <= tick - far_tick < count:
             far_stage(tick - far_tick)
+        if 0 <= tick - 1 < count:
+            near_stage(tick - 1)
+        if tick == 8:
+            whole(Given.memory, wide)
+        if 0 <= tick < count:
+            core_stage(tick)
         for hop in range(hops):
             if 0 <= tick - hop_tick - hop < count and tick - hop_tick - hop not in direct:
                 hop_stage(tick - hop_tick - hop, hop)
@@ -1364,12 +1386,6 @@
             last_stage(tick - last_tick)
         if tick - hop_tick - 1 in direct:
             last_stage(tick - hop_tick - 1)
-        if 0 <= tick - 1 < count:
-            near_stage(tick - 1)
-        if tick == 8:
-            whole(Given.memory, wide)
-        if 0 <= tick < count:
-            core_stage(tick)
         for job in schedule.get(tick, ()):
             job()
     for unit in range(count - 2, count):
@@ -1525,7 +1541,7 @@
     if by_kernel:
         (
             queries_one, keys_one, values_one, mixed_one, exact_one, scale_one, hidden_one, hidden_one_low, normed_one,
-            inverse_one, queries_two, mixed_two, exact_two, scale_two, keys_two, values_two,
+            queries_two, inverse_one, mixed_two, exact_two, scale_two, keys_two, values_two,
         ) = forward
         keys_two, values_two = keys_two.reshape(-1, D), values_two.reshape(-1, D)
     else:

time: 435 us -> 425 us (0.977)
  Pallas kernels: 386 us -> 377 us
    pallas_call x1, Pallas kernels: 212 us -> 203 us  [scatter_by_kernel(): pl.pallas_call(functools.partial(scatter_kernel, members, items_here, mem...]
where the time goes in v5:
time: 425 us; the launch traced here: 421 us
  Pallas kernels  377 us (89%)
  local copies, waits for them, and re-layouts  17.1 us (4%)
  matrix products  13.5 us (3%)
  other arithmetic  12 us (3%)
    pallas_call x1, Pallas kernels, scatter_by_kernel(): pl.pallas_call(functools.partial(scatter_kernel, members, items_here, mem...  203 us
    pallas_call x1, Pallas kernels, gather_by_kernel(): pl.pallas_call(functools.partial(gather_kernel, members, items_here, tupl...  174 us
    dot_general x3, matrix products, product(): return jnp.dot(first_op, second_op, preferred_element_type=F32)  13.5 us
    unnamed x47, local copies, waits for them, and re-layouts  8.51 us

profile of v5, /device:TPU:0, one launch (start us, length us, event | category | flops | bytes accessed | tf_op | source)
XLA Modules:
  0.0 420.7 jit_solution(5503280993265861384)
XLA Ops:
  0.7 0.8 dynamic-slice_bitcast_fusion
  1.4 0.6 pad_add_fusion.refs_13_.refs_35_
  2.0 1.3 pad_maximum_fusion.refs_11_
  3.3 173.9 %gather_all.1 = (bf16[1024,1024]{1,0:T(8,128)(2,1)}, bf16[1024,1024]{1,0:T(8,128)(2,1)}, bf16[1024,1024]{1,0:T(8,128)(2,1)}, bf16[1024,1024]{1,0:T(8,128)(2,1)},...) custom-call(bf16[128,256]{1,0:T(8,128)(2,1)} %refs_0_.1, ...), custom_call_target="tpu_custom_call" | custom-call | tf_op jit(solution)/shard_map/gather_all/pallas_call | solution.py:553
  177.2 0.8 slice.99
  178.0 1.3 slice.103.refs_34_
  179.3 0.9 fusion.15
  180.2 2.8 fusion.16
  183.0 0.3 multiply_reduce_fusion.1
  183.3 0.8 copy.35.refs_33_
  184.1 0.3 fusion.13
  184.4 0.0 copy-start.1
  184.4 0.0 copy-start
  184.4 0.0 slice-start.1
  184.4 8.3 %fusion.3 = (f32[256,4096]{1,0:T(8,128)}, bf16[256,4096]{1,0:T(8,128)(2,1)S(1)}) fusion(f32[4096]{0:T(1024)S(1)} %bitcast.45, bf16[256,1024]{1,0:T(8,128)(2,1)S(1)} %get-tuple-element.141.refs_2_, bf16[1024,4096]{1,0:T(8,128)(2,1)} %get-tuple-element.97.refs_5_), kind=kOutput, calls=%fused_computation.5 | convolution fusion | flops 2159017984 | bytes 15220736 | tf_op jit(solution)/shard_map/dot_general | solution.py:27
  192.7 0.0 copy-done.1
  192.7 0.0 copy-done
  192.7 0.0 copy-start.3
  192.7 2.4 fusion.17
  195.2 0.2 multiply_reduce_fusion
  195.5 0.5 fusion.12
  196.0 2.0 convert_reduce_fusion.1
  198.0 0.1 scatter.11
  198.1 0.1 scatter.14.refs_36_
  198.2 0.0 copy-start.7
  198.3 0.6 copy-done.7
  198.9 203.1 %scatter_all.1 = (f32[512,256]{1,0:T(8,128)}, f32[128,1024]{1,0:T(8,128)}, f32[128,256]{1,0:T(8,128)}, f32[128,256]{1,0:T(8,128)}, f32[128,256]{1,0:T(8,128)}, /...) custom-call(bf16[256,4096]{1,0:T(8,128)(2,1)} %copy-done.2, ...), custom_call_target="tpu_custom_call" | custom-call | tf_op jit(solution)/shard_map/scatter_all/pallas_call | solution.py:1418
  402.0 1.3 slice_bitcast_fusion
  403.3 1.3 slice.94
  404.5 1.3 slice.93
  405.9 6.8 %convert_element_type.27 = f32[8,256,1024]{2,1,0:T(8,128)} convert(bf16[8,256,1024]{2,1,0:T(8,128)(2,1)} %get-tuple-element.122) | non-fusion elementwise | flops 2097152 | bytes 12582912 | tf_op jit(solution)/shard_map/convert_element_type | solution.py:1600
  412.7 1.0 copy.49
  413.7 0.7 copy.50
  414.3 0.7 copy.51
  415.0 0.7 copy.52
  415.6 0.0 copy-done.12
  415.6 0.7 copy.53
  416.3 0.0 copy-done.11
  416.3 0.7 copy.54
  417.0 0.0 copy-done.10
  417.0 0.7 copy.55
  417.6 0.0 copy-done.9
  417.6 0.7 copy.56
  418.3 0.0 copy-done.8
  418.3 0.7 copy.57
  418.9 0.8 copy.58
  419.7 0.0 copy-done.5
  419.7 0.8 copy.59
  (30 shorter events, 0.1 us)
Async XLA Ops:
  184.1 8.6 %slice-start = ((s8[8388608]{0:T(1024)(128)(4,1)}), s8[4194304]{0:T(1024)(128)(4,1)S(1)}, s32[]{:S(2)}) async-start(s8[8388608]{0:T(1024)(128)(4,1)} %bitcast.31), calls=%async_computation | async-start | bytes 8388608
  184.4 8.3 %copy-start.1 = (bf16[256,1024]{1,0:T(8,128)(2,1)}, bf16[256,1024]{1,0:T(8,128)(2,1)S(1)}, u32[]{:S(2)}) copy-start(bf16[256,1024]{1,0:T(8,128)(2,1)S(1)} %get-tuple-element.141.refs_2_) | copy-start | bytes 1572868
  184.4 8.3 %copy-start = (f32[256,1024]{1,0:T(8,128)}, f32[256,1024]{1,0:T(8,128)S(1)}, u32[]{:S(2)}) copy-start(f32[256,1024]{1,0:T(8,128)S(1)} %get-tuple-element.142.refs_7_) | copy-start | bytes 3145732
  184.4 8.3 %slice-start.1 = ((s8[8388608]{0:T(1024)(128)(4,1)}), s8[4194304]{0:T(1024)(128)(4,1)S(1)}, s32[]{:S(2)}) async-start(s8[8388608]{0:T(1024)(128)(4,1)} %bitcast.31), calls=%async_computation.1 | async-start | bytes 8388608
  192.7 2.5 copy-start.2
  192.7 2.7 copy-start.3
  198.2 0.6 copy-start.7
  405.8 6.8 %copy-start.4 = (f32[256,1024]{1,0:T(8,128)S(1)}, f32[256,1024]{1,0:T(8,128)}, u32[]{:S(2)}) copy-start(f32[256,1024]{1,0:T(8,128)} %get-tuple-element.175) | copy-start | bytes 3145732
  405.8 7.8 %copy-start.15 = (f32[128,256]{1,0:T(8,128)S(1)}, f32[128,256]{1,0:T(8,128)}, u32[]{:S(2)}) copy-start(f32[128,256]{1,0:T(8,128)} %get-tuple-element.177) | copy-start | bytes 393220
  405.8 8.5 %copy-start.14 = (f32[128,256]{1,0:T(8,128)S(1)}, f32[128,256]{1,0:T(8,128)}, u32[]{:S(2)}) copy-start(f32[128,256]{1,0:T(8,128)} %get-tuple-element.178) | copy-start | bytes 393220
  405.8 9.1 %copy-start.13 = (f32[128,256]{1,0:T(8,128)S(1)}, f32[128,256]{1,0:T(8,128)}, u32[]{:S(2)}) copy-start(f32[128,256]{1,0:T(8,128)} %get-tuple-element.179) | copy-start | bytes 393220
  405.9 9.8 %copy-start.12 = (f32[128,256]{1,0:T(8,128)S(1)}, f32[128,256]{1,0:T(8,128)}, u32[]{:S(2)}) copy-start(f32[128,256]{1,0:T(8,128)} %get-tuple-element.180) | copy-start | bytes 393220
  405.9 10.4 %copy-start.11 = (f32[128,256]{1,0:T(8,128)S(1)}, f32[128,256]{1,0:T(8,128)}, u32[]{:S(2)}) copy-start(f32[128,256]{1,0:T(8,128)} %get-tuple-element.181) | copy-start | bytes 393220
  405.9 11.1 %copy-start.10 = (f32[128,256]{1,0:T(8,128)S(1)}, f32[128,256]{1,0:T(8,128)}, u32[]{:S(2)}) copy-start(f32[128,256]{1,0:T(8,128)} %get-tuple-element.182) | copy-start | bytes 393220
  405.9 11.7 %copy-start.9 = (f32[128,256]{1,0:T(8,128)S(1)}, f32[128,256]{1,0:T(8,128)}, u32[]{:S(2)}) copy-start(f32[128,256]{1,0:T(8,128)} %get-tuple-element.183) | copy-start | bytes 393220
  405.9 12.4 %copy-start.8 = (f32[128,256]{1,0:T(8,128)S(1)}, f32[128,256]{1,0:T(8,128)}, u32[]{:S(2)}) copy-start(f32[128,256]{1,0:T(8,128)} %get-tuple-element.184) | copy-start | bytes 393220
  412.7 6.2 %copy-start.6 = (f32[128,1024]{1,0:T(8,128)S(1)}, f32[128,1024]{1,0:T(8,128)}, u32[]{:S(2)}) copy-start(f32[128,1024]{1,0:T(8,128)} %get-tuple-element.185) | copy-start | bytes 1572868
  412.7 7.0 %copy-start.5 = (f32[512,256]{1,0:T(8,128)S(1)}, f32[512,256]{1,0:T(8,128)}, u32[]{:S(2)}) copy-start(f32[512,256]{1,0:T(8,128)} %get-tuple-element.186) | copy-start | bytes 1572868

commit v6 on v5

--- a/solution.py
+++ b/solution.py
@@ -18,7 +18,7 @@
 MESH = pl.DeviceIdType.MESH
 F32 = jnp.float32
 BF16 = jnp.bfloat16
-X_LAG, FIRST_PIECE, SPREAD, STRAIGHT = 1, 2, 16, 3
+X_LAG, FIRST_PIECE, SPREAD, STRAIGHT = 1, 2, 17, 3
 ANY = pl.BlockSpec(memory_space=pl.ANY)
 VMEM = pl.BlockSpec(memory_space=pltpu.VMEM)
 
@@ -761,7 +761,7 @@
     ]
 
 RING, KEPT, ROUND, CORES = 4, 6, 10, 3
-BACK_PIECES, BACK_EARLY, BACK_LATE, DIRECT = 8, 6, 3, 0
+BACK_PIECES, BACK_EARLY, BACK_LATE, DIRECT = 8, 6, 4, 0
 S_LAG = 2
 
 

time: 425 us -> 424 us (level)
  no operation moved by 1% of the time
where the time goes in v6:
time: 424 us; the launch traced here: 419 us
  Pallas kernels  375 us (88%)
  local copies, waits for them, and re-layouts  17.1 us (4%)
  matrix products  13.5 us (3%)
  other arithmetic  12 us (3%)
    pallas_call x1, Pallas kernels, scatter_by_kernel(): pl.pallas_call(functools.partial(scatter_kernel, members, items_here, mem...  202 us
    pallas_call x1, Pallas kernels, gather_by_kernel(): pl.pallas_call(functools.partial(gather_kernel, members, items_here, tupl...  174 us
    dot_general x3, matrix products, product(): return jnp.dot(first_op, second_op, preferred_element_type=F32)  13.5 us
    unnamed x47, local copies, waits for them, and re-layouts  8.51 us

profile of v6, /device:TPU:0, one launch (start us, length us, event | category | flops | bytes accessed | tf_op | source)
XLA Modules:
  0.0 419.1 jit_solution(14252102538220308117)
XLA Ops:
  0.7 0.8 dynamic-slice_bitcast_fusion
  1.4 0.6 pad_add_fusion.refs_13_.refs_35_
  2.0 1.3 pad_maximum_fusion.refs_11_
  3.3 173.9 %gather_all.1 = (bf16[1024,1024]{1,0:T(8,128)(2,1)}, bf16[1024,1024]{1,0:T(8,128)(2,1)}, bf16[1024,1024]{1,0:T(8,128)(2,1)}, bf16[1024,1024]{1,0:T(8,128)(2,1)},...) custom-call(bf16[128,256]{1,0:T(8,128)(2,1)} %refs_0_.1, ...), custom_call_target="tpu_custom_call" | custom-call | tf_op jit(solution)/shard_map/gather_all/pallas_call | solution.py:553
  177.2 0.8 slice.99
  178.0 1.3 slice.103.refs_34_
  179.3 0.9 fusion.15
  180.2 2.8 fusion.16
  183.0 0.3 multiply_reduce_fusion.1
  183.3 0.8 copy.35.refs_33_
  184.1 0.3 fusion.13
  184.4 0.0 copy-start.1
  184.4 0.0 copy-start
  184.4 0.0 slice-start.1
  184.4 8.3 %fusion.3 = (f32[256,4096]{1,0:T(8,128)}, bf16[256,4096]{1,0:T(8,128)(2,1)S(1)}) fusion(f32[4096]{0:T(1024)S(1)} %bitcast.45, bf16[256,1024]{1,0:T(8,128)(2,1)S(1)} %get-tuple-element.141.refs_2_, bf16[1024,4096]{1,0:T(8,128)(2,1)} %get-tuple-element.97.refs_5_), kind=kOutput, calls=%fused_computation.5 | convolution fusion | flops 2159017984 | bytes 15220736 | tf_op jit(solution)/shard_map/dot_general | solution.py:27
  192.7 0.0 copy-done.1
  192.7 0.0 copy-done
  192.7 0.0 slice-done
  192.7 0.0 slice-done.1
  192.7 0.0 copy-start.3
  192.7 2.4 fusion.17
  195.2 0.0 copy-done.2
  195.2 0.2 multiply_reduce_fusion
  195.5 0.0 copy-done.3
  195.5 0.5 fusion.12
  196.0 2.0 convert_reduce_fusion.1
  198.0 0.1 scatter.11
  198.1 0.1 scatter.14.refs_36_
  198.2 0.0 copy-start.7
  198.3 0.6 copy-done.7
  198.9 201.5 %scatter_all.1 = (f32[512,256]{1,0:T(8,128)}, f32[128,1024]{1,0:T(8,128)}, f32[128,256]{1,0:T(8,128)}, f32[128,256]{1,0:T(8,128)}, f32[128,256]{1,0:T(8,128)}, /...) custom-call(bf16[256,4096]{1,0:T(8,128)(2,1)} %copy-done.2, ...), custom_call_target="tpu_custom_call" | custom-call | tf_op jit(solution)/shard_map/scatter_all/pallas_call | solution.py:1418
  400.4 1.3 slice_bitcast_fusion
  401.7 1.3 slice.94
  403.0 1.3 slice.93
  404.3 6.8 %convert_element_type.27 = f32[8,256,1024]{2,1,0:T(8,128)} convert(bf16[8,256,1024]{2,1,0:T(8,128)(2,1)} %get-tuple-element.122) | non-fusion elementwise | flops 2097152 | bytes 12582912 | tf_op jit(solution)/shard_map/convert_element_type | solution.py:1600
  411.1 1.0 copy.49
  412.1 0.0 copy-done.15
  412.1 0.7 copy.50
  412.7 0.0 copy-done.14
  412.7 0.7 copy.51
  413.4 0.7 copy.52
  414.1 0.7 copy.53
  414.7 0.7 copy.54
  415.4 0.7 copy.55
  416.0 0.7 copy.56
  416.7 0.7 copy.57
  417.4 0.8 copy.58
  418.1 0.8 copy.59
  (30 shorter events, 0.1 us)
Async XLA Ops:
  184.1 8.6 %slice-start = ((s8[8388608]{0:T(1024)(128)(4,1)}), s8[4194304]{0:T(1024)(128)(4,1)S(1)}, s32[]{:S(2)}) async-start(s8[8388608]{0:T(1024)(128)(4,1)} %bitcast.31), calls=%async_computation | async-start | bytes 8388608
  184.4 8.3 %copy-start.1 = (bf16[256,1024]{1,0:T(8,128)(2,1)}, bf16[256,1024]{1,0:T(8,128)(2,1)S(1)}, u32[]{:S(2)}) copy-start(bf16[256,1024]{1,0:T(8,128)(2,1)S(1)} %get-tuple-element.141.refs_2_) | copy-start | bytes 1572868
  184.4 8.3 %copy-start = (f32[256,1024]{1,0:T(8,128)}, f32[256,1024]{1,0:T(8,128)S(1)}, u32[]{:S(2)}) copy-start(f32[256,1024]{1,0:T(8,128)S(1)} %get-tuple-element.142.refs_7_) | copy-start | bytes 3145732
  184.4 8.3 %slice-start.1 = ((s8[8388608]{0:T(1024)(128)(4,1)}), s8[4194304]{0:T(1024)(128)(4,1)S(1)}, s32[]{:S(2)}) async-start(s8[8388608]{0:T(1024)(128)(4,1)} %bitcast.31), calls=%async_computation.1 | async-start | bytes 8388608
  192.7 2.5 copy-start.2
  192.7 2.7 copy-start.3
  198.2 0.6 copy-start.7
  404.3 6.8 %copy-start.4 = (f32[256,1024]{1,0:T(8,128)S(1)}, f32[256,1024]{1,0:T(8,128)}, u32[]{:S(2)}) copy-start(f32[256,1024]{1,0:T(8,128)} %get-tuple-element.175) | copy-start | bytes 3145732
  404.3 7.8 %copy-start.15 = (f32[128,256]{1,0:T(8,128)S(1)}, f32[128,256]{1,0:T(8,128)}, u32[]{:S(2)}) copy-start(f32[128,256]{1,0:T(8,128)} %get-tuple-element.177) | copy-start | bytes 393220
  404.3 8.5 %copy-start.14 = (f32[128,256]{1,0:T(8,128)S(1)}, f32[128,256]{1,0:T(8,128)}, u32[]{:S(2)}) copy-start(f32[128,256]{1,0:T(8,128)} %get-tuple-element.178) | copy-start | bytes 393220
  404.3 9.1 %copy-start.13 = (f32[128,256]{1,0:T(8,128)S(1)}, f32[128,256]{1,0:T(8,128)}, u32[]{:S(2)}) copy-start(f32[128,256]{1,0:T(8,128)} %get-tuple-element.179) | copy-start | bytes 393220
  404.3 9.8 %copy-start.12 = (f32[128,256]{1,0:T(8,128)S(1)}, f32[128,256]{1,0:T(8,128)}, u32[]{:S(2)}) copy-start(f32[128,256]{1,0:T(8,128)} %get-tuple-element.180) | copy-start | bytes 393220
  404.3 10.4 %copy-start.11 = (f32[128,256]{1,0:T(8,128)S(1)}, f32[128,256]{1,0:T(8,128)}, u32[]{:S(2)}) copy-start(f32[128,256]{1,0:T(8,128)} %get-tuple-element.181) | copy-start | bytes 393220
  404.3 11.1 %copy-start.10 = (f32[128,256]{1,0:T(8,128)S(1)}, f32[128,256]{1,0:T(8,128)}, u32[]{:S(2)}) copy-start(f32[128,256]{1,0:T(8,128)} %get-tuple-element.182) | copy-start | bytes 393220
  404.3 11.7 %copy-start.9 = (f32[128,256]{1,0:T(8,128)S(1)}, f32[128,256]{1,0:T(8,128)}, u32[]{:S(2)}) copy-start(f32[128,256]{1,0:T(8,128)} %get-tuple-element.183) | copy-start | bytes 393220
  404.3 12.4 %copy-start.8 = (f32[128,256]{1,0:T(8,128)S(1)}, f32[128,256]{1,0:T(8,128)}, u32[]{:S(2)}) copy-start(f32[128,256]{1,0:T(8,128)} %get-tuple-element.184) | copy-start | bytes 393220
  411.1 6.2 %copy-start.6 = (f32[128,1024]{1,0:T(8,128)S(1)}, f32[128,1024]{1,0:T(8,128)}, u32[]{:S(2)}) copy-start(f32[128,1024]{1,0:T(8,128)} %get-tuple-element.185) | copy-start | bytes 1572868
  411.1 7.0 %copy-start.5 = (f32[512,256]{1,0:T(8,128)S(1)}, f32[512,256]{1,0:T(8,128)}, u32[]{:S(2)}) copy-start(f32[512,256]{1,0:T(8,128)} %get-tuple-element.186) | copy-start | bytes 1572868
